TPU v7x, 32 devices: a whole 2x2x4 slice. The times are simulated.
32 devices in a mesh: dp: 8 (over y, x, core), tensor: 4 (over z).
Axes of the slice: x: 2, y: 2, z: 4, core: 2. Of those that a mesh axis runs over, the one named last changes fastest.
Arguments:
- tokens: bfloat16 [4096, 1024], P(('dp', 'tensor')), may hold values from -6 to 6
- segment_ids: int32 [8, 512], P('dp'), may hold values from 0 to 3, never falling along the last dimension, each value on 1 to 256 neighbouring positions
- query_weight: float32 [2, 1024, 1024], P(None, 'dp', 'tensor'), may hold values from -0.1875 to 0.1875
- key_weight: float32 [2, 1024, 1024], P(None, 'dp', 'tensor'), may hold values from -0.1875 to 0.1875
- value_weight: float32 [2, 1024, 2048], P(None, 'dp', 'tensor'), may hold values from -0.1875 to 0.1875
- gate_weight: float32 [2, 1024, 2048], P(None, 'dp', 'tensor'), may hold values from -0.1875 to 0.1875
- decay_weight: float32 [2, 1024, 16], P(None, 'dp', 'tensor'), may hold values from -0.1875 to 0.1875
- out_weight: float32 [2, 1024, 2048], P(None, 'dp', 'tensor'), may hold values from -0.25 to 0.25
- swiglu_gate: float32 [2, 1024, 2816], P(None, 'dp', 'tensor'), may hold values from -0.1875 to 0.1875
- swiglu_up: float32 [2, 1024, 2816], P(None, 'dp', 'tensor'), may hold values from -0.1875 to 0.1875
- swiglu_down: float32 [2, 1024, 2816], P(None, 'dp', 'tensor'), may hold values from -0.21875 to 0.21875
- conv_query_key: float32 [2, 2, 4, 1024], P(None, None, None, 'tensor'), may hold values from -3 to 3
- conv_value: float32 [2, 4, 2048], P(None, None, 'tensor'), may hold values from -3 to 3
- head_params: float32 [2, 2, 8], P(None, None, 'tensor'), may hold values from -6 to 0
- norm_gains: float32 [2, 2, 1024], replicated, may hold values from 0.1 to 1.9
- out_gain: float32 [2, 256], replicated, may hold values from 0.1 to 1.9
- cotangent: bfloat16 [4096, 1024], P(('dp', 'tensor')), may hold values from -6 to 6
Outputs:
- output: float32 [4096, 1024], P(('dp', 'tensor'))
- input_grad: float32 [4096, 1024], P(('dp', 'tensor'))
- query_weight_grad: float32 [2, 1024, 1024], P(None, 'dp', 'tensor')
- key_weight_grad: float32 [2, 1024, 1024], P(None, 'dp', 'tensor')
- value_weight_grad: float32 [2, 1024, 2048], P(None, 'dp', 'tensor')
- gate_weight_grad: float32 [2, 1024, 2048], P(None, 'dp', 'tensor')
- decay_weight_grad: float32 [2, 1024, 16], P(None, 'dp', 'tensor')
- out_weight_grad: float32 [2, 1024, 2048], P(None, 'dp', 'tensor')
- swiglu_gate_grad: float32 [2, 1024, 2816], P(None, 'dp', 'tensor')
- swiglu_up_grad: float32 [2, 1024, 2816], P(None, 'dp', 'tensor')
- swiglu_down_grad: float32 [2, 1024, 2816], P(None, 'dp', 'tensor')
- conv_query_key_grad: float32 [2, 2, 4, 1024], P(None, None, None, 'tensor')
- conv_value_grad: float32 [2, 4, 2048], P(None, None, 'tensor')
- head_params_grad: float32 [2, 2, 8], P(None, None, 'tensor')
- norm_gains_grad: float32 [2, 2, 1024], replicated
- out_gain_grad: float32 [2, 256], replicated
Inputs may be any that keep to these rules, and one draw needn't show every extreme that they name: `segment_ids`: segment ids never fall along a sequence; every document holds 1 to 256 tokens.
All inputs are finite; a program needn't handle non-finite values.
Results may differ from a plain program's by a relative error of at most 0.025.
Values may be sent and summed in bfloat16 or wider, within the bound.
A program may use at most 192 MiB of HBM per device.

v0:
```python
from functools import partial

import jax
import jax.numpy as jnp
from jax import lax
from jax.sharding import PartitionSpec as P

SPAN = 64
LAYERS = 2


epsilon = 1e-06
out_floor = 0.01
highest = lax.Precision.HIGHEST


def rms_gain(matrix, gain_vector):
    scaling = lax.rsqrt(jnp.mean(matrix * matrix, axis=-1, keepdims=True) + epsilon)
    return matrix * scaling * gain_vector


def causal_conv(signal, kernel, segment_ids):
    length = signal.shape[1]
    summed = signal * kernel[0]
    for offset in range(1, kernel.shape[0]):
        shifted = jnp.pad(signal, ((0, 0), (offset, 0), (0, 0)))[:, :length]
        earlier = jnp.pad(segment_ids, ((0, 0), (offset, 0)), constant_values=-1)[:, :length]
        matching = (earlier == segment_ids).astype(signal.dtype)[:, :, None]
        summed = summed + shifted * matching * kernel[offset]
    return summed


def block_step(carried, block_in):
    memory_state, last_segment = carried
    queries, keys_in, values_in, beta_gate, log_decay, segment_block = block_in
    kind = keys_in.dtype
    extent = segment_block.shape[1]
    cumulative = jnp.cumsum(log_decay, axis=-1)
    positions = jnp.arange(extent, dtype=jnp.int32)
    lower_incl = positions[:, None] >= positions[None, :]
    strict_lower = (positions[:, None] > positions[None, :]).astype(kind)
    same_segment = segment_block[:, :, None] == segment_block[:, None, :]
    allowed = (same_segment & lower_incl[None]).astype(kind)[:, None]
    fading = jnp.exp((cumulative[..., :, None] - cumulative[..., None, :]) * allowed) * allowed
    carried_mask = (segment_block == last_segment[:, None]).astype(kind)[:, None, :]
    entry_scale = jnp.exp(cumulative) * carried_mask
    key_products = jnp.einsum("bhtk,bhsk->bhts", keys_in, keys_in, precision=highest)
    mixing = beta_gate[..., :, None] * key_products * fading * strict_lower
    recalled = jnp.einsum("bhtk,bhkv->bhtv", keys_in, memory_state, precision=highest)
    target = beta_gate[..., None] * (values_in - entry_scale[..., None] * recalled)
    unit_lower = jnp.eye(extent, dtype=kind) + mixing
    corrected = jax.scipy.linalg.solve_triangular(
        unit_lower, target, lower=True, unit_diagonal=True
    )
    query_keys = jnp.einsum("bhtk,bhsk->bhts", queries, keys_in, precision=highest)
    from_state = jnp.einsum("bhtk,bhkv->bhtv", queries, memory_state, precision=highest)
    outputs = entry_scale[..., None] * from_state + jnp.einsum(
        "bhts,bhsv->bhtv", query_keys * fading, corrected, precision=highest
    )
    final_segment = segment_block[:, -1]
    tail_mask = (segment_block == final_segment[:, None]).astype(kind)[:, None, :]
    tail_weight = jnp.exp(cumulative[..., -1:] - cumulative) * tail_mask
    new_state = entry_scale[..., -1][..., None, None] * memory_state + jnp.einsum(
        "bhsk,bhsv->bhkv", keys_in * tail_weight[..., None], corrected, precision=highest
    )
    return ((new_state, final_segment), outputs)


def delta_core(
    proj_query,
    proj_key,
    proj_value,
    proj_gate,
    proj_pair,
    kernel_pair,
    kernel_value,
    head_table,
    gain_vector,
    segment_ids,
):
    batches, length = segment_ids.shape
    head_count = proj_pair.shape[1] // 2
    key_dim = proj_query.shape[1] // head_count
    value_dim = proj_value.shape[1] // head_count
    blocks = length // SPAN

    def sequences(matrix):
        return matrix.reshape(batches, length, matrix.shape[1])

    queries = jax.nn.silu(causal_conv(sequences(proj_query), kernel_pair[0], segment_ids))
    keys_in = jax.nn.silu(causal_conv(sequences(proj_key), kernel_pair[1], segment_ids))
    values_in = jax.nn.silu(causal_conv(sequences(proj_value), kernel_value, segment_ids))
    queries = queries.reshape(batches, length, head_count, key_dim)
    keys_in = keys_in.reshape(batches, length, head_count, key_dim)
    values_in = values_in.reshape(batches, length, head_count, value_dim)
    queries = (
        queries
        * lax.rsqrt(jnp.sum(queries * queries, axis=-1, keepdims=True) + epsilon)
        * key_dim ** (-0.5)
    )
    keys_in = keys_in * lax.rsqrt(jnp.sum(keys_in * keys_in, axis=-1, keepdims=True) + epsilon)
    pairs = proj_pair.reshape(batches, length, head_count, 2)
    beta_gate = jax.nn.sigmoid(pairs[..., 1])
    log_decay = -jnp.exp(head_table[0]) * jax.nn.softplus(pairs[..., 0] + head_table[1])

    def to_blocks(array):
        array = array.reshape((batches, blocks, SPAN) + array.shape[2:])
        return jnp.moveaxis(jnp.moveaxis(array, 1, 0), 3, 2)

    segment_blocks = jnp.moveaxis(segment_ids.reshape(batches, blocks, SPAN), 1, 0)
    start_state = jnp.zeros((batches, head_count, key_dim, value_dim), keys_in.dtype)
    inputs = (
        to_blocks(queries),
        to_blocks(keys_in),
        to_blocks(values_in),
        to_blocks(beta_gate),
        to_blocks(log_decay),
        segment_blocks,
    )
    ignored, outputs = lax.scan(
        jax.checkpoint(block_step), (start_state, segment_ids[:, 0]), inputs
    )
    recurrent = jnp.moveaxis(jnp.moveaxis(outputs, 0, 1), 2, 3).reshape(
        batches * length, head_count, value_dim
    )
    gate_pre = proj_gate.reshape(batches * length, head_count, value_dim)
    normalized = recurrent * lax.rsqrt(
        jnp.mean(recurrent * recurrent, axis=-1, keepdims=True) + out_floor
    )
    return (normalized * gain_vector * jax.nn.silu(gate_pre)).reshape(
        batches * length, head_count * value_dim
    )


def times_transposed(left, right):
    return lax.dot_general(
        left, right, (((1,), (1,)), ((), ())), preferred_element_type=jnp.float32
    )


def over_rows(left, right):
    return lax.dot_general(
        left, right, (((0,), (0,)), ((), ())), preferred_element_type=jnp.float32
    )


def body(
    tokens,
    segment_ids,
    query_weight,
    key_weight,
    value_weight,
    gate_weight,
    decay_weight,
    out_weight,
    swiglu_gate,
    swiglu_up,
    swiglu_down,
    conv_query_key,
    conv_value,
    head_params,
    norm_gains,
    out_gain,
    cotangent,
):
    local_rows = tokens.shape[0]

    def layer_weights(layer_idx):
        return (
            lax.all_gather(query_weight[layer_idx].astype(jnp.bfloat16), "dp", axis=0, tiled=True),
            lax.all_gather(key_weight[layer_idx].astype(jnp.bfloat16), "dp", axis=0, tiled=True),
            lax.all_gather(value_weight[layer_idx].astype(jnp.bfloat16), "dp", axis=0, tiled=True),
            lax.all_gather(gate_weight[layer_idx].astype(jnp.bfloat16), "dp", axis=0, tiled=True),
            lax.all_gather(decay_weight[layer_idx].astype(jnp.bfloat16), "dp", axis=0, tiled=True),
            lax.all_gather(out_weight[layer_idx].astype(jnp.bfloat16), "dp", axis=0, tiled=True),
            lax.all_gather(swiglu_gate[layer_idx].astype(jnp.bfloat16), "dp", axis=0, tiled=True),
            lax.all_gather(swiglu_up[layer_idx].astype(jnp.bfloat16), "dp", axis=0, tiled=True),
            lax.all_gather(swiglu_down[layer_idx].astype(jnp.bfloat16), "dp", axis=0, tiled=True),
        )

    def spread_input(matrix):
        return lax.all_gather(matrix, "tensor", axis=0, tiled=True)

    def spread_cotangent(matrix):
        return lax.all_gather(matrix, "tensor", axis=0, tiled=True)

    def collect_output(term_fn):
        return lax.psum_scatter(
            term_fn(jnp.int32(0), lax.axis_size("tensor") * local_rows),
            "tensor",
            scatter_dimension=0,
            tiled=True,
        )

    def collect_grad(term_fn):
        return lax.psum_scatter(
            term_fn(jnp.int32(0), local_rows * lax.axis_size("tensor")).astype(jnp.bfloat16),
            "tensor",
            scatter_dimension=0,
            tiled=True,
        ).astype(jnp.float32)

    residual = tokens.astype(jnp.float32)
    kept = []
    for layer_idx in range(LAYERS):
        weights = layer_weights(layer_idx)
        first_norm, first_back = jax.vjp(rms_gain, residual, norm_gains[layer_idx, 0])
        normed = spread_input(first_norm.astype(jnp.bfloat16))
        projected = tuple(
            (jnp.dot(normed, matrix, preferred_element_type=jnp.float32) for matrix in weights[:5])
        )
        mixer_out, core_back = jax.vjp(
            partial(delta_core, segment_ids=segment_ids),
            projected[0],
            projected[1],
            projected[2],
            projected[3],
            projected[4],
            conv_query_key[layer_idx],
            conv_value[layer_idx],
            head_params[layer_idx],
            out_gain[layer_idx],
        )
        mixer_rows = mixer_out.astype(jnp.bfloat16)
        out_matrix = weights[5]

        def mixer_term(first_row, row_count):
            return times_transposed(mixer_rows, out_matrix)

        middle = residual + collect_output(mixer_term)
        second_norm, second_back = jax.vjp(rms_gain, middle, norm_gains[layer_idx, 1])
        normed_ffn = spread_input(second_norm.astype(jnp.bfloat16))
        gate_pre = jnp.dot(normed_ffn, weights[6], preferred_element_type=jnp.float32)
        up_pre = jnp.dot(normed_ffn, weights[7], preferred_element_type=jnp.float32)
        hidden = (jax.nn.silu(gate_pre) * up_pre).astype(jnp.bfloat16)
        down_matrix = weights[8]

        def swiglu_term(first_row, row_count):
            return times_transposed(hidden, down_matrix)

        residual = middle + collect_output(swiglu_term)
        kept.append(
            (
                weights,
                first_back,
                normed,
                core_back,
                mixer_rows,
                second_back,
                normed_ffn,
                gate_pre,
                up_pre,
                hidden,
            )
        )
    grad_rows = cotangent.astype(jnp.float32)
    matrix_grads = [None] * LAYERS
    small_grads = [None] * LAYERS
    norm_grads = [None] * LAYERS
    for layer_idx in reversed(range(LAYERS)):
        (
            saved_weights,
            first_back,
            normed,
            core_back,
            mixer_rows,
            second_back,
            normed_ffn,
            gate_pre,
            up_pre,
            hidden,
        ) = kept[layer_idx]
        weights = layer_weights(layer_idx)
        ffn_cot = spread_cotangent(grad_rows.astype(jnp.bfloat16))
        down_grad = over_rows(ffn_cot, hidden)
        d_hidden = jnp.dot(ffn_cot, weights[8], preferred_element_type=jnp.float32)
        sigmoid_gate = jax.nn.sigmoid(gate_pre)
        d_gate = (
            d_hidden * up_pre * sigmoid_gate * (1.0 + gate_pre * (1.0 - sigmoid_gate))
        ).astype(jnp.bfloat16)
        d_up = (d_hidden * gate_pre * sigmoid_gate).astype(jnp.bfloat16)
        gate_grad = over_rows(normed_ffn, d_gate)
        up_grad = over_rows(normed_ffn, d_up)
        gate_matrix = weights[6]
        up_matrix = weights[7]

        def swiglu_back(first_row, row_count):
            return times_transposed(d_gate, gate_matrix) + times_transposed(d_up, up_matrix)

        d_middle, second_gain_grad = second_back(collect_grad(swiglu_back))
        grad_rows = grad_rows + d_middle
        mixer_cot = spread_cotangent(grad_rows.astype(jnp.bfloat16))
        out_grad = over_rows(mixer_cot, mixer_rows)
        d_mixer = jnp.dot(mixer_cot, weights[5], preferred_element_type=jnp.float32)
        core_grads = core_back(d_mixer)
        d_projected = tuple((term.astype(jnp.bfloat16) for term in core_grads[:5]))
        query_grad, key_grad, value_grad, gate_out_grad, decay_grad = tuple(
            (over_rows(normed, term) for term in d_projected)
        )
        in_matrices = weights[:5]

        def mixer_back(first_row, row_count):
            return sum(
                (times_transposed(d_projected[member], in_matrices[member]) for member in range(5))
            )

        d_input, first_gain_grad = first_back(collect_grad(mixer_back))
        grad_rows = grad_rows + d_input
        matrix_grads[layer_idx] = (
            lax.psum_scatter(query_grad, "dp", scatter_dimension=0, tiled=True),
            lax.psum_scatter(key_grad, "dp", scatter_dimension=0, tiled=True),
            lax.psum_scatter(value_grad, "dp", scatter_dimension=0, tiled=True),
            lax.psum_scatter(gate_out_grad, "dp", scatter_dimension=0, tiled=True),
            lax.psum_scatter(decay_grad, "dp", scatter_dimension=0, tiled=True),
            lax.psum_scatter(out_grad, "dp", scatter_dimension=0, tiled=True),
            lax.psum_scatter(gate_grad, "dp", scatter_dimension=0, tiled=True),
            lax.psum_scatter(up_grad, "dp", scatter_dimension=0, tiled=True),
            lax.psum_scatter(down_grad, "dp", scatter_dimension=0, tiled=True),
        )
        small_grads[layer_idx] = core_grads[5:]
        norm_grads[layer_idx] = jnp.stack([first_gain_grad, second_gain_grad])
    stacked = tuple(
        (
            jnp.stack([matrix_grads[layer_pos][member] for layer_pos in range(LAYERS)])
            for member in range(9)
        )
    )
    pair_grad = jnp.stack([small_grads[layer_pos][0] for layer_pos in range(LAYERS)])
    value_conv_grad = jnp.stack([small_grads[layer_pos][1] for layer_pos in range(LAYERS)])
    head_grad = jnp.stack([small_grads[layer_pos][2] for layer_pos in range(LAYERS)])
    out_gain_part = jnp.stack([small_grads[layer_pos][3] for layer_pos in range(LAYERS)])
    pair_grad, value_conv_grad, head_grad = lax.psum((pair_grad, value_conv_grad, head_grad), "dp")
    norm_gain_grad, out_gain_grad = lax.psum(
        (jnp.stack(norm_grads), out_gain_part), ("dp", "tensor")
    )
    return (
        residual,
        grad_rows,
        stacked[0],
        stacked[1],
        stacked[2],
        stacked[3],
        stacked[4],
        stacked[5],
        stacked[6],
        stacked[7],
        stacked[8],
        pair_grad,
        value_conv_grad,
        head_grad,
        norm_gain_grad,
        out_gain_grad,
    )


def solution(mesh):
    return jax.shard_map(
        body,
        mesh=mesh,
        in_specs=(
            P(("dp", "tensor"), None),
            P("dp", None),
            P(None, "dp", "tensor"),
            P(None, "dp", "tensor"),
            P(None, "dp", "tensor"),
            P(None, "dp", "tensor"),
            P(None, "dp", "tensor"),
            P(None, "dp", "tensor"),
            P(None, "dp", "tensor"),
            P(None, "dp", "tensor"),
            P(None, "dp", "tensor"),
            P(None, None, None, "tensor"),
            P(None, None, "tensor"),
            P(None, None, "tensor"),
            P(),
            P(),
            P(("dp", "tensor"), None),
        ),
        out_specs=(
            P(("dp", "tensor"), None),
            P(("dp", "tensor"), None),
            P(None, "dp", "tensor"),
            P(None, "dp", "tensor"),
            P(None, "dp", "tensor"),
            P(None, "dp", "tensor"),
            P(None, "dp", "tensor"),
            P(None, "dp", "tensor"),
            P(None, "dp", "tensor"),
            P(None, "dp", "tensor"),
            P(None, "dp", "tensor"),
            P(None, None, None, "tensor"),
            P(None, None, "tensor"),
            P(None, None, "tensor"),
            P(),
            P(),
        ),
        check_vma=False,
    )
```

profile of v0, /device:TPU:0, one launch (start us, length us, event | category | flops | bytes accessed | tf_op | source)
XLA Modules:
  0.0 2660.2 jit_solution(15524928698072118296)
XLA Ops:
  77.9 184.1 %while.88 = (s32[]{:T(128)}, f32[1,2,128,256]{3,2,1,0:T(8,128)S(1)}, s32[1]{0:T(128)}, f32[8,1,2,64,256]{4,3,2,1,0:T(8,128)S(1)}, f32[8,1,2,128,256]{4,3,2,1,0:T...) while((s32[]{:T(128)}, ...), condition=%wide.region_5.8_spmd.clone, body=%wide.region_3.7_spmd.clone.sunk | while | flops 227226304 | bytes 3569689 | solution.py:120
  275.2 42.0 %reduce-scatter.31.cloned.1.call-done = f32[128,1024]{1,0:T(8,128)} async-done(((f32[512,1024]{1,0:T(8,128)}), f32[128,1024]{1,0:T(8,128)}) %reduce-scatter.31.cloned.1.call-update) | async-done | bytes 524304 | tf_op jit(solution)/shard_map/reduce_scatter | solution.py:188
  344.3 30.2 %all-gather.41.cloned.1.call-done = bf16[512,1024]{1,0:T(8,128)(2,1)} async-done(((bf16[128,1024]{1,0:T(8,128)(2,1)}), bf16[512,1024]{1,0:T(8,128)(2,1)}) %all-gather.41.cloned.1.call-update) | async-done | bytes 1048592 | tf_op jit(solution)/shard_map/all_gather | solution.py:182
  406.0 23.8 all-gather.65.cloned.1.call-done
  433.9 43.9 %reduce-scatter.33.cloned.1.call-done = f32[128,1024]{1,0:T(8,128)} async-done(((f32[512,1024]{1,0:T(8,128)}), f32[128,1024]{1,0:T(8,128)}) %reduce-scatter.33.cloned.1.call-update) | async-done | bytes 524304 | tf_op jit(solution)/shard_map/reduce_scatter | solution.py:188
  546.8 216.4 %while.89 = (s32[]{:T(128)}, f32[1,2,128,256]{3,2,1,0:T(8,128)S(1)}, s32[1]{0:T(128)}, f32[8,1,2,64,256]{4,3,2,1,0:T(8,128)S(1)}, f32[8,1,2,128,256]{4,3,2,1,0:T...) while((s32[]{:T(128)}, ...), condition=%wide.region_15.18_spmd.clone, body=%wide.region_13.17_spmd.clone.sunk | while | flops 227226304 | bytes 3635253 | solution.py:120
  775.1 43.4 %reduce-scatter.35.cloned.1.call-done = f32[128,1024]{1,0:T(8,128)} async-done(((f32[512,1024]{1,0:T(8,128)}), f32[128,1024]{1,0:T(8,128)}) %reduce-scatter.35.cloned.1.call-update) | async-done | bytes 524304 | tf_op jit(solution)/shard_map/reduce_scatter | solution.py:188
  845.6 30.0 %all-gather.45.cloned.1.call-done = bf16[512,1024]{1,0:T(8,128)(2,1)} async-done(((bf16[128,1024]{1,0:T(8,128)(2,1)}), bf16[512,1024]{1,0:T(8,128)(2,1)}) %all-gather.45.cloned.1.call-update) | async-done | bytes 1048592 | tf_op jit(solution)/shard_map/all_gather | solution.py:182
  906.1 25.9 all-gather.47.cloned.1.call-done
  931.9 26.7 %all-gather.77.cloned.1.call-done = bf16[1,1024,704]{1,2,0:T(8,128)(2,1)} async-done(((bf16[1,128,704]{1,2,0:T(8,128)(2,1)}), bf16[1,1024,704]{1,2,0:T(8,128)(2,1)}) %all-gather.77.cloned.1.call-update) | async-done | bytes 1441808 | tf_op jit(solution)/shard_map/all_gather | solution.py:178
  967.6 27.2 %reduce-scatter.39.cloned.1.call-done = bf16[128,1024]{1,0:T(8,128)(2,1)} async-done(((bf16[512,1024]{1,0:T(8,128)(2,1)}), bf16[128,1024]{1,0:T(8,128)(2,1)}) %reduce-scatter.39.cloned.1.call-update) | async-done | bytes 262160 | tf_op jit(solution)/shard_map/reduce_scatter | solution.py:196
  1041.7 296.9 %while.90 = (s32[]{:T(128)}, f32[1,2,128,256]{2,3,1,0:T(8,128)}, f32[8,1,2,64,128]{4,3,0,2,1:T(8,128)}, f32[8,1,2,64,128]{4,3,0,2,1:T(8,128)}, f32[8,1,2,64,256]...) while((s32[]{:T(128)}, f32[1,2,128,256]{2,3,1,0:T(8,128)}, ...), condition=%wide.region_35.39_spmd.clone, body=%wide.region_23.38_spmd.clone.sunk | while | flops 612030272 | bytes 11862847 | solution.py:120
  1416.3 43.1 %reduce-scatter.37.cloned.1.call-done = f32[128,1024]{1,0:T(8,128)} async-done(((f32[512,1024]{1,0:T(8,128)}), f32[128,1024]{1,0:T(8,128)}) %reduce-scatter.37.cloned.1.call-update) | async-done | bytes 524304 | tf_op jit(solution)/shard_map/reduce_scatter | solution.py:188
  1462.1 27.4 %all-gather.51.cloned.1.call-done = bf16[512,1024]{1,0:T(8,128)(2,1)} async-done(((bf16[128,1024]{1,0:T(8,128)(2,1)}), bf16[512,1024]{1,0:T(8,128)(2,1)}) %all-gather.51.cloned.1.call-update) | async-done | bytes 1048592 | tf_op jit(solution)/shard_map/all_gather | solution.py:185
  1497.4 26.7 %reduce-scatter.43.cloned.1.call-done = bf16[128,1024]{1,0:T(8,128)(2,1)} async-done(((bf16[512,1024]{1,0:T(8,128)(2,1)}), bf16[128,1024]{1,0:T(8,128)(2,1)}) %reduce-scatter.43.cloned.1.call-update) | async-done | bytes 262160 | tf_op jit(solution)/shard_map/reduce_scatter | solution.py:196
  1569.8 297.6 %while.91 = (s32[]{:T(128)}, f32[1,2,128,256]{2,3,1,0:T(8,128)}, f32[8,1,2,64,128]{4,3,0,2,1:T(8,128)}, f32[8,1,2,64,128]{4,3,0,2,1:T(8,128)}, f32[8,1,2,64,256]...) while((s32[]{:T(128)}, f32[1,2,128,256]{2,3,1,0:T(8,128)}, ...), condition=%wide.region_55.59_spmd.clone, body=%wide.region_43.58_spmd.clone.sunk | while | flops 612030272 | bytes 11862847 | solution.py:120
  1975.4 25.3 all-reduce.80
  2005.3 46.7 %reduce-scatter.73.cloned.1.call-done = f32[128,704]{0,1:T(8,128)} async-done(((f32[1024,704]{0,1:T(8,128)}), f32[128,704]{0,1:T(8,128)}) %reduce-scatter.73.cloned.1.call-update) | async-done | bytes 360464 | tf_op jit(solution)/shard_map/reduce_scatter | solution.py:317
  2052.0 48.2 %reduce-scatter.71.cloned.1.call-done = f32[128,704]{0,1:T(8,128)} async-done(((f32[1024,704]{0,1:T(8,128)}), f32[128,704]{0,1:T(8,128)}) %reduce-scatter.71.cloned.1.call-update) | async-done | bytes 360464 | tf_op jit(solution)/shard_map/reduce_scatter | solution.py:317
  2102.1 46.7 %reduce-scatter.77.cloned.1.call-done = f32[128,704]{0,1:T(8,128)} async-done(((f32[1024,704]{0,1:T(8,128)}), f32[128,704]{0,1:T(8,128)}) %reduce-scatter.77.cloned.1.call-update) | async-done | bytes 360464 | tf_op jit(solution)/shard_map/reduce_scatter | solution.py:318
  2148.8 48.3 %reduce-scatter.75.cloned.1.call-done = f32[128,704]{0,1:T(8,128)} async-done(((f32[1024,704]{0,1:T(8,128)}), f32[128,704]{0,1:T(8,128)}) %reduce-scatter.75.cloned.1.call-update) | async-done | bytes 360464 | tf_op jit(solution)/shard_map/reduce_scatter | solution.py:318
  2199.2 37.3 %reduce-scatter.49.cloned.1.call-done = f32[128,256]{1,0:T(8,128)} async-done(((f32[1024,256]{1,0:T(8,128)}), f32[128,256]{1,0:T(8,128)}) %reduce-scatter.49.cloned.1.call-update) | async-done | bytes 131088 | tf_op jit(solution)/shard_map/reduce_scatter | solution.py:310
  2236.5 39.4 %reduce-scatter.47.cloned.1.call-done = f32[128,256]{1,0:T(8,128)} async-done(((f32[1024,256]{1,0:T(8,128)}), f32[128,256]{1,0:T(8,128)}) %reduce-scatter.47.cloned.1.call-update) | async-done | bytes 131088 | tf_op jit(solution)/shard_map/reduce_scatter | solution.py:310
  2277.6 37.9 %reduce-scatter.53.cloned.1.call-done = f32[128,256]{1,0:T(8,128)} async-done(((f32[1024,256]{1,0:T(8,128)}), f32[128,256]{1,0:T(8,128)}) %reduce-scatter.53.cloned.1.call-update) | async-done | bytes 131088 | tf_op jit(solution)/shard_map/reduce_scatter | solution.py:311
  2315.5 39.4 %reduce-scatter.51.cloned.1.call-done = f32[128,256]{1,0:T(8,128)} async-done(((f32[1024,256]{1,0:T(8,128)}), f32[128,256]{1,0:T(8,128)}) %reduce-scatter.51.cloned.1.call-update) | async-done | bytes 131088 | tf_op jit(solution)/shard_map/reduce_scatter | solution.py:311
  2356.6 27.9 %reduce-scatter.45.cloned.1.call-done = bf16[128,1024]{1,0:T(8,128)(2,1)} async-done(((bf16[512,1024]{1,0:T(8,128)(2,1)}), bf16[128,1024]{1,0:T(8,128)(2,1)}) %reduce-scatter.45.cloned.1.call-update) | async-done | bytes 262160 | tf_op jit(solution)/shard_map/reduce_scatter | solution.py:196
  2385.7 39.3 %all-reduce.79 = (f32[2,2,1024]{2,1,0:T(2,128)}, f32[2,256]{1,0:T(2,128)}) all-reduce(f32[2,2,1024]{2,1,0:T(2,128)S(1)} %pad_maximum_fusion.10, f32[2,256]{1,0:T(2,128)S(1)} %pad_maximum_fusion.13), channel_id=1, replica_groups=mesh['dp'=8,'tensor'=4] {'dp','tensor'}, use_global_device_ids=true, to_apply=%region_113.117 | all-reduce | flops 4608 | bytes 36864 | tf_op jit(solution)/shard_map/psum | solution.py:333
  2427.8 45.0 %reduce-scatter.55.cloned.1.call-done = f32[128,512]{1,0:T(8,128)} async-done(((f32[1024,512]{1,0:T(8,128)}), f32[128,512]{1,0:T(8,128)}) %reduce-scatter.55.cloned.1.call-update) | async-done | bytes 262160 | tf_op jit(solution)/shard_map/reduce_scatter | solution.py:312
  2474.7 42.5 %reduce-scatter.61.cloned.1.call-done = f32[128,512]{1,0:T(8,128)} async-done(((f32[1024,512]{1,0:T(8,128)}), f32[128,512]{1,0:T(8,128)}) %reduce-scatter.61.cloned.1.call-update) | async-done | bytes 262160 | tf_op jit(solution)/shard_map/reduce_scatter | solution.py:313
  2517.2 44.9 %reduce-scatter.59.cloned.1.call-done = f32[128,512]{1,0:T(8,128)} async-done(((f32[1024,512]{1,0:T(8,128)}), f32[128,512]{1,0:T(8,128)}) %reduce-scatter.59.cloned.1.call-update) | async-done | bytes 262160 | tf_op jit(solution)/shard_map/reduce_scatter | solution.py:313
  2564.0 42.5 %reduce-scatter.65.cloned.1.call-done = f32[128,512]{1,0:T(8,128)} async-done(((f32[1024,512]{1,0:T(8,128)}), f32[128,512]{1,0:T(8,128)}) %reduce-scatter.65.cloned.1.call-update) | async-done | bytes 262160 | tf_op jit(solution)/shard_map/reduce_scatter | solution.py:315
  2606.6 44.8 %reduce-scatter.63.cloned.1.call-done = f32[128,512]{1,0:T(8,128)} async-done(((f32[1024,512]{1,0:T(8,128)}), f32[128,512]{1,0:T(8,128)}) %reduce-scatter.63.cloned.1.call-update) | async-done | bytes 262160 | tf_op jit(solution)/shard_map/reduce_scatter | solution.py:315
  (2603 shorter events, 1579.4 us)
Async XLA Ops:
  12.6 253.8 %all-gather.57.cloned.1.call-start = ((), (), s32[]{:S(2)}) async-start(), calls=%async_computation.59 | async-start | bytes 1179648 | tf_op jit(solution)/shard_map/all_gather | solution.py:173
  13.4 256.3 %all-gather.59.cloned.1.call-start = ((), (), s32[]{:S(2)}) async-start(), calls=%async_computation.60 | async-start | bytes 1179648 | tf_op jit(solution)/shard_map/all_gather | solution.py:175
  14.3 302.9 %reduce-scatter.31.cloned.1.call-start = ((), (), s32[]{:S(2)}) async-start(), calls=%async_computation.27 | async-start | bytes 2621440 | tf_op jit(solution)/shard_map/reduce_scatter | solution.py:188
  320.2 109.7 %all-gather.65.cloned.1.call-start = ((), (), s32[]{:S(2)}) async-start(), calls=%async_computation.63 | async-start | bytes 1622016 | tf_op jit(solution)/shard_map/all_gather | solution.py:178
  321.1 156.8 %reduce-scatter.33.cloned.1.call-start = ((), (), s32[]{:S(2)}) async-start(), calls=%async_computation.29 | async-start | bytes 2621440 | tf_op jit(solution)/shard_map/reduce_scatter | solution.py:188
  480.5 286.6 %all-gather.69.cloned.1.call-start = ((), (), s32[]{:S(2)}) async-start(), calls=%async_computation.65 | async-start | bytes 1179648 | tf_op jit(solution)/shard_map/all_gather | solution.py:173
  481.3 289.7 %all-gather.71.cloned.1.call-start = ((), (), s32[]{:S(2)}) async-start(), calls=%async_computation.66 | async-start | bytes 1179648 | tf_op jit(solution)/shard_map/all_gather | solution.py:175
  481.8 336.6 %reduce-scatter.35.cloned.1.call-start = ((), (), s32[]{:S(2)}) async-start(), calls=%async_computation.31 | async-start | bytes 2621440 | tf_op jit(solution)/shard_map/reduce_scatter | solution.py:188
  775.0 100.6 %all-gather.45.cloned.1.call-start = ((), (), s32[]{:S(2)}) async-start(), calls=%async_computation.32 | async-start | bytes 1310720 | tf_op jit(solution)/shard_map/all_gather | solution.py:182
  822.0 109.9 %all-gather.47.cloned.1.call-start = ((), (), s32[]{:S(2)}) async-start(), calls=%async_computation.34 | async-start | bytes 1310720 | tf_op jit(solution)/shard_map/all_gather | solution.py:185
  822.8 135.9 %all-gather.77.cloned.1.call-start = ((), (), s32[]{:S(2)}) async-start(), calls=%async_computation.69 | async-start | bytes 1622016 | tf_op jit(solution)/shard_map/all_gather | solution.py:178
  823.4 171.5 %reduce-scatter.39.cloned.1.call-start = ((), (), s32[]{:S(2)}) async-start(), calls=%async_computation.35 | async-start | bytes 1310720 | tf_op jit(solution)/shard_map/reduce_scatter | solution.py:196
  999.3 415.2 %reduce-scatter.41.cloned.1.call-start = ((), (), s32[]{:S(2)}) async-start(), calls=%async_computation.37 | async-start | bytes 1310720 | tf_op jit(solution)/shard_map/reduce_scatter | solution.py:196
  1527.7 443.7 %reduce-scatter.81.cloned.1.call-start = ((), (), s32[]{:S(2)}) async-start(), calls=%async_computation.71 | async-start | bytes 589824
  1532.0 468.8 %reduce-scatter.79.cloned.1.call-start = ((), (), s32[]{:S(2)}) async-start(), calls=%async_computation.70 | async-start | bytes 589824
  1872.1 130.2 %reduce-scatter.69.cloned.1.call-start = ((), (), s32[]{:S(2)}) async-start(), calls=%async_computation.53 | async-start | bytes 3244032 | tf_op jit(solution)/shard_map/reduce_scatter | solution.py:316
  1875.8 127.4 %reduce-scatter.67.cloned.1.call-start = ((), (), s32[]{:S(2)}) async-start(), calls=%async_computation.52 | async-start | bytes 3244032 | tf_op jit(solution)/shard_map/reduce_scatter | solution.py:316
  1880.7 171.2 %reduce-scatter.73.cloned.1.call-start = ((), (), s32[]{:S(2)}) async-start(), calls=%async_computation.55 | async-start | bytes 3244032 | tf_op jit(solution)/shard_map/reduce_scatter | solution.py:317
  1884.7 215.4 %reduce-scatter.71.cloned.1.call-start = ((), (), s32[]{:S(2)}) async-start(), calls=%async_computation.54 | async-start | bytes 3244032 | tf_op jit(solution)/shard_map/reduce_scatter | solution.py:317
  1888.4 260.4 %reduce-scatter.77.cloned.1.call-start = ((), (), s32[]{:S(2)}) async-start(), calls=%async_computation.57 | async-start | bytes 3244032 | tf_op jit(solution)/shard_map/reduce_scatter | solution.py:318
  1893.3 303.8 %reduce-scatter.75.cloned.1.call-start = ((), (), s32[]{:S(2)}) async-start(), calls=%async_computation.56 | async-start | bytes 3244032 | tf_op jit(solution)/shard_map/reduce_scatter | solution.py:318
  1898.1 338.4 %reduce-scatter.49.cloned.1.call-start = ((), (), s32[]{:S(2)}) async-start(), calls=%async_computation.43 | async-start | bytes 1179648 | tf_op jit(solution)/shard_map/reduce_scatter | solution.py:310
  1902.2 373.7 %reduce-scatter.47.cloned.1.call-start = ((), (), s32[]{:S(2)}) async-start(), calls=%async_computation.42 | async-start | bytes 1179648 | tf_op jit(solution)/shard_map/reduce_scatter | solution.py:310
  1929.8 385.7 %reduce-scatter.53.cloned.1.call-start = ((), (), s32[]{:S(2)}) async-start(), calls=%async_computation.45 | async-start | bytes 1179648 | tf_op jit(solution)/shard_map/reduce_scatter | solution.py:311
  1931.3 423.6 %reduce-scatter.51.cloned.1.call-start = ((), (), s32[]{:S(2)}) async-start(), calls=%async_computation.44 | async-start | bytes 1179648 | tf_op jit(solution)/shard_map/reduce_scatter | solution.py:311
  1946.7 437.8 %reduce-scatter.45.cloned.1.call-start = ((), (), s32[]{:S(2)}) async-start(), calls=%async_computation.41 | async-start | bytes 1310720 | tf_op jit(solution)/shard_map/reduce_scatter | solution.py:196
  1956.5 471.3 %reduce-scatter.57.cloned.1.call-start = ((), (), s32[]{:S(2)}) async-start(), calls=%async_computation.47 | async-start | bytes 2359296 | tf_op jit(solution)/shard_map/reduce_scatter | solution.py:312
  1958.7 514.1 %reduce-scatter.55.cloned.1.call-start = ((), (), s32[]{:S(2)}) async-start(), calls=%async_computation.46 | async-start | bytes 2359296 | tf_op jit(solution)/shard_map/reduce_scatter | solution.py:312
  1961.9 555.3 %reduce-scatter.61.cloned.1.call-start = ((), (), s32[]{:S(2)}) async-start(), calls=%async_computation.49 | async-start | bytes 2359296 | tf_op jit(solution)/shard_map/reduce_scatter | solution.py:313
  1965.0 597.1 %reduce-scatter.59.cloned.1.call-start = ((), (), s32[]{:S(2)}) async-start(), calls=%async_computation.48 | async-start | bytes 2359296 | tf_op jit(solution)/shard_map/reduce_scatter | solution.py:313
  1967.2 639.3 %reduce-scatter.65.cloned.1.call-start = ((), (), s32[]{:S(2)}) async-start(), calls=%async_computation.51 | async-start | bytes 2359296 | tf_op jit(solution)/shard_map/reduce_scatter | solution.py:315
  1970.8 680.5 %reduce-scatter.63.cloned.1.call-start = ((), (), s32[]{:S(2)}) async-start(), calls=%async_computation.50 | async-start | bytes 2359296 | tf_op jit(solution)/shard_map/reduce_scatter | solution.py:315
  (503 other events, 9077.7 us)
Sparse Core Ops, SparseCore 0:
  11.7 30.6 all-gather.38
  273.3 43.7 reduce-scatter.30
  346.5 27.9 all-gather.40
  433.9 43.8 reduce-scatter.32
  480.0 27.2 all-gather.42
  774.6 43.8 reduce-scatter.34
  847.6 27.9 all-gather.44
  904.0 27.9 all-gather.46
  967.7 27.1 reduce-scatter.38
  1387.9 26.6 reduce-scatter.40
  1416.8 42.5 reduce-scatter.36
  1462.1 27.2 all-gather.50
  1497.5 26.6 reduce-scatter.42
  1557.8 33.7 reduce-scatter.80
  1872.2 33.5 reduce-scatter.78
  1909.4 44.8 reduce-scatter.68
  1957.8 45.4 reduce-scatter.66
  2007.0 44.8 reduce-scatter.72
  2055.2 44.8 reduce-scatter.70
  2103.9 44.8 reduce-scatter.76
  2152.2 44.8 reduce-scatter.74
  2200.4 36.0 reduce-scatter.48
  2239.8 36.0 reduce-scatter.46
  2279.4 36.0 reduce-scatter.52
  2318.8 36.0 reduce-scatter.50
  2357.3 27.0 reduce-scatter.44
  2387.7 40.0 reduce-scatter.56
  2431.4 41.3 reduce-scatter.54
  2476.0 41.2 reduce-scatter.60
  2520.9 41.2 reduce-scatter.58
  2565.3 41.2 reduce-scatter.64
  2610.0 41.2 reduce-scatter.62
  (14 shorter events, 342.6 us)
where the time goes:
time: 2680 us; the launch traced here: 2660 us
  waiting for transfers between devices  1150 us (43%)
  other arithmetic  560 us (21%)
  matrix products  458 us (17%)
  local copies, waits for them, and re-layouts  330 us (12%)
  blocking collectives  122 us (5%)
    another operation x128, other arithmetic, block_step(): jax.scipy.linalg.solve_triangular(unit_lower, target, lower=True, unit_di...  330 us
    reduce_scatter x4, waiting for transfers between devices, collect_output(): lax.psum_scatter(term_fn(jnp.int32(0), lax.axis_size('tensor') * local_ro...  172 us
    reduce_scatter x4, waiting for transfers between devices, collect_grad(): lax.psum_scatter(term_fn(jnp.int32(0), local_rows * lax.axis_size('tensor...  105 us
    all_gather x4, waiting for transfers between devices, spread_cotangent(): return lax.all_gather(matrix, 'tensor', axis=0, tiled=True)  95.5 us
    reduce_scatter x2, waiting for transfers between devices, body(): lax.psum_scatter(down_grad, 'dp', scatter_dimension=0, tiled=True)  95 us
    reduce_scatter x2, waiting for transfers between devices, body(): lax.psum_scatter(up_grad, 'dp', scatter_dimension=0, tiled=True)  94.8 us
    reduce_scatter x2, waiting for transfers between devices, body(): lax.psum_scatter(gate_out_grad, 'dp', scatter_dimension=0, tiled=True)  87.5 us
    reduce_scatter x2, waiting for transfers between devices, body(): lax.psum_scatter(out_grad, 'dp', scatter_dimension=0, tiled=True)  87.3 us
  transfers between devices with their start and end apart: 46, of which 37 were waited for; matrix products, arithmetic and copies ran while one was open for 34% of the time, Pallas kernels for 0%

commit v1 on v0

v1 whole, which is shorter than its diff:
```python
import functools
import jax
import jax.numpy as jnp
from jax import lax
from jax.experimental import pallas as pl
from jax.experimental.pallas import tpu as pltpu
from jax.sharding import PartitionSpec as P

F32 = jnp.float32
BF16 = jnp.bfloat16
NN = (((1,), (0,)), ((), ()))
NT = (((1,), (1,)), ((), ()))
TN = (((0,), (0,)), ((), ()))
EPS = 1e-6
FLOOR = 0.01


def split(x):
    high = x.astype(BF16)
    return high, (x - high.astype(F32)).astype(BF16)


def mm(a, b, dims, passes=1):
    def one(p, q):
        return lax.dot_general(p, q, dims, preferred_element_type=F32)

    if passes == 1:
        return one(a.astype(BF16), b.astype(BF16))
    ah, al = split(a)
    bh, bl = split(b)
    return one(ah, bh) + (one(ah, bl) + one(al, bh))


def iota(shape, axis):
    return lax.broadcasted_iota(jnp.int32, shape, axis)


def shifted_rows(x, by):
    return pltpu.roll(x, by % x.shape[0], 0) if by else x


def conv(signal, taps, masks):
    total = signal * taps[0:1]
    for j in range(1, 4):
        total = total + shifted_rows(signal, j) * masks[j - 1] * taps[j : j + 1]
    return total


def chunk_scan(row, chunk, backward=False):
    length = row.shape[1]
    place = iota(row.shape, 1) % chunk
    step = 1
    while step < chunk:
        if backward:
            moved = pltpu.roll(row, length - step, 1)
            row = row + jnp.where(place < chunk - step, moved, 0.0)
        else:
            moved = pltpu.roll(row, step, 1)
            row = row + jnp.where(place >= step, moved, 0.0)
        step *= 2
    return row


def unit_lower_inverse(lower, refine):
    size = lower[0].shape[0]
    rows, cols = iota((size, size), 0), iota((size, size), 1)
    eye = (rows == cols).astype(F32)

    def off(block):
        return ((rows // (2 * block) == cols // (2 * block)) & (rows // block != cols // block)).astype(F32)

    found = [eye - part * off(1) for part in lower]
    block = 2
    while block < size:
        mask = off(block)
        half = [mm(x, part * mask, NN) for x, part in zip(found, lower)]
        found = [x - mm(t, x, NN) for x, t in zip(found, half)]
        block *= 2
    for _ in range(refine):
        rest = [(x - eye) + mm(part, x, NN, 3) for x, part in zip(found, lower)]
        found = [x - mm(x, r, NN, 1) for x, r in zip(found, rest)]
    return found


def prepared(head, chunk, qref, kref, vref, pair_ref, tap_qk, tap_v, head_table, col_info, row_info):
    length, dk = qref.shape
    masks = [col_info[:, j : j + 1] for j in range(3)]
    masks = [jnp.broadcast_to(m, (length, dk)) for m in masks]
    dv = vref.shape[1]
    wide = [jnp.concatenate([m] * (dv // dk), axis=1) for m in masks]
    pre_q = conv(qref[...], tap_qk[0], masks)
    pre_k = conv(kref[...], tap_qk[1], masks)
    pre_v = conv(vref[...], tap_v[...], wide)
    out = dict(masks=masks, wide=wide, pre_q=pre_q, pre_k=pre_k, pre_v=pre_v)
    for name, pre in (("q", pre_q), ("k", pre_k), ("v", pre_v)):
        sig = lax.logistic(pre)
        out["sig_" + name] = sig
        out["act_" + name] = pre * sig
    out["inv_q"] = lax.rsqrt(jnp.sum(out["act_q"] ** 2, axis=1, keepdims=True) + EPS)
    out["inv_k"] = lax.rsqrt(jnp.sum(out["act_k"] ** 2, axis=1, keepdims=True) + EPS)
    out["q"] = out["act_q"] * out["inv_q"] * dk ** (-0.5)
    out["k"] = out["act_k"] * out["inv_k"]
    out["v"] = out["act_v"]
    pair = jnp.transpose(pair_ref[...])
    picked = iota(pair.shape, 0)
    a_row = jnp.sum(jnp.where(picked == 2 * head, pair, 0.0), axis=0, keepdims=True)
    b_row = jnp.sum(jnp.where(picked == 2 * head + 1, pair, 0.0), axis=0, keepdims=True)
    rate = jnp.exp(jnp.full((1, length), head_table[0, head], F32))
    a_row = a_row + head_table[1, head]
    softplus = jnp.maximum(a_row, 0.0) + jnp.log1p(jnp.exp(-jnp.abs(a_row)))
    decay = -rate * softplus
    beta = lax.logistic(b_row)
    total = chunk_scan(decay, chunk)
    entry = jnp.exp(total) * row_info[0:1]
    chunks = length // chunk
    place = iota((1, length), 1)
    ends = [total[:, (i + 1) * chunk - 1 : (i + 1) * chunk] for i in range(chunks)]
    last = ends[0]
    for i in range(1, chunks):
        last = jnp.where(place >= i * chunk, ends[i], jnp.broadcast_to(last, (1, length)))
    tail = jnp.exp(last - total) * row_info[1:2]
    rows = jnp.concatenate([beta, total, entry, tail, jnp.zeros((124, length), F32)], axis=0)
    cols = jnp.transpose(rows)
    out.update(
        a_row=a_row, rate=rate, decay=decay, beta_row=beta, total_row=total, entry_row=entry, tail_row=tail,
        beta=cols[:, 0:1], total=cols[:, 1:2], entry=cols[:, 2:3], tail=cols[:, 3:4],
    )
    return out


def chunk_parts(pre, i, chunk, col_info, row_info):
    s = slice(i * chunk, (i + 1) * chunk)
    q, k, v = pre["q"][s], pre["k"][s], pre["v"][s]
    beta, total, entry, tail = pre["beta"][s], pre["total"][s], pre["entry"][s], pre["tail"][s]
    rows, cols = iota((chunk, chunk), 0), iota((chunk, chunk), 1)
    allowed = (col_info[s, 3:4] == row_info[2:3, s]) & (rows >= cols)
    fading = jnp.where(allowed, jnp.exp(jnp.where(allowed, total - pre["total_row"][:, s], 0.0)), 0.0)
    both = mm(jnp.concatenate([q, k], axis=0), k, NT)
    strict_fading = jnp.where(rows > cols, fading, 0.0)
    qk, kk = both[:chunk], both[chunk:]
    return dict(
        q=q, k=k, v=v, beta=beta, entry=entry, tail=tail, fading=fading, strict=strict_fading,
        mixed=qk * fading, kk_faded=kk * strict_fading, lower=beta * (kk * strict_fading),
        exit=pre["entry_row"][:, (i + 1) * chunk - 1 : (i + 1) * chunk], rows=s,
    )


def forward_kernel(
    chunk, refine, qref, kref, vref, gref, pair_ref, tap_qk, tap_v, head_table, gain, col_ref, row_ref,
    mix_ref, rec_ref, fix_ref, inv_ref, state_ref,
):
    head = pl.program_id(1)
    col_info, row_info = col_ref[0], row_ref[0]
    pre = prepared(head, chunk, qref, kref, vref, pair_ref, tap_qk, tap_v, head_table, col_info, row_info)
    length, dk = qref.shape
    dv = vref.shape[1]
    chunks = length // chunk
    parts = [chunk_parts(pre, i, chunk, col_info, row_info) for i in range(chunks)]
    inverses = unit_lower_inverse([p["lower"] for p in parts], refine)
    state = jnp.zeros((dk, dv), F32)
    steps = []
    for p, inverse in zip(parts, inverses):
        target = jnp.concatenate([p["beta"] * p["entry"] * p["k"], p["beta"] * p["v"]], axis=1)
        solved = mm(inverse, target, NN)
        pushed = mm(p["k"] * p["tail"], solved, TN)
        steps.append((solved, pushed))
    states = []
    for p, (solved, pushed) in zip(parts, steps):
        states.append(state)
        state = p["exit"] * state - mm(pushed[:, :dk], state, NN) + pushed[:, dk:]
    gain_row = gain[...]
    for i, (p, inverse, (solved, pushed)) in enumerate(zip(parts, inverses, steps)):
        seen = mm(jnp.concatenate([solved[:, :dk], p["q"] * p["entry"]], axis=0), states[i], NN)
        fixed = solved[:, dk:] - seen[:chunk]
        rec = seen[chunk:] + mm(p["mixed"], fixed, NN)
        s = p["rows"]
        rec_ref[s, :] = rec
        fix_ref[s, :] = fixed
        inv_ref[0, 0, i] = inverse
        state_ref[0, 0, i] = states[i]
        normal = rec * lax.rsqrt(jnp.mean(rec * rec, axis=1, keepdims=True) + FLOOR)
        gate = gref[s, :]
        mix_ref[s, :] = (normal * gain_row * (gate * lax.logistic(gate))).astype(BF16)


def silu_grad(pre, sig):
    return sig * (1.0 + pre * (1.0 - sig))


def backward_kernel(
    chunk, heads, qref, kref, vref, gref, pair_ref, tap_qk, tap_v, head_table, gain, col_ref, row_ref,
    rec_ref, fix_ref, inv_ref, state_ref, dmix_ref,
    dproj_ref, dtap_qk, dtap_v, dhead_ref, dgain_ref,
):
    seq, head = pl.program_id(0), pl.program_id(1)
    col_info, row_info = col_ref[0], row_ref[0]
    pre = prepared(head, chunk, qref, kref, vref, pair_ref, tap_qk, tap_v, head_table, col_info, row_info)
    length, dk = qref.shape
    dv = vref.shape[1]
    chunks = length // chunk
    parts = [chunk_parts(pre, i, chunk, col_info, row_info) for i in range(chunks)]
    gain_row = gain[...]
    dgain = jnp.zeros((1, dv), F32)
    v_at = 2 * heads * dk
    g_at = v_at + heads * dv
    p_at = g_at + heads * dv
    for p in parts:
        s = p["rows"]
        rec, gate, dmix = rec_ref[s, :], gref[s, :], dmix_ref[s, :]
        scale = lax.rsqrt(jnp.mean(rec * rec, axis=1, keepdims=True) + FLOOR)
        sig = lax.logistic(gate)
        gated = dmix * (gate * sig)
        normal = rec * scale
        dgain = dgain + jnp.sum(gated * normal, axis=0, keepdims=True)
        dgate = dmix * normal * gain_row * silu_grad(gate, sig)
        dproj_ref[s, pl.ds(pl.multiple_of(g_at + head * dv, dv), dv)] = dgate.astype(BF16)
        dn = gated * gain_row
        p["drec"] = scale * dn - rec * (scale * scale * scale) * jnp.mean(dn * rec, axis=1, keepdims=True)
    for i, p in enumerate(parts):
        inverse = inv_ref[0, 0, i]
        p["inverse"] = inverse
        solved = mm(inverse, p["beta"] * p["entry"] * p["k"], NN)
        back = mm(p["mixed"], p["drec"], TN)
        p["back"] = back
        ahead = mm(solved, p["k"] * p["tail"], TN)
        given = mm(
            jnp.concatenate([p["q"] * p["entry"], -solved], axis=0),
            jnp.concatenate([p["drec"], back], axis=0), TN,
        )
        p["ahead"], p["given"] = ahead, given
    dstate = jnp.zeros((dk, dv), F32)
    for p in reversed(parts):
        p["dstate"] = dstate
        dstate = p["exit"] * dstate - mm(p["ahead"], dstate, NN) + p["given"]
    cols = iota((chunk, 8), 1)
    col_parts, row_parts, dqs, dks, dvs = [], [], [], [], []
    for i, p in enumerate(parts):
        s = p["rows"]
        state, dstate, fixed, drec = state_ref[0, 0, i], p["dstate"], fix_ref[s, :], p["drec"]
        q, k, v, beta, entry, tail = p["q"], p["k"], p["v"], p["beta"], p["entry"], p["tail"]
        dfixed = p["back"] + mm(k * tail, dstate, NN)
        dtarget = mm(p["inverse"], dfixed, TN)
        outer = mm(
            jnp.concatenate([drec, dtarget], axis=0), jnp.concatenate([state, fixed], axis=0), NT
        )
        drec_state, dtarget_state = outer[:chunk, :dk], outer[chunk:, :dk]
        dmixed, dlower = outer[:chunk, dk:], -outer[chunk:, dk:]
        fixed_dstate = mm(fixed, dstate, NT)
        g1 = dmixed * p["fading"]
        g2 = (beta * dlower) * p["strict"]
        stacked = jnp.concatenate([g1, g2], axis=0)
        first = mm(stacked, k, NN)
        second = mm(stacked, jnp.concatenate([q, k], axis=0), TN)
        key_state = jnp.sum(dtarget_state * k, axis=1, keepdims=True)
        dqs.append(entry * drec_state + first[:chunk])
        dks.append(first[chunk:] + second + tail * fixed_dstate - (beta * entry) * dtarget_state)
        dvs.append(beta * dtarget)
        dentry = jnp.sum(drec_state * q, axis=1, keepdims=True) - beta * key_state
        dtail = jnp.sum(fixed_dstate * k, axis=1, keepdims=True) * tail
        high = dmixed * p["mixed"] + dlower * p["lower"]
        dbeta = (
            jnp.sum(dtarget * v, axis=1, keepdims=True)
            - entry * key_state
            + jnp.sum(dlower * p["kk_faded"], axis=1, keepdims=True)
        )
        dtotal = jnp.sum(high, axis=1, keepdims=True) + dentry * entry - dtail
        end = p["exit"] * jnp.sum(jnp.sum(dstate * state, axis=1, keepdims=True), axis=0, keepdims=True)
        end = end + jnp.sum(dtail, axis=0, keepdims=True)
        dtotal = dtotal + jnp.where(iota((chunk, 1), 0) == chunk - 1, end, 0.0)
        row_parts.append(jnp.sum(high, axis=0, keepdims=True))
        col_parts.append(jnp.where(cols == 0, dtotal, jnp.where(cols == 1, dbeta, 0.0)))
    lanes = jnp.concatenate(col_parts, axis=0)
    lanes = jnp.concatenate([lanes, jnp.zeros((length, 120), F32)], axis=1)
    turned = jnp.transpose(lanes)
    dtotal_row = turned[0:1] - jnp.concatenate(row_parts, axis=1)
    dbeta_row = turned[1:2]
    ddecay = chunk_scan(dtotal_row, chunk, backward=True)
    da = -ddecay * pre["rate"] * lax.logistic(pre["a_row"])
    db = dbeta_row * pre["beta_row"] * (1.0 - pre["beta_row"])
    spread = iota((128, length), 0)
    dpair = jnp.where(spread == 2 * head, da, jnp.where(spread == 2 * head + 1, db, 0.0))
    dpair = jnp.transpose(dpair).astype(BF16)

    @pl.when(head == 0)
    def _():
        dproj_ref[:, p_at:] = dpair

    @pl.when(head != 0)
    def _():
        dproj_ref[:, p_at:] = dproj_ref[:, p_at:] + dpair

    dscale = jnp.sum(ddecay * pre["decay"], axis=1, keepdims=True)
    dbias = jnp.sum(da, axis=1, keepdims=True)
    which = iota((8, 128), 0)
    dhead = jnp.where(which == 0, dscale, jnp.where(which == 1, dbias, 0.0))
    dq, dk_all, dv_all = (jnp.concatenate(x, axis=0) for x in (dqs, dks, dvs))

    def through_norm(grad, act, inv, factor):
        return factor * (inv * grad - act * (inv * inv * inv) * jnp.sum(grad * act, axis=1, keepdims=True))

    dq = through_norm(dq, pre["act_q"], pre["inv_q"], dk ** (-0.5))
    dk_all = through_norm(dk_all, pre["act_k"], pre["inv_k"], 1.0)
    taps_out = []
    for grad, name, src, taps, masks, at in (
        (dq, "q", qref, tap_qk[0], pre["masks"], head * dk),
        (dk_all, "k", kref, tap_qk[1], pre["masks"], heads * dk + head * dk),
        (dv_all, "v", vref, tap_v[...], pre["wide"], v_at + head * dv),
    ):
        dpre = grad * silu_grad(pre["pre_" + name], pre["sig_" + name])
        signal = src[...]
        dsignal = dpre * taps[0:1]
        dtaps = [jnp.sum(dpre * signal, axis=0, keepdims=True)]
        for j in range(1, 4):
            masked = dpre * masks[j - 1]
            dsignal = dsignal + shifted_rows(masked, -j) * taps[j : j + 1]
            dtaps.append(jnp.sum(masked * shifted_rows(signal, j), axis=0, keepdims=True))
        width = grad.shape[1]
        dproj_ref[:, pl.ds(pl.multiple_of(at, width), width)] = dsignal.astype(BF16)
        taps_out.append(jnp.concatenate(dtaps, axis=0))
    dtap_qk[0, 0] = taps_out[0]
    dtap_qk[0, 1] = taps_out[1]
    dtap_v[0] = taps_out[2]
    dhead_ref[0, 0] = dhead
    dgain_ref[0, 0] = dgain


def specs(length, heads, dk, dv):
    v_block = 2 * heads * dk // dv
    return [
        pl.BlockSpec((length, dk), lambda s, h: (s, h)),
        pl.BlockSpec((length, dk), lambda s, h: (s, heads + h)),
        pl.BlockSpec((length, dv), lambda s, h: (s, v_block + h)),
        pl.BlockSpec((length, dv), lambda s, h: (s, v_block + heads + h)),
        pl.BlockSpec((length, 128), lambda s, h: (s, (2 * heads * dk + 2 * heads * dv) // 128)),
        pl.BlockSpec((2, 4, dk), lambda s, h: (0, 0, h)),
        pl.BlockSpec((4, dv), lambda s, h: (0, h)),
        pl.BlockSpec(memory_space=pltpu.SMEM),
        pl.BlockSpec((1, dv), lambda s, h: (0, 0)),
        pl.BlockSpec((1, length, 8), lambda s, h: (s, 0, 0)),
        pl.BlockSpec((1, 8, length), lambda s, h: (s, 0, 0)),
    ]


def segment_tables(segment_ids, chunk):
    seqs, length = segment_ids.shape
    place = jnp.arange(length)
    conv_masks = []
    for j in range(1, 4):
        earlier = jnp.pad(segment_ids, ((0, 0), (j, 0)), constant_values=-1)[:, :length]
        conv_masks.append(earlier == segment_ids)
    blocks = segment_ids.reshape(seqs, length // chunk, chunk)
    finals = blocks[:, :, -1]
    before = jnp.concatenate([segment_ids[:, :1], finals[:, :-1]], axis=1)
    carried = (blocks == before[:, :, None]).reshape(seqs, length)
    tailed = (blocks == finals[:, :, None]).reshape(seqs, length)
    zero = jnp.zeros((seqs, length), F32)
    ids = segment_ids.astype(F32)
    rows = jnp.stack([carried.astype(F32), tailed.astype(F32), ids] + [zero] * 5, axis=1)
    cols = jnp.stack([m.astype(F32) for m in conv_masks] + [ids] + [zero] * 4, axis=2)
    return cols, rows


def delta_forward(proj, taps_qk, taps_v, head_table, gain, tables, seqs, heads, chunk, refine):
    cols, rows = tables
    length = cols.shape[1]
    dk, dv = taps_qk.shape[2] // heads, taps_v.shape[1] // heads
    chunks = length // chunk
    tokens = seqs * length
    column = pl.BlockSpec((length, dv), lambda s, h: (s, h))
    return pl.pallas_call(
        functools.partial(forward_kernel, chunk, refine),
        grid=(seqs, heads),
        in_specs=specs(length, heads, dk, dv),
        out_specs=[
            column, column, column,
            pl.BlockSpec((1, 1, chunks, chunk, chunk), lambda s, h: (s, h, 0, 0, 0)),
            pl.BlockSpec((1, 1, chunks, dk, dv), lambda s, h: (s, h, 0, 0, 0)),
        ],
        out_shape=[
            jax.ShapeDtypeStruct((tokens, heads * dv), BF16),
            jax.ShapeDtypeStruct((tokens, heads * dv), F32),
            jax.ShapeDtypeStruct((tokens, heads * dv), F32),
            jax.ShapeDtypeStruct((seqs, heads, chunks, chunk, chunk), F32),
            jax.ShapeDtypeStruct((seqs, heads, chunks, dk, dv), F32),
        ],
        compiler_params=pltpu.CompilerParams(vmem_limit_bytes=48 * 2**20),
        name="delta_forward",
    )(proj, proj, proj, proj, proj, taps_qk, taps_v, head_table, gain, cols, rows)


def delta_backward(proj, taps_qk, taps_v, head_table, gain, tables, saved, dmix, seqs, heads, chunk):
    cols, rows = tables
    length = cols.shape[1]
    dk, dv = taps_qk.shape[2] // heads, taps_v.shape[1] // heads
    chunks = length // chunk
    tokens = seqs * length
    width = proj.shape[1]
    column = pl.BlockSpec((length, dv), lambda s, h: (s, h))
    return pl.pallas_call(
        functools.partial(backward_kernel, chunk, heads),
        grid=(seqs, heads),
        in_specs=specs(length, heads, dk, dv)
        + [
            column, column,
            pl.BlockSpec((1, 1, chunks, chunk, chunk), lambda s, h: (s, h, 0, 0, 0)),
            pl.BlockSpec((1, 1, chunks, dk, dv), lambda s, h: (s, h, 0, 0, 0)),
            column,
        ],
        out_specs=[
            pl.BlockSpec((length, width), lambda s, h: (s, 0)),
            pl.BlockSpec((1, 2, 4, dk), lambda s, h: (s, 0, 0, h)),
            pl.BlockSpec((1, 4, dv), lambda s, h: (s, 0, h)),
            pl.BlockSpec((1, 1, 8, 128), lambda s, h: (s, h, 0, 0)),
            pl.BlockSpec((1, 1, 1, dv), lambda s, h: (s, h, 0, 0)),
        ],
        out_shape=[
            jax.ShapeDtypeStruct((tokens, width), BF16),
            jax.ShapeDtypeStruct((seqs, 2, 4, heads * dk), F32),
            jax.ShapeDtypeStruct((seqs, 4, heads * dv), F32),
            jax.ShapeDtypeStruct((seqs, heads, 8, 128), F32),
            jax.ShapeDtypeStruct((seqs, heads, 1, dv), F32),
        ],
        compiler_params=pltpu.CompilerParams(vmem_limit_bytes=56 * 2**20),
        name="delta_backward",
    )(proj, proj, proj, proj, proj, taps_qk, taps_v, head_table, gain, cols, rows, *saved, dmix)


LAYERS = 2
CHUNK = 128
REFINE = 1


def rms_gain(matrix, gain_vector):
    scaling = lax.rsqrt(jnp.mean(matrix * matrix, axis=-1, keepdims=True) + EPS)
    return matrix * scaling * gain_vector


def times_transposed(left, right):
    return lax.dot_general(left, right, NT, preferred_element_type=F32)


def over_rows(left, right):
    return lax.dot_general(left, right, TN, preferred_element_type=F32)


def times(left, right):
    return jnp.dot(left, right, preferred_element_type=F32)


def padded(matrix, width):
    return jnp.pad(matrix, ((0, 0), (0, width - matrix.shape[1])))


def up_to(size, unit):
    return -(-size // unit) * unit


def body(
    tokens,
    segment_ids,
    query_weight,
    key_weight,
    value_weight,
    gate_weight,
    decay_weight,
    out_weight,
    swiglu_gate,
    swiglu_up,
    swiglu_down,
    conv_query_key,
    conv_value,
    head_params,
    norm_gains,
    out_gain,
    cotangent,
):
    seqs, length = segment_ids.shape
    heads = head_params.shape[2]
    qk_width, v_width, pair_width = query_weight.shape[2], value_weight.shape[2], decay_weight.shape[2]
    hidden_width = swiglu_gate.shape[2]
    hidden_pad = up_to(hidden_width, 128)
    in_width = 2 * qk_width + 2 * v_width + 128
    tables = segment_tables(segment_ids, CHUNK)

    def gathered(matrix):
        return lax.all_gather(matrix, "dp", axis=0, tiled=True)

    def layer_weights(l):
        low = lambda m: m[l].astype(BF16)
        first = gathered(jnp.concatenate(
            [low(query_weight), low(key_weight), low(value_weight), low(gate_weight), padded(low(decay_weight), 128)], axis=1
        ))
        second = gathered(jnp.concatenate(
            [low(out_weight), padded(low(swiglu_gate), hidden_pad), padded(low(swiglu_up), hidden_pad),
             padded(low(swiglu_down), hidden_pad)], axis=1
        ))
        return (
            first, second[:, :v_width], second[:, v_width : v_width + 2 * hidden_pad], second[:, v_width + 2 * hidden_pad :]
        )

    def spread(matrix):
        return lax.all_gather(matrix.astype(BF16), "tensor", axis=0, tiled=True)

    def collect(term):
        return lax.psum_scatter(term.astype(BF16), "tensor", scatter_dimension=0, tiled=True).astype(F32)

    residual = tokens.astype(F32)
    kept = []
    for l in range(LAYERS):
        w_in, w_out, w_up, w_down = layer_weights(l)
        first_norm, first_back = jax.vjp(rms_gain, residual, norm_gains[l, 0])
        normed = spread(first_norm)
        proj = times(normed, w_in)
        small = (conv_query_key[l], conv_value[l], head_params[l], out_gain[l][None])
        mixer, *saved = delta_forward(proj, *small, tables, seqs, heads, CHUNK, REFINE)
        middle = residual + collect(times_transposed(mixer, w_out))
        second_norm, second_back = jax.vjp(rms_gain, middle, norm_gains[l, 1])
        normed_ffn = spread(second_norm)
        pre = times(normed_ffn, w_up)
        hidden = (jax.nn.silu(pre[:, :hidden_pad]) * pre[:, hidden_pad:]).astype(BF16)
        residual = middle + collect(times_transposed(hidden, w_down))
        kept.append((w_in, w_out, w_up, w_down, first_back, normed, proj, small, mixer, saved, second_back, normed_ffn, pre, hidden))
    grad = cotangent.astype(F32)
    ffn_grads, mixer_grads, tap_grads, norm_grads, gain_grads = ([None] * LAYERS for _ in range(5))
    for l in reversed(range(LAYERS)):
        w_in, w_out, w_up, w_down, first_back, normed, proj, small, mixer, saved, second_back, normed_ffn, pre, hidden = kept[l]
        ffn_cot = spread(grad)
        down_grad = over_rows(ffn_cot, hidden)
        d_hidden = times(ffn_cot, w_down)
        gate_pre, up_pre = pre[:, :hidden_pad], pre[:, hidden_pad:]
        sig = jax.nn.sigmoid(gate_pre)
        d_pre = jnp.concatenate(
            [d_hidden * up_pre * sig * (1.0 + gate_pre * (1.0 - sig)), d_hidden * gate_pre * sig], axis=1
        ).astype(BF16)
        d_middle, second_gain = second_back(collect(times_transposed(d_pre, w_up)))
        up_grad = over_rows(normed_ffn, d_pre)
        ffn_grads[l] = lax.psum_scatter(
            jnp.concatenate([down_grad, up_grad], axis=1).astype(BF16), "dp", scatter_dimension=0, tiled=True
        )
        grad = grad + d_middle
        mixer_cot = spread(grad)
        d_mixer = times(mixer_cot, w_out)
        d_proj, d_qk, d_v, d_head, d_gain = delta_backward(
            proj, *small, tables, saved, d_mixer, seqs, heads, CHUNK
        )
        d_input, first_gain = first_back(collect(times_transposed(d_proj, w_in)))
        out_grad = over_rows(mixer_cot, mixer)
        in_grad = over_rows(normed, d_proj)
        mixer_grads[l] = lax.psum_scatter(
            jnp.concatenate([out_grad, in_grad], axis=1).astype(BF16), "dp", scatter_dimension=0, tiled=True
        )
        grad = grad + d_input
        tap_grads[l] = (d_qk.sum(0), d_v.sum(0), d_head.sum(0)[:, :2, 0].T)
        norm_grads[l] = jnp.stack([first_gain, second_gain])
        gain_grads[l] = d_gain.sum((0, 1, 2))

    def columns(parts, start, width):
        return jnp.stack([part[:, start : start + width] for part in parts]).astype(F32)

    at = v_width
    in_grads = []
    for width in (qk_width, qk_width, v_width, v_width, pair_width):
        in_grads.append(columns(mixer_grads, at, width))
        at += width
    out_grad = columns(mixer_grads, 0, v_width)
    down_grad = columns(ffn_grads, 0, hidden_width)
    gate_grad = columns(ffn_grads, hidden_pad, hidden_width)
    up_grad = columns(ffn_grads, 2 * hidden_pad, hidden_width)
    taps = tuple(jnp.stack([tap_grads[l][i] for l in range(LAYERS)]) for i in range(3))
    taps = lax.psum(taps, "dp")
    norms = lax.psum((jnp.stack(norm_grads), jnp.stack(gain_grads)), ("dp", "tensor"))
    return (residual, grad, *in_grads, out_grad, gate_grad, up_grad, down_grad, *taps, *norms)


def solution(mesh):
    rows = P(("dp", "tensor"), None)
    weight = P(None, "dp", "tensor")
    small = (P(None, None, None, "tensor"), P(None, None, "tensor"), P(None, None, "tensor"), P(), P())
    return jax.shard_map(
        body,
        mesh=mesh,
        in_specs=(rows, P("dp", None)) + (weight,) * 9 + small + (rows,),
        out_specs=(rows, rows) + (weight,) * 9 + small,
        check_vma=False,
    )
```

time: 2680 us -> 950 us (0.35)
  waiting for transfers between devices: 1150 us -> 616 us
  other arithmetic: 560 us -> 44 us
  matrix products: 458 us -> 91.1 us
  local copies, waits for them, and re-layouts: 330 us -> 37.2 us
  Pallas kernels: 0 us -> 70.1 us
  blocking collectives: 122 us -> 64.2 us
    reduce_scatter x24 -> x12, waiting for transfers between devices: 842 us -> 308 us  [the longest x8 185 us: collect(): lax.psum_scatter(term.astype(BF16), 'tensor', scatter_dimension=0, tiled=...]
    another operation x234 -> x14, other arithmetic: 387 us -> 2.95 us  [the longest x128 330 us: block_step(): jax.scipy.linalg.solve_triangular(unit_lower, target, lower=True, unit_di...]
    dot_general x420 -> x24, matrix products: 396 us -> 91.1 us  [the longest x8 37.7 us: times(): return jnp.dot(left, right, preferred_element_type=F32)]
    pallas_call x0 -> x4, Pallas kernels: none -> 70.1 us  [the longest x2 45.4 us: delta_backward(): pl.pallas_call(functools.partial(backward_kernel, chunk, heads), grid=(se...]
    squeeze x80 -> x3, local copies, waits for them, and re-layouts: 62.1 us -> 0.01 us  [the longest x1 0.01 us: body(): conv_query_key[l]]
    mul x137 -> x0, other arithmetic: 59.3 us -> none  [the longest x64 31 us: block_step(): entry_scale = jnp.exp(cumulative) * carried_mask]
    another operation x64 -> x0, matrix products: 59 us -> none  [block_step(): jax.scipy.linalg.solve_triangular(unit_lower, target, lower=True, unit_di...]
    all_gather x6 -> x0, blocking collectives: 57.8 us -> none  [the longest x2 20.2 us: layer_weights(): lax.all_gather(decay_weight[layer_idx].astype(jnp.bfloat16), 'dp', axis=0...]
  transfers between devices with their start and end apart: 46 -> 24, of which waited for: 37 -> 24; matrix products, arithmetic and copies ran while one was open for 34% -> 10% of each run, Pallas kernels for 0% -> 5%
where the time goes in v1:
time: 950 us; the launch traced here: 940 us
  waiting for transfers between devices  616 us (65%)
  matrix products  91.1 us (10%)
  Pallas kernels  70.1 us (7%)
  blocking collectives  64.2 us (7%)
  other arithmetic  44 us (5%)
  local copies, waits for them, and re-layouts  37.2 us (4%)
  between operations  15.7 us (2%)
    all_gather x8, waiting for transfers between devices, spread(): return lax.all_gather(matrix.astype(BF16), 'tensor', axis=0, tiled=True)  191 us
    reduce_scatter x8, waiting for transfers between devices, collect(): lax.psum_scatter(term.astype(BF16), 'tensor', scatter_dimension=0, tiled=...  185 us
    all_gather x4, waiting for transfers between devices, gathered(): return lax.all_gather(matrix, 'dp', axis=0, tiled=True)  115 us
    reduce_scatter x2, waiting for transfers between devices, body(): lax.psum_scatter(jnp.concatenate([out_grad, in_grad], axis=1).astype(BF16...  107 us
    pallas_call x2, Pallas kernels, delta_backward(): pl.pallas_call(functools.partial(backward_kernel, chunk, heads), grid=(se...  45.4 us
    psum x1, blocking collectives, body(): lax.psum((jnp.stack(norm_grads), jnp.stack(gain_grads)), ('dp', 'tensor'))  39.5 us
    dot_general x8, matrix products, times(): return jnp.dot(left, right, preferred_element_type=F32)  37.7 us
    dot_general x8, matrix products, times_transposed(): return lax.dot_general(left, right, NT, preferred_element_type=F32)  31.7 us
  transfers between devices with their start and end apart: 24, of which 24 were waited for; matrix products, arithmetic and copies ran while one was open for 10% of the time, Pallas kernels for 5%

profile of v1, /device:TPU:0, one launch (start us, length us, event | category | flops | bytes accessed | tf_op | source)
XLA Modules:
  0.0 940.2 jit_solution(3300357097218079030)
XLA Ops:
  22.0 19.8 %all-gather.13.cloned.1.call-done = bf16[512,1024]{1,0:T(8,128)(2,1)} async-done(((bf16[128,1024]{1,0:T(8,128)(2,1)}), bf16[512,1024]{1,0:T(8,128)(2,1)}) %all-gather.13.cloned.1.call-update) | async-done | bytes 1048592 | tf_op jit(solution)/shard_map/all_gather | solution.py:502
  41.8 35.4 %all-gather.15.cloned.1.call-done = bf16[1024,1664]{1,0:T(8,128)(2,1)} async-done(((bf16[128,1664]{1,0:T(8,128)(2,1)}), bf16[1024,1664]{1,0:T(8,128)(2,1)}) %all-gather.15.cloned.1.call-update) | async-done | bytes 3407888 | tf_op jit(solution)/shard_map/all_gather | solution.py:486
  77.2 6.1 fusion.95.qref.kref.vref.gref.pair_ref
  83.4 12.3 %delta_forward.2 = (bf16[512,512]{1,0:T(8,128)(2,1)S(1)}, f32[512,512]{1,0:T(8,128)S(1)}, f32[512,512]{1,0:T(8,128)S(1)}, f32[1,2,4,128,128]{4,3,2,1,0:T(8,128)S(1)}, f32[1,2,4,128,256]{4,3,2,1,0:T(8,128)S(1)}) custom-call(f32[512,1664]{1,0:T(8,128)} %fusion.95.qref.kref.vref.gref.pair_ref, f32[512,1664]{1,0:T(8,128)} %fusion.95.qref.kref.vref.gref.pair_ref, ...), custom_call_target="tpu_custom_call" | custom-call | tf_op jit(solution)/shard_map/delta_forward/pallas_call | solution.py:370
  99.5 24.5 %all-gather.17.cloned.1.call-done = bf16[1024,2816]{0,1:T(8,128)(2,1)} async-done(((bf16[128,2816]{0,1:T(8,128)(2,1)}), bf16[1024,2816]{0,1:T(8,128)(2,1)}) %all-gather.17.cloned.1.call-update) | async-done | bytes 5767184 | tf_op jit(solution)/shard_map/all_gather | solution.py:486
  127.1 27.2 %reduce-scatter.13.cloned.1.call-done = bf16[128,1024]{1,0:T(8,128)(2,1)} async-done(((bf16[512,1024]{1,0:T(8,128)(2,1)}), bf16[128,1024]{1,0:T(8,128)(2,1)}) %reduce-scatter.13.cloned.1.call-update) | async-done | bytes 262160 | tf_op jit(solution)/shard_map/reduce_scatter | solution.py:505
  157.3 26.7 %all-gather.19.cloned.1.call-done = bf16[512,1024]{1,0:T(8,128)(2,1)} async-done(((bf16[128,1024]{1,0:T(8,128)(2,1)}), bf16[512,1024]{1,0:T(8,128)(2,1)}) %all-gather.19.cloned.1.call-update) | async-done | bytes 1048592 | tf_op jit(solution)/shard_map/all_gather | solution.py:502
  195.4 25.9 %reduce-scatter.15.cloned.1.call-done = bf16[128,1024]{1,0:T(8,128)(2,1)} async-done(((bf16[512,1024]{1,0:T(8,128)(2,1)}), bf16[128,1024]{1,0:T(8,128)(2,1)}) %reduce-scatter.15.cloned.1.call-update) | async-done | bytes 262160 | tf_op jit(solution)/shard_map/reduce_scatter | solution.py:505
  224.6 31.3 %all-gather.23.cloned.1.call-done = bf16[1024,1664]{1,0:T(8,128)(2,1)} async-done(((bf16[128,1664]{1,0:T(8,128)(2,1)}), bf16[1024,1664]{1,0:T(8,128)(2,1)}) %all-gather.23.cloned.1.call-update) | async-done | bytes 3407888 | tf_op jit(solution)/shard_map/all_gather | solution.py:486
  255.9 30.1 %all-gather.21.cloned.1.call-done = bf16[512,1024]{1,0:T(8,128)(2,1)} async-done(((bf16[128,1024]{1,0:T(8,128)(2,1)}), bf16[512,1024]{1,0:T(8,128)(2,1)}) %all-gather.21.cloned.1.call-update) | async-done | bytes 1048592 | tf_op jit(solution)/shard_map/all_gather | solution.py:502
  286.0 6.1 fusion.96.qref.kref.vref.gref.pair_ref
  292.2 12.4 %delta_forward.3 = (bf16[512,512]{1,0:T(8,128)(2,1)S(1)}, f32[512,512]{1,0:T(8,128)S(1)}, f32[512,512]{1,0:T(8,128)S(1)}, f32[1,2,4,128,128]{4,3,2,1,0:T(8,128)S(1)}, f32[1,2,4,128,256]{4,3,2,1,0:T(8,128)S(1)}) custom-call(f32[512,1664]{1,0:T(8,128)} %fusion.96.qref.kref.vref.gref.pair_ref, f32[512,1664]{1,0:T(8,128)} %fusion.96.qref.kref.vref.gref.pair_ref, ...), custom_call_target="tpu_custom_call" | custom-call | tf_op jit(solution)/shard_map/delta_forward/pallas_call | solution.py:370
  308.3 24.0 %all-gather.25.cloned.1.call-done = bf16[1024,2816]{0,1:T(8,128)(2,1)} async-done(((bf16[128,2816]{0,1:T(8,128)(2,1)}), bf16[1024,2816]{0,1:T(8,128)(2,1)}) %all-gather.25.cloned.1.call-update) | async-done | bytes 5767184 | tf_op jit(solution)/shard_map/all_gather | solution.py:486
  335.4 27.2 %reduce-scatter.17.cloned.1.call-done = bf16[128,1024]{1,0:T(8,128)(2,1)} async-done(((bf16[512,1024]{1,0:T(8,128)(2,1)}), bf16[128,1024]{1,0:T(8,128)(2,1)}) %reduce-scatter.17.cloned.1.call-update) | async-done | bytes 262160 | tf_op jit(solution)/shard_map/reduce_scatter | solution.py:505
  366.2 26.1 %all-gather.27.cloned.1.call-done = bf16[512,1024]{1,0:T(8,128)(2,1)} async-done(((bf16[128,1024]{1,0:T(8,128)(2,1)}), bf16[512,1024]{1,0:T(8,128)(2,1)}) %all-gather.27.cloned.1.call-update) | async-done | bytes 1048592 | tf_op jit(solution)/shard_map/all_gather | solution.py:502
  392.3 5.7 fusion.2
  398.0 23.3 %all-gather.29.cloned.1.call-done = bf16[512,1024]{1,0:T(8,128)(2,1)} async-done(((bf16[128,1024]{1,0:T(8,128)(2,1)}), bf16[512,1024]{1,0:T(8,128)(2,1)}) %all-gather.29.cloned.1.call-update) | async-done | bytes 1048592 | tf_op jit(solution)/shard_map/all_gather | solution.py:502
  421.3 5.1 fusion.10
  432.4 26.7 %reduce-scatter.21.cloned.1.call-done = bf16[128,1024]{1,0:T(8,128)(2,1)} async-done(((bf16[512,1024]{1,0:T(8,128)(2,1)}), bf16[128,1024]{1,0:T(8,128)(2,1)}) %reduce-scatter.21.cloned.1.call-update) | async-done | bytes 262160 | tf_op jit(solution)/shard_map/reduce_scatter | solution.py:505
  462.6 26.3 %all-gather.31.cloned.1.call-done = bf16[512,1024]{1,0:T(8,128)(2,1)} async-done(((bf16[128,1024]{1,0:T(8,128)(2,1)}), bf16[512,1024]{1,0:T(8,128)(2,1)}) %all-gather.31.cloned.1.call-update) | async-done | bytes 1048592 | tf_op jit(solution)/shard_map/all_gather | solution.py:502
  492.2 22.7 %delta_backward.2 = (bf16[512,1664]{1,0:T(8,128)(2,1)}, f32[1,2,4,256]{3,2,1,0:T(4,128)}, f32[1,4,512]{2,1,0:T(4,128)}, f32[1,2,8,128]{3,2,1,0:T(8,128)}, f32[1,2,1,256]{3,2,1,0:T(1,128)}) custom-call(f32[512,1664]{1,0:T(8,128)} %fusion.96.qref.kref.vref.gref.pair_ref, f32[512,1664]{1,0:T(8,128)} %fusion.96.qref.kref.vref.gref.pair_ref, ...), custom_call_target="tpu_custom_call" | custom-call | tf_op jit(solution)/shard_map/delta_backward/pallas_call | solution.py:399
  523.3 22.9 %reduce-scatter.23.cloned.1.call-done = bf16[128,1024]{1,0:T(8,128)(2,1)} async-done(((bf16[512,1024]{1,0:T(8,128)(2,1)}), bf16[128,1024]{1,0:T(8,128)(2,1)}) %reduce-scatter.23.cloned.1.call-update) | async-done | bytes 262160 | tf_op jit(solution)/shard_map/reduce_scatter | solution.py:505
  547.4 26.9 %reduce-scatter.19.cloned.1.call-done = bf16[128,1024]{1,0:T(8,128)(2,1)} async-done(((bf16[512,1024]{1,0:T(8,128)(2,1)}), bf16[128,1024]{1,0:T(8,128)(2,1)}) %reduce-scatter.19.cloned.1.call-update) | async-done | bytes 262160 | tf_op jit(solution)/shard_map/reduce_scatter | solution.py:505
  576.8 26.5 %all-gather.33.cloned.1.call-done = bf16[512,1024]{1,0:T(8,128)(2,1)} async-done(((bf16[128,1024]{1,0:T(8,128)(2,1)}), bf16[512,1024]{1,0:T(8,128)(2,1)}) %all-gather.33.cloned.1.call-update) | async-done | bytes 1048592 | tf_op jit(solution)/shard_map/all_gather | solution.py:502
  613.1 26.7 %reduce-scatter.25.cloned.1.call-done = bf16[128,1024]{1,0:T(8,128)(2,1)} async-done(((bf16[512,1024]{1,0:T(8,128)(2,1)}), bf16[128,1024]{1,0:T(8,128)(2,1)}) %reduce-scatter.25.cloned.1.call-update) | async-done | bytes 262160 | tf_op jit(solution)/shard_map/reduce_scatter | solution.py:505
  657.1 12.5 %all-gather.35.cloned.1.call-done = bf16[512,1024]{1,0:T(8,128)(2,1)} async-done(((bf16[128,1024]{1,0:T(8,128)(2,1)}), bf16[512,1024]{1,0:T(8,128)(2,1)}) %all-gather.35.cloned.1.call-update) | async-done | bytes 1048592 | tf_op jit(solution)/shard_map/all_gather | solution.py:502
  673.0 22.7 %delta_backward.3 = (bf16[512,1664]{1,0:T(8,128)(2,1)}, f32[1,2,4,256]{3,2,1,0:T(4,128)}, f32[1,4,512]{2,1,0:T(4,128)}, f32[1,2,8,128]{3,2,1,0:T(8,128)}, f32[1,2,1,256]{3,2,1,0:T(1,128)}) custom-call(f32[512,1664]{1,0:T(8,128)} %fusion.95.qref.kref.vref.gref.pair_ref, f32[512,1664]{1,0:T(8,128)} %fusion.95.qref.kref.vref.gref.pair_ref, ...), custom_call_target="tpu_custom_call" | custom-call | tf_op jit(solution)/shard_map/delta_backward/pallas_call | solution.py:399
  728.0 55.0 %reduce-scatter.31.cloned.1.call-done = bf16[128,2176]{1,0:T(8,128)(2,1)} async-done(((bf16[1024,2176]{1,0:T(8,128)(2,1)}), bf16[128,2176]{1,0:T(8,128)(2,1)}) %reduce-scatter.31.cloned.1.call-update) | async-done | bytes 557072 | tf_op jit(solution)/shard_map/reduce_scatter | solution.py:549
  786.8 24.7 %all-reduce.12 = (f32[2,2,4,256]{3,2,1,0:T(4,128)}, f32[2,4,512]{2,1,0:T(4,128)}, f32[2,2,2]{2,1,0:T(2,128)}) all-reduce(f32[2,2,4,256]{3,2,1,0:T(4,128)S(1)} %pad_maximum_fusion.10, f32[2,4,512]{2,1,0:T(4,128)S(1)} %pad_maximum_fusion.11, f32[2,2,2]{2,1,0:T(2,128)S(1)} %pad_maximum_fusion.13), channel_id=1, replica_groups=mesh['dp'=8,'tensor'=4] {'dp'}, use_global_device_ids=true, to_apply=%region_20.21 | all-reduce | flops 8200 | bytes 65600 | tf_op jit(solution)/shard_map/psum | solution.py:570
  813.8 39.5 %all-reduce.11 = (f32[2,2,1024]{2,1,0:T(2,128)}, f32[2,256]{1,0:T(2,128)}) all-reduce(f32[2,2,1024]{2,1,0:T(2,128)S(1)} %pad_maximum_fusion.12, f32[2,256]{1,0:T(2,128)S(1)} %pad_maximum_fusion.14), channel_id=1, replica_groups=mesh['dp'=8,'tensor'=4] {'dp','tensor'}, use_global_device_ids=true, to_apply=%region_27.28 | all-reduce | flops 4608 | bytes 36864 | tf_op jit(solution)/shard_map/psum | solution.py:571
  855.4 13.7 %reduce-scatter.33.cloned.1.call-done = bf16[128,2304]{1,0:T(8,128)(2,1)} async-done(((bf16[1024,2304]{1,0:T(8,128)(2,1)}), bf16[128,2304]{1,0:T(8,128)(2,1)}) %reduce-scatter.33.cloned.1.call-update) | async-done | bytes 589840 | tf_op jit(solution)/shard_map/reduce_scatter | solution.py:537
  873.9 51.7 %reduce-scatter.29.cloned.1.call-done = bf16[128,2176]{1,0:T(8,128)(2,1)} async-done(((bf16[1024,2176]{1,0:T(8,128)(2,1)}), bf16[128,2176]{1,0:T(8,128)(2,1)}) %reduce-scatter.29.cloned.1.call-update) | async-done | bytes 557072 | tf_op jit(solution)/shard_map/reduce_scatter | solution.py:549
  (290 shorter events, 156.4 us)
Async XLA Ops:
  7.2 34.6 %all-gather.13.cloned.1.call-start = ((), (), s32[]{:S(2)}) async-start(), calls=%async_computation.12 | async-start | bytes 1310720 | tf_op jit(solution)/shard_map/all_gather | solution.py:502
  11.0 66.2 %all-gather.15.cloned.1.call-start = ((), (), s32[]{:S(2)}) async-start(), calls=%async_computation.13 | async-start | bytes 3833856 | tf_op jit(solution)/shard_map/all_gather | solution.py:486
  17.4 106.7 %all-gather.17.cloned.1.call-start = ((), (), s32[]{:S(2)}) async-start(), calls=%async_computation.14 | async-start | bytes 6488064 | tf_op jit(solution)/shard_map/all_gather | solution.py:486
  19.9 134.4 %reduce-scatter.13.cloned.1.call-start = ((), (), s32[]{:S(2)}) async-start(), calls=%async_computation.15 | async-start | bytes 1310720 | tf_op jit(solution)/shard_map/reduce_scatter | solution.py:505
  21.8 270.4 %copy-start = (f32[1,512,8]{2,1,0:T(8,128)}, f32[1,512,8]{2,1,0:T(8,128)S(1)}, u32[]{:S(2)}) copy-start(f32[1,512,8]{2,1,0:T(8,128)S(1)} %copy.69.col_ref) | copy-start | bytes 49156
  21.8 270.3 %copy-start.9 = (f32[1,8,512]{2,1,0:T(8,128)}, f32[1,8,512]{2,1,0:T(8,128)S(1)}, u32[]{:S(2)}) copy-start(f32[1,8,512]{2,1,0:T(8,128)S(1)} %stack.191.row_ref) | copy-start | bytes 49156
  21.9 270.3 %copy-start.16 = (f32[2,2]{1,0:T(2,128)}, f32[2,2]{1,0:T(2,128)S(1)}, u32[]{:S(2)}) copy-start(f32[2,2]{1,0:T(2,128)S(1)} %get-tuple-element.169.head_table) | copy-start | bytes 52
  21.9 270.2 %copy-start.17 = (f32[1,256]{1,0:T(1,128)}, f32[1,256]{1,0:T(1,128)S(1)}, u32[]{:S(2)}) copy-start(f32[1,256]{1,0:T(1,128)S(1)} %get-tuple-element.167.gain) | copy-start | bytes 3076
  22.0 270.2 %copy-start.12 = (f32[2,4,256]{2,1,0:T(4,128)}, f32[2,4,256]{2,1,0:T(4,128)S(1)}, u32[]{:S(2)}) copy-start(f32[2,4,256]{2,1,0:T(4,128)S(1)} %get-tuple-element.161.tap_qk) | copy-start | bytes 24580
  22.0 270.2 %copy-start.13 = (f32[4,512]{1,0:T(4,128)}, f32[4,512]{1,0:T(4,128)S(1)}, u32[]{:S(2)}) copy-start(f32[4,512]{1,0:T(4,128)S(1)} %get-tuple-element.159.tap_v) | copy-start | bytes 24580
  127.0 57.0 %all-gather.19.cloned.1.call-start = ((), (), s32[]{:S(2)}) async-start(), calls=%async_computation.16 | async-start | bytes 1310720 | tf_op jit(solution)/shard_map/all_gather | solution.py:502
  157.2 64.1 %reduce-scatter.15.cloned.1.call-start = ((), (), s32[]{:S(2)}) async-start(), calls=%async_computation.17 | async-start | bytes 1310720 | tf_op jit(solution)/shard_map/reduce_scatter | solution.py:505
  194.5 61.4 %all-gather.23.cloned.1.call-start = ((), (), s32[]{:S(2)}) async-start(), calls=%async_computation.19 | async-start | bytes 3833856 | tf_op jit(solution)/shard_map/all_gather | solution.py:486
  195.4 90.6 %all-gather.21.cloned.1.call-start = ((), (), s32[]{:S(2)}) async-start(), calls=%async_computation.18 | async-start | bytes 1310720 | tf_op jit(solution)/shard_map/all_gather | solution.py:502
  223.3 109.0 %all-gather.25.cloned.1.call-start = ((), (), s32[]{:S(2)}) async-start(), calls=%async_computation.20 | async-start | bytes 6488064 | tf_op jit(solution)/shard_map/all_gather | solution.py:486
  224.3 138.3 %reduce-scatter.17.cloned.1.call-start = ((), (), s32[]{:S(2)}) async-start(), calls=%async_computation.21 | async-start | bytes 1310720 | tf_op jit(solution)/shard_map/reduce_scatter | solution.py:505
  335.4 56.9 %all-gather.27.cloned.1.call-start = ((), (), s32[]{:S(2)}) async-start(), calls=%async_computation.22 | async-start | bytes 1310720 | tf_op jit(solution)/shard_map/all_gather | solution.py:502
  365.6 55.7 %all-gather.29.cloned.1.call-start = ((), (), s32[]{:S(2)}) async-start(), calls=%async_computation.24 | async-start | bytes 1310720 | tf_op jit(solution)/shard_map/all_gather | solution.py:502
  366.1 93.0 %reduce-scatter.21.cloned.1.call-start = ((), (), s32[]{:S(2)}) async-start(), calls=%async_computation.25 | async-start | bytes 1310720 | tf_op jit(solution)/shard_map/reduce_scatter | solution.py:505
  432.3 56.6 %all-gather.31.cloned.1.call-start = ((), (), s32[]{:S(2)}) async-start(), calls=%async_computation.26 | async-start | bytes 1310720 | tf_op jit(solution)/shard_map/all_gather | solution.py:502
  462.2 84.1 %reduce-scatter.23.cloned.1.call-start = ((), (), s32[]{:S(2)}) async-start(), calls=%async_computation.27 | async-start | bytes 1310720 | tf_op jit(solution)/shard_map/reduce_scatter | solution.py:505
  519.4 54.9 %reduce-scatter.19.cloned.1.call-start = ((), (), s32[]{:S(2)}) async-start(), calls=%async_computation.23 | async-start | bytes 1310720 | tf_op jit(solution)/shard_map/reduce_scatter | solution.py:505
  523.2 80.1 %all-gather.33.cloned.1.call-start = ((), (), s32[]{:S(2)}) async-start(), calls=%async_computation.28 | async-start | bytes 1310720 | tf_op jit(solution)/shard_map/all_gather | solution.py:502
  576.6 63.2 %reduce-scatter.25.cloned.1.call-start = ((), (), s32[]{:S(2)}) async-start(), calls=%async_computation.29 | async-start | bytes 1310720 | tf_op jit(solution)/shard_map/reduce_scatter | solution.py:505
  613.0 56.6 %all-gather.35.cloned.1.call-start = ((), (), s32[]{:S(2)}) async-start(), calls=%async_computation.30 | async-start | bytes 1310720 | tf_op jit(solution)/shard_map/all_gather | solution.py:502
  642.9 83.9 %reduce-scatter.35.cloned.1.call-start = ((), (), s32[]{:S(2)}) async-start(), calls=%async_computation.35 | async-start | bytes 5308416 | tf_op jit(solution)/shard_map/reduce_scatter | solution.py:537
  650.1 132.9 %reduce-scatter.31.cloned.1.call-start = ((), (), s32[]{:S(2)}) async-start(), calls=%async_computation.33 | async-start | bytes 5013504 | tf_op jit(solution)/shard_map/reduce_scatter | solution.py:549
  656.9 155.7 %reduce-scatter.27.cloned.1.call-start = ((), (), s32[]{:S(2)}) async-start(), calls=%async_computation.31 | async-start | bytes 1310720 | tf_op jit(solution)/shard_map/reduce_scatter | solution.py:505
  700.4 168.7 %reduce-scatter.33.cloned.1.call-start = ((), (), s32[]{:S(2)}) async-start(), calls=%async_computation.34 | async-start | bytes 5308416 | tf_op jit(solution)/shard_map/reduce_scatter | solution.py:537
  711.9 213.7 %reduce-scatter.29.cloned.1.call-start = ((), (), s32[]{:S(2)}) async-start(), calls=%async_computation.32 | async-start | bytes 5013504 | tf_op jit(solution)/shard_map/reduce_scatter | solution.py:549
  723.0 63.8 %copy-start.36 = (f32[1,4,512]{2,1,0:T(4,128)S(1)}, f32[1,4,512]{2,1,0:T(4,128)}, u32[]{:S(2)}) copy-start(f32[1,4,512]{2,1,0:T(4,128)} %get-tuple-element.51) | copy-start | bytes 24580
  723.0 130.3 %copy-start.22 = (bf16[128,1024]{1,0:T(8,128)(2,1)S(1)}, bf16[128,1024]{1,0:T(8,128)(2,1)}, u32[]{:S(2)}) copy-start(bf16[128,1024]{1,0:T(8,128)(2,1)} %reduce-scatter.25.cloned.1.call-done) | copy-start | bytes 786436
  (48 other events, 823.6 us)
Sparse Core Ops, SparseCore 0:
  11.1 30.6 all-gather.12
  44.3 32.9 all-gather.14
  79.7 44.3 all-gather.16
  127.1 27.1 reduce-scatter.12
  157.4 26.5 all-gather.18
  194.7 26.6 reduce-scatter.14
  223.8 32.0 all-gather.22
  258.0 27.9 all-gather.20
  288.5 43.8 all-gather.24
  335.5 27.1 reduce-scatter.16
  365.7 26.5 all-gather.26
  393.8 27.4 all-gather.28
  432.4 26.6 reduce-scatter.20
  462.3 26.5 all-gather.30
  519.6 26.6 reduce-scatter.22
  548.5 25.7 reduce-scatter.18
  576.7 26.5 all-gather.32
  613.1 26.6 reduce-scatter.24
  643.0 26.5 all-gather.34
  673.3 53.4 reduce-scatter.34
  730.3 52.7 reduce-scatter.30
  785.4 27.1 reduce-scatter.26
  816.0 53.0 reduce-scatter.32
  872.8 52.6 reduce-scatter.28

commit v2 on v1

--- a/solution.py
+++ b/solution.py
@@ -425,34 +425,425 @@
     )(proj, proj, proj, proj, proj, taps_qk, taps_v, head_table, gain, cols, rows, *saved, dmix)
 
 
+MESH = pl.DeviceIdType.MESH
+VMEM_LIMIT = 58 * 2**20
+HALVES = 2
+
+
+class Line:
+    def __init__(self, send_sem, recv_sem):
+        self.send_sem, self.recv_sem = send_sem, recv_sem
+        self.me = lax.axis_index("tensor")
+
+    def greet(self):
+        barrier = pltpu.get_barrier_semaphore()
+        for m in range(4):
+            @pl.when(self.me == m)
+            def _():
+                others = [t for t in range(4) if t != m and {t, m} != {0, 3}]
+                for t in others:
+                    pl.semaphore_signal(barrier, inc=1, device_id={"tensor": t}, device_id_type=MESH)
+                pl.semaphore_wait(barrier, len(others))
+
+    def copy(self, phase, source, target, to, send_at, recv_at):
+        return pltpu.make_async_remote_copy(
+            src_ref=source, dst_ref=target, send_sem=self.send_sem.at[phase, send_at],
+            recv_sem=self.recv_sem.at[phase, recv_at], device_id={"tensor": to}, device_id_type=MESH,
+        )
+
+    def gather_start(self, phase, blocks):
+        for m in range(4):
+            @pl.when(self.me == m)
+            def _():
+                for t in range(4):
+                    if t != m and {t, m} != {0, 3}:
+                        self.copy(phase, blocks[m], blocks[m], t, t, m).start()
+
+    def gather_finish(self, phase, blocks):
+        for m in range(4):
+            @pl.when(self.me == m)
+            def _():
+                if m in (1, 2):
+                    far, to = (3, 0) if m == 1 else (0, 3)
+                    self.copy(phase, blocks[far], blocks[far], to, m, far).wait_recv()
+                    self.copy(phase, blocks[far], blocks[far], to, m, far).start()
+                for b in range(4):
+                    if b != m and not (m in (1, 2) and b == (3 if m == 1 else 0)):
+                        self.copy(phase, blocks[b], blocks[b], b, b, b).wait_recv()
+
+    def gather_drain(self, phase, blocks):
+        for m in range(4):
+            @pl.when(self.me == m)
+            def _():
+                for t in range(4):
+                    if t != m and {t, m} != {0, 3}:
+                        self.copy(phase, blocks[m], blocks[m], t, t, m).wait_send()
+                if m in (1, 2):
+                    far, to = (3, 0) if m == 1 else (0, 3)
+                    self.copy(phase, blocks[far], blocks[far], to, m, far).wait_send()
+
+    def scatter_start(self, phase, parts, slots):
+        for m in range(4):
+            @pl.when(self.me == m)
+            def _():
+                if m in (0, 3):
+                    through = 1 if m == 0 else 2
+                    self.copy(phase, parts[3 - m], slots[4], through, 3 - m, 4).start()
+                for t in range(4):
+                    if t != m and {t, m} != {0, 3}:
+                        if not (m in (1, 2) and t == (3 if m == 1 else 0)):
+                            self.copy(phase, parts[t], slots[m], t, t, m).start()
+
+    def scatter_relay(self, phase, parts, slots):
+        for m in (1, 2):
+            @pl.when(self.me == m)
+            def _():
+                t = 3 if m == 1 else 0
+                self.copy(phase, parts[t], slots[4], t, t, 4).wait_recv()
+                parts[t][...] = (parts[t][...].astype(F32) + slots[4][...].astype(F32)).astype(BF16)
+                self.copy(phase, parts[t], slots[m], t, t, m).start()
+
+    def scatter_wait(self, phase, parts, slots):
+        for m in range(4):
+            @pl.when(self.me == m)
+            def _():
+                for s in range(4):
+                    if s != m and {s, m} != {0, 3}:
+                        self.copy(phase, parts[s], slots[s], s, s, s).wait_recv()
+
+    def scatter_sum(self, total, parts, slots):
+        for m in range(4):
+            @pl.when(self.me == m)
+            def _():
+                value = parts[m][...].astype(F32)
+                for s in range(4):
+                    if s != m and {s, m} != {0, 3}:
+                        value = value + slots[s][...].astype(F32)
+                total[...] = value
+
+    def scatter_drain(self, phase, parts, slots):
+        for m in range(4):
+            @pl.when(self.me == m)
+            def _():
+                for t in range(4):
+                    if t != m:
+                        self.copy(phase, parts[t], slots[m], t, t, m).wait_send()
+
+
+def half_of(ref, h):
+    value = ref[:, h]
+    return value.reshape(value.shape[0] * value.shape[1], value.shape[2])
+
+
+def blocks_of(ref, h):
+    return [ref.at[b, h] for b in range(4)]
+
+
+def parts_of(part, slots, k, h):
+    return [part.at[k, h, t] for t in range(4)], [slots.at[k, h, s] for s in range(5)]
+
+
+def for_tiles(size, tile, step):
+    def run(i, carry):
+        step(pl.multiple_of(i * tile, tile))
+        return carry
+
+    lax.fori_loop(0, size // tile, run, 0)
+
+
+def partial_sums(left, weight, part, k, h):
+    def step(n):
+        value = lax.dot_general(left, weight[pl.ds(n, 256), :], NT, preferred_element_type=F32)
+        part[k, h, :, :, pl.ds(n, 256)] = value.astype(BF16).reshape(4, left.shape[0] // 4, 256)
+
+    for_tiles(weight.shape[0], 256, step)
+
+
+def row_grads(left, right, out, column):
+    rows = left.shape[0] * left.shape[1] * left.shape[2]
+    width = right.shape[3]
+
+    def piece(m):
+        m = pl.multiple_of(m * 256, 256)
+        turned = jnp.transpose(left[:, :, :, pl.ds(m, 256)].reshape(rows, 256))
+        for n in range(0, width, 512):
+            size = min(512, width - n)
+            tile = right[:, :, :, n : n + size].reshape(rows, size)
+            value = lax.dot_general(turned, tile, NN, preferred_element_type=F32)
+            out[pl.ds(m, 256), column + n : column + n + size] = value.astype(BF16)
+
+    return piece
+
+
+def run_pieces(pieces, first, last):
+    def run(m, carry):
+        for piece in pieces:
+            piece(m)
+        return carry
+
+    lax.fori_loop(first, last, run, 0)
+
+
+def rms(value, gain):
+    return value * lax.rsqrt(jnp.mean(value * value, axis=1, keepdims=True) + EPS) * gain
+
+
+def rms_back(value, gain, grad):
+    scale = lax.rsqrt(jnp.mean(value * value, axis=1, keepdims=True) + EPS)
+    scaled = gain * grad
+    back = scale * scaled - value * (scale * scale * scale) * jnp.mean(value * scaled, axis=1, keepdims=True)
+    return back, jnp.sum(value * scale * grad, axis=0, keepdims=True)
+
+
+def start_kernel(rows, cot, gain, normed, cot_all, send_sem, recv_sem):
+    line = Line(send_sem, recv_sem)
+    for h in range(HALVES):
+        normed[line.me, h] = rms(rows[h].astype(F32), gain[...]).astype(BF16)
+        cot_all[line.me, h] = cot[h]
+    line.greet()
+    for k, ref in ((0, normed), (2, cot_all)):
+        for h in range(HALVES):
+            line.gather_start(k + h, blocks_of(ref, h))
+    for k, ref in ((0, normed), (2, cot_all)):
+        for h in range(HALVES):
+            line.gather_finish(k + h, blocks_of(ref, h))
+    for k, ref in ((0, normed), (2, cot_all)):
+        for h in range(HALVES):
+            line.gather_drain(k + h, blocks_of(ref, h))
+
+
+def ffn_forward_kernel(
+    last, mixer, w_out, w_up, w_down, rows, gain, gain_next, middle, normed, pre, hidden, out_rows, *rest
+):
+    if last:
+        part, slots, total, send_sem, recv_sem = rest
+    else:
+        normed_next, part, slots, total, send_sem, recv_sem = rest
+    line = Line(send_sem, recv_sem)
+    wide = w_down.shape[1]
+    block = rows.shape[1]
+    line.greet()
+    for h in range(HALVES):
+        partial_sums(half_of(mixer, h), w_out, part, 0, h)
+        line.scatter_start(h, *parts_of(part, slots, 0, h))
+    for h in range(HALVES):
+        line.scatter_relay(h, *parts_of(part, slots, 0, h))
+    for h in range(HALVES):
+        both = parts_of(part, slots, 0, h)
+        line.scatter_wait(h, *both)
+        line.scatter_sum(total, *both)
+        value = rows[h].astype(F32) + total[...]
+        middle[h] = value
+        normed[line.me, h] = rms(value, gain[...]).astype(BF16)
+        line.gather_start(2 + h, blocks_of(normed, h))
+    for h in range(HALVES):
+        line.gather_finish(2 + h, blocks_of(normed, h))
+        left = half_of(normed, h)
+
+        def step(n):
+            gate = jnp.dot(left, w_up[:, pl.ds(n, 256)], preferred_element_type=F32)
+            up = jnp.dot(left, w_up[:, pl.ds(n + wide, 256)], preferred_element_type=F32)
+            pre[:, h, :, pl.ds(n, 256)] = gate.reshape(4, block, 256)
+            pre[:, h, :, pl.ds(n + wide, 256)] = up.reshape(4, block, 256)
+            value = gate * lax.logistic(gate) * up
+            hidden[:, h, :, pl.ds(n, 256)] = value.astype(BF16).reshape(4, block, 256)
+
+        for_tiles(wide, 256, step)
+        partial_sums(half_of(hidden, h), w_down, part, 1, h)
+        line.scatter_start(4 + h, *parts_of(part, slots, 1, h))
+    for h in range(HALVES):
+        line.scatter_relay(4 + h, *parts_of(part, slots, 1, h))
+    for h in range(HALVES):
+        both = parts_of(part, slots, 1, h)
+        line.scatter_wait(4 + h, *both)
+        line.scatter_sum(total, *both)
+        value = middle[h] + total[...]
+        out_rows[h] = value
+        if not last:
+            normed_next[line.me, h] = rms(value, gain_next[...]).astype(BF16)
+            line.gather_start(6 + h, blocks_of(normed_next, h))
+    if not last:
+        for h in range(HALVES):
+            line.gather_finish(6 + h, blocks_of(normed_next, h))
+    for h in range(HALVES):
+        line.scatter_drain(h, *parts_of(part, slots, 0, h))
+        line.gather_drain(2 + h, blocks_of(normed, h))
+        line.scatter_drain(4 + h, *parts_of(part, slots, 1, h))
+        if not last:
+            line.gather_drain(6 + h, blocks_of(normed_next, h))
+
+
+def ffn_backward_kernel(
+    cot, hidden, pre, normed, middle, grad, gain, w_down, w_up, w_out,
+    d_mixer, grads, mixer_cot, grad_out, d_gain, d_pre, part, slots, total, send_sem, recv_sem,
+):
+    line = Line(send_sem, recv_sem)
+    wide = w_down.shape[1]
+    block = middle.shape[1]
+    line.greet()
+    for h in range(HALVES):
+        left = half_of(cot, h)
+
+        def step(n):
+            d_hidden = jnp.dot(left, w_down[:, pl.ds(n, 256)], preferred_element_type=F32)
+            gate = pre[:, h, :, pl.ds(n, 256)].reshape(4 * block, 256)
+            up = pre[:, h, :, pl.ds(n + wide, 256)].reshape(4 * block, 256)
+            sig = lax.logistic(gate)
+            d_gate = d_hidden * up * sig * (1.0 + gate * (1.0 - sig))
+            d_up = d_hidden * gate * sig
+            d_pre[:, h, :, pl.ds(n, 256)] = d_gate.astype(BF16).reshape(4, block, 256)
+            d_pre[:, h, :, pl.ds(n + wide, 256)] = d_up.astype(BF16).reshape(4, block, 256)
+
+        for_tiles(wide, 256, step)
+        partial_sums(half_of(d_pre, h), w_up, part, 0, h)
+        line.scatter_start(h, *parts_of(part, slots, 0, h))
+    pieces = [row_grads(cot, hidden, grads, 0), row_grads(normed, d_pre, grads, wide)]
+    run_pieces(pieces, 0, 2)
+    for h in range(HALVES):
+        line.scatter_relay(h, *parts_of(part, slots, 0, h))
+    run_pieces(pieces, 2, 4)
+    d_gain[...] = jnp.zeros_like(d_gain)
+    for h in range(HALVES):
+        both = parts_of(part, slots, 0, h)
+        line.scatter_wait(h, *both)
+        line.scatter_sum(total, *both)
+        back, gain_part = rms_back(middle[h], gain[...], total[...])
+        d_gain[...] += gain_part
+        value = grad[h].astype(F32) + back
+        grad_out[h] = value
+        mixer_cot[line.me, h] = value.astype(BF16)
+        line.gather_start(2 + h, blocks_of(mixer_cot, h))
+    for h in range(HALVES):
+        line.gather_finish(2 + h, blocks_of(mixer_cot, h))
+        left = half_of(mixer_cot, h)
+        for n in range(0, w_out.shape[1], 256):
+            value = jnp.dot(left, w_out[:, n : n + 256], preferred_element_type=F32)
+            d_mixer[:, h, :, n : n + 256] = value.reshape(4, block, 256)
+    for h in range(HALVES):
+        line.scatter_drain(h, *parts_of(part, slots, 0, h))
+        line.gather_drain(2 + h, blocks_of(mixer_cot, h))
+
+
+def mixer_backward_kernel(last, d_proj, w_in, normed, mixer, mixer_cot, rows, grad, gain, grad_out, d_gain, *rest):
+    if last:
+        part, slots, total, send_sem, recv_sem = rest
+    else:
+        grads, cot, part, slots, total, send_sem, recv_sem = rest
+    line = Line(send_sem, recv_sem)
+    line.greet()
+    for h in range(HALVES):
+        partial_sums(half_of(d_proj, h), w_in, part, 0, h)
+        line.scatter_start(h, *parts_of(part, slots, 0, h))
+    if not last:
+        width = mixer.shape[3]
+        pieces = [row_grads(mixer_cot, mixer, grads, 0), row_grads(normed, d_proj, grads, width)]
+        run_pieces(pieces, 0, 2)
+    for h in range(HALVES):
+        line.scatter_relay(h, *parts_of(part, slots, 0, h))
+    if not last:
+        run_pieces(pieces, 2, 4)
+    d_gain[...] = jnp.zeros_like(d_gain)
+    for h in range(HALVES):
+        both = parts_of(part, slots, 0, h)
+        line.scatter_wait(h, *both)
+        line.scatter_sum(total, *both)
+        back, gain_part = rms_back(rows[h].astype(F32), gain[...], total[...])
+        d_gain[...] += gain_part
+        value = grad[h] + back
+        grad_out[h] = value
+        if not last:
+            cot[line.me, h] = value.astype(BF16)
+            line.gather_start(2 + h, blocks_of(cot, h))
+    if not last:
+        for h in range(HALVES):
+            line.gather_finish(2 + h, blocks_of(cot, h))
+    for h in range(HALVES):
+        line.scatter_drain(h, *parts_of(part, slots, 0, h))
+        if not last:
+            line.gather_drain(2 + h, blocks_of(cot, h))
+
+
+def line_call(kernel, operands, outs, scratch, phases, number, name):
+    return pl.pallas_call(
+        kernel,
+        in_specs=[pl.BlockSpec(memory_space=pltpu.VMEM)] * len(operands),
+        out_specs=[pl.BlockSpec(memory_space=pltpu.VMEM)] * len(outs),
+        out_shape=[jax.ShapeDtypeStruct(*out) for out in outs],
+        scratch_shapes=[pltpu.VMEM(*item) for item in scratch]
+        + [pltpu.SemaphoreType.DMA((phases, 4)), pltpu.SemaphoreType.DMA((phases, 5))],
+        compiler_params=pltpu.CompilerParams(
+            collective_id=number, has_side_effects=True, vmem_limit_bytes=VMEM_LIMIT
+        ),
+        name=name,
+    )(*operands)
+
+
+def exchange_scratch(sums, block, width):
+    return [
+        ((sums, HALVES, 4, block, width), BF16),
+        ((sums, HALVES, 5, block, width), BF16),
+        ((block, width), F32),
+    ]
+
+
+def start_call(rows, cot, gain):
+    _, block, width = rows.shape
+    whole = ((4, HALVES, block, width), BF16)
+    return line_call(start_kernel, (rows, cot, gain), [whole, whole], [], 4, 1, "start")
+
+
+def ffn_forward_call(mixer, w_out, w_up, w_down, rows, gain, gain_next, layer, last):
+    _, block, width = rows.shape
+    wide = w_down.shape[1]
+    own, whole = ((HALVES, block, width), F32), ((4, HALVES, block, width), BF16)
+    outs = [own, whole, ((4, HALVES, block, 2 * wide), F32), ((4, HALVES, block, wide), BF16), own]
+    if not last:
+        outs.append(whole)
+    return line_call(
+        functools.partial(ffn_forward_kernel, last),
+        (mixer, w_out, w_up, w_down, rows, gain, gain_next), outs,
+        exchange_scratch(2, block, width), 8, 2 + layer, "ffn_forward",
+    )
+
+
+def ffn_backward_call(cot, hidden, pre, normed, middle, grad, gain, w_down, w_up, w_out, layer):
+    _, block, width = middle.shape
+    wide = w_down.shape[1]
+    whole = ((4, HALVES, block, width), BF16)
+    outs = [
+        ((4, HALVES, block, w_out.shape[1]), F32), ((width, 3 * wide), BF16), whole,
+        ((HALVES, block, width), F32), ((1, width), F32),
+    ]
+    scratch = [((4, HALVES, block, 2 * wide), BF16)] + exchange_scratch(1, block, width)
+    return line_call(
+        ffn_backward_kernel, (cot, hidden, pre, normed, middle, grad, gain, w_down, w_up, w_out), outs,
+        scratch, 4, 4 + layer, "ffn_backward",
+    )
+
+
+def mixer_backward_call(d_proj, w_in, normed, mixer, mixer_cot, rows, grad, gain, layer, last):
+    _, block, width = rows.shape
+    outs = [((HALVES, block, width), F32), ((1, width), F32)]
+    if not last:
+        outs += [((width, mixer.shape[3] + w_in.shape[1]), BF16), ((4, HALVES, block, width), BF16)]
+    return line_call(
+        functools.partial(mixer_backward_kernel, last),
+        (d_proj, w_in, normed, mixer, mixer_cot, rows, grad, gain), outs,
+        exchange_scratch(1, block, width), 4, 6 + layer, "mixer_backward",
+    )
+
+
 LAYERS = 2
 CHUNK = 128
 REFINE = 1
 
 
-def rms_gain(matrix, gain_vector):
-    scaling = lax.rsqrt(jnp.mean(matrix * matrix, axis=-1, keepdims=True) + EPS)
-    return matrix * scaling * gain_vector
-
-
-def times_transposed(left, right):
-    return lax.dot_general(left, right, NT, preferred_element_type=F32)
-
-
 def over_rows(left, right):
     return lax.dot_general(left, right, TN, preferred_element_type=F32)
 
 
-def times(left, right):
-    return jnp.dot(left, right, preferred_element_type=F32)
-
-
 def padded(matrix, width):
     return jnp.pad(matrix, ((0, 0), (0, width - matrix.shape[1])))
-
-
-def up_to(size, unit):
-    return -(-size // unit) * unit
 
 
 def body(
@@ -478,12 +869,17 @@
     heads = head_params.shape[2]
     qk_width, v_width, pair_width = query_weight.shape[2], value_weight.shape[2], decay_weight.shape[2]
     hidden_width = swiglu_gate.shape[2]
-    hidden_pad = up_to(hidden_width, 128)
-    in_width = 2 * qk_width + 2 * v_width + 128
+    hidden_pad = -(-hidden_width // 256) * 256
+    local_rows, width = tokens.shape
+    block = local_rows // HALVES
+    total_rows = 4 * local_rows
     tables = segment_tables(segment_ids, CHUNK)
 
     def gathered(matrix):
         return lax.all_gather(matrix, "dp", axis=0, tiled=True)
+
+    def reduced(matrix):
+        return lax.psum_scatter(matrix, "dp", scatter_dimension=0, tiled=True)
 
     def layer_weights(l):
         low = lambda m: m[l].astype(BF16)
@@ -498,70 +894,75 @@
             first, second[:, :v_width], second[:, v_width : v_width + 2 * hidden_pad], second[:, v_width + 2 * hidden_pad :]
         )
 
-    def spread(matrix):
-        return lax.all_gather(matrix.astype(BF16), "tensor", axis=0, tiled=True)
-
-    def collect(term):
-        return lax.psum_scatter(term.astype(BF16), "tensor", scatter_dimension=0, tiled=True).astype(F32)
-
-    residual = tokens.astype(F32)
+    def split_rows(matrix):
+        return matrix.reshape(HALVES, block, matrix.shape[1])
+
+    def split_all(matrix):
+        return matrix.reshape(4, HALVES, block, matrix.shape[1])
+
+    def merged(array):
+        return array.reshape(total_rows, array.shape[3])
+
+    def gain_of(l, i):
+        return norm_gains[l, i][None]
+
+    weights = [layer_weights(l) for l in range(LAYERS)]
+    rows = split_rows(tokens)
+    cot_rows = split_rows(cotangent)
+    normed, cot = start_call(rows, cot_rows, gain_of(0, 0))
     kept = []
     for l in range(LAYERS):
-        w_in, w_out, w_up, w_down = layer_weights(l)
-        first_norm, first_back = jax.vjp(rms_gain, residual, norm_gains[l, 0])
-        normed = spread(first_norm)
-        proj = times(normed, w_in)
+        w_in, w_out, w_up, w_down = weights[l]
+        last = l == LAYERS - 1
+        proj = jnp.dot(merged(normed), w_in, preferred_element_type=F32)
         small = (conv_query_key[l], conv_value[l], head_params[l], out_gain[l][None])
         mixer, *saved = delta_forward(proj, *small, tables, seqs, heads, CHUNK, REFINE)
-        middle = residual + collect(times_transposed(mixer, w_out))
-        second_norm, second_back = jax.vjp(rms_gain, middle, norm_gains[l, 1])
-        normed_ffn = spread(second_norm)
-        pre = times(normed_ffn, w_up)
-        hidden = (jax.nn.silu(pre[:, :hidden_pad]) * pre[:, hidden_pad:]).astype(BF16)
-        residual = middle + collect(times_transposed(hidden, w_down))
-        kept.append((w_in, w_out, w_up, w_down, first_back, normed, proj, small, mixer, saved, second_back, normed_ffn, pre, hidden))
-    grad = cotangent.astype(F32)
+        mixer = split_all(mixer)
+        following = gain_of(min(l + 1, LAYERS - 1), 0)
+        middle, normed_ffn, pre, hidden, out_rows, *following = ffn_forward_call(
+            mixer, w_out, w_up, w_down, rows, gain_of(l, 1), following, l, last
+        )
+        kept.append((rows, normed, proj, small, mixer, saved, middle, normed_ffn, pre, hidden))
+        rows = out_rows
+        if not last:
+            normed = following[0]
+    output = rows.reshape(local_rows, width)
+    grad = cot_rows
     ffn_grads, mixer_grads, tap_grads, norm_grads, gain_grads = ([None] * LAYERS for _ in range(5))
     for l in reversed(range(LAYERS)):
-        w_in, w_out, w_up, w_down, first_back, normed, proj, small, mixer, saved, second_back, normed_ffn, pre, hidden = kept[l]
-        ffn_cot = spread(grad)
-        down_grad = over_rows(ffn_cot, hidden)
-        d_hidden = times(ffn_cot, w_down)
-        gate_pre, up_pre = pre[:, :hidden_pad], pre[:, hidden_pad:]
-        sig = jax.nn.sigmoid(gate_pre)
-        d_pre = jnp.concatenate(
-            [d_hidden * up_pre * sig * (1.0 + gate_pre * (1.0 - sig)), d_hidden * gate_pre * sig], axis=1
-        ).astype(BF16)
-        d_middle, second_gain = second_back(collect(times_transposed(d_pre, w_up)))
-        up_grad = over_rows(normed_ffn, d_pre)
-        ffn_grads[l] = lax.psum_scatter(
-            jnp.concatenate([down_grad, up_grad], axis=1).astype(BF16), "dp", scatter_dimension=0, tiled=True
+        w_in, w_out, w_up, w_down = weights[l]
+        rows, normed, proj, small, mixer, saved, middle, normed_ffn, pre, hidden = kept[l]
+        last = l == 0
+        d_mixer, ffn_grad, mixer_cot, grad, second_gain = ffn_backward_call(
+            cot, hidden, pre, normed_ffn, middle, grad, gain_of(l, 1), w_down, w_up, w_out, l
         )
-        grad = grad + d_middle
-        mixer_cot = spread(grad)
-        d_mixer = times(mixer_cot, w_out)
+        ffn_grads[l] = reduced(ffn_grad)
         d_proj, d_qk, d_v, d_head, d_gain = delta_backward(
-            proj, *small, tables, saved, d_mixer, seqs, heads, CHUNK
+            proj, *small, tables, saved, merged(d_mixer), seqs, heads, CHUNK
         )
-        d_input, first_gain = first_back(collect(times_transposed(d_proj, w_in)))
-        out_grad = over_rows(mixer_cot, mixer)
-        in_grad = over_rows(normed, d_proj)
-        mixer_grads[l] = lax.psum_scatter(
-            jnp.concatenate([out_grad, in_grad], axis=1).astype(BF16), "dp", scatter_dimension=0, tiled=True
+        if last:
+            mixer_grad = jnp.concatenate(
+                [over_rows(merged(mixer_cot), merged(mixer)), over_rows(merged(normed), d_proj)], axis=1
+            ).astype(BF16)
+            mixer_grads[l] = reduced(mixer_grad)
+        grad, first_gain, *others = mixer_backward_call(
+            split_all(d_proj), w_in, normed, mixer, mixer_cot, rows, grad, gain_of(l, 0), l, last
         )
-        grad = grad + d_input
+        if not last:
+            mixer_grads[l] = reduced(others[0])
+            cot = others[1]
         tap_grads[l] = (d_qk.sum(0), d_v.sum(0), d_head.sum(0)[:, :2, 0].T)
-        norm_grads[l] = jnp.stack([first_gain, second_gain])
+        norm_grads[l] = jnp.concatenate([first_gain, second_gain], axis=0)
         gain_grads[l] = d_gain.sum((0, 1, 2))
 
-    def columns(parts, start, width):
-        return jnp.stack([part[:, start : start + width] for part in parts]).astype(F32)
-
-    at = v_width
+    def columns(parts, start, size):
+        return jnp.stack([part[:, start : start + size] for part in parts]).astype(F32)
+
+    start = v_width
     in_grads = []
-    for width in (qk_width, qk_width, v_width, v_width, pair_width):
-        in_grads.append(columns(mixer_grads, at, width))
-        at += width
+    for size in (qk_width, qk_width, v_width, v_width, pair_width):
+        in_grads.append(columns(mixer_grads, start, size))
+        start += size
     out_grad = columns(mixer_grads, 0, v_width)
     down_grad = columns(ffn_grads, 0, hidden_width)
     gate_grad = columns(ffn_grads, hidden_pad, hidden_width)
@@ -569,7 +970,9 @@
     taps = tuple(jnp.stack([tap_grads[l][i] for l in range(LAYERS)]) for i in range(3))
     taps = lax.psum(taps, "dp")
     norms = lax.psum((jnp.stack(norm_grads), jnp.stack(gain_grads)), ("dp", "tensor"))
-    return (residual, grad, *in_grads, out_grad, gate_grad, up_grad, down_grad, *taps, *norms)
+    return (
+        output, grad.reshape(local_rows, width), *in_grads, out_grad, gate_grad, up_grad, down_grad, *taps, *norms
+    )
 
 
 def solution(mesh):

time: 950 us -> 659 us (0.69)
  waiting for transfers between devices: 616 us -> 76 us
  Pallas kernels: 70.1 us -> 420 us
  matrix products: 91.1 us -> 15.1 us
  other arithmetic: 44 us -> 14.7 us
    pallas_call x0 -> x7, Pallas kernels: none -> 350 us  [line_call(): pl.pallas_call(kernel, in_specs=[pl.BlockSpec(memory_space=pltpu.VMEM)] *...]
    reduce_scatter x12 -> x4, waiting for transfers between devices: 308 us -> 65.5 us  [reduced(): return lax.psum_scatter(matrix, 'dp', scatter_dimension=0, tiled=True)]
    all_gather x8 -> x0, waiting for transfers between devices: 191 us -> none  [spread(): return lax.all_gather(matrix.astype(BF16), 'tensor', axis=0, tiled=True)]
    all_gather x4, waiting for transfers between devices: 115 us -> 8.95 us  [gathered(): return lax.all_gather(matrix, 'dp', axis=0, tiled=True)]
    dot_general x16 -> x2, matrix products: 69.5 us -> 12.2 us  [body(): proj = jnp.dot(merged(normed), w_in, preferred_element_type=F32)]
    dot_general x8 -> x2, matrix products: 21.7 us -> 2.86 us  [over_rows(): return lax.dot_general(left, right, TN, preferred_element_type=F32)]
    slice x1 -> x6, local copies, waits for them, and re-layouts: 0.8 us -> 17.5 us  [the longest x2 7.58 us: layer_weights(): second[:, v_width:v_width + 2 * hidden_pad]]
    convert_element_type x17 -> x9, other arithmetic: 17.3 us -> 4.75 us  [columns(): jnp.stack([part[:, start:start + size] for part in parts]).astype(F32)]
  transfers between devices with their start and end apart: 24 -> 8, of which waited for: 24 -> 3; matrix products, arithmetic and copies ran while one was open for 10% -> 7% of each run, Pallas kernels for 5% -> 37%
where the time goes in v2:
time: 659 us; the launch traced here: 650 us
  Pallas kernels  420 us (64%)
  waiting for transfers between devices  76 us (12%)
  blocking collectives  63.1 us (10%)
  local copies, waits for them, and re-layouts  45.2 us (7%)
  between operations  15.2 us (2%)
  matrix products  15.1 us (2%)
  other arithmetic  14.7 us (2%)
    pallas_call x7, Pallas kernels, line_call(): pl.pallas_call(kernel, in_specs=[pl.BlockSpec(memory_space=pltpu.VMEM)] *...  350 us
    reduce_scatter x4, waiting for transfers between devices, reduced(): return lax.psum_scatter(matrix, 'dp', scatter_dimension=0, tiled=True)  65.5 us
    pallas_call x2, Pallas kernels, delta_backward(): pl.pallas_call(functools.partial(backward_kernel, chunk, heads), grid=(se...  45.4 us
    psum x1, blocking collectives, body(): lax.psum((jnp.stack(norm_grads), jnp.stack(gain_grads)), ('dp', 'tensor'))  37.9 us
    psum x1, blocking collectives, body(): taps = lax.psum(taps, 'dp')  25.1 us
    pallas_call x2, Pallas kernels, delta_forward(): pl.pallas_call(functools.partial(forward_kernel, chunk, refine), grid=(se...  24.7 us
    unnamed x112, local copies, waits for them, and re-layouts  18.2 us
  transfers between devices with their start and end apart: 8, of which 3 were waited for; matrix products, arithmetic and copies ran while one was open for 7% of the time, Pallas kernels for 37%

profile of v2, /device:TPU:0, one launch (start us, length us, event | category | flops | bytes accessed | tf_op | source)
XLA Modules:
  0.0 649.6 jit_solution(10027283486072175478)
XLA Ops:
  12.2 1.1 convert.52
  19.4 42.6 %start.1 = (bf16[4,2,64,1024]{3,2,1,0:T(8,128)(2,1)}, bf16[4,2,64,1024]{3,2,1,0:T(8,128)(2,1)}) custom-call(bf16[2,64,1024]{2,1,0:T(8,128)(2,1)} %bitcast.167, bf16[2,64,1024]{2,1,0:T(8,128)(2,1)} %bitcast.174, f32[1,1024]{1,0:T(1,128)} %get-tuple-element.203.gain), custom_call_target="tpu_custom_call" | custom-call | tf_op jit(solution)/shard_map/start/pallas_call | solution.py:767
  62.3 6.1 fusion.28.qref.kref.vref.gref.pair_ref
  68.4 12.3 %delta_forward.2 = (bf16[512,512]{1,0:T(8,128)(2,1)S(1)}, f32[512,512]{1,0:T(8,128)S(1)}, f32[512,512]{1,0:T(8,128)S(1)}, f32[1,2,4,128,128]{4,3,2,1,0:T(8,128)S(1)}, f32[1,2,4,128,256]{4,3,2,1,0:T(8,128)S(1)}) custom-call(f32[512,1664]{1,0:T(8,128)} %fusion.28.qref.kref.vref.gref.pair_ref, f32[512,1664]{1,0:T(8,128)} %fusion.28.qref.kref.vref.gref.pair_ref, ...), custom_call_target="tpu_custom_call" | custom-call | tf_op jit(solution)/shard_map/delta_forward/pallas_call | solution.py:370
  85.3 8.9 %all-gather.7.cloned.1.call-done = bf16[1024,2816]{1,0:T(8,128)(2,1)} async-done(((bf16[128,2816]{1,0:T(8,128)(2,1)}), bf16[1024,2816]{1,0:T(8,128)(2,1)}) %all-gather.7.cloned.1.call-update) | async-done | bytes 5767184 | tf_op jit(solution)/shard_map/all_gather | solution.py:879
  94.2 2.3 slice.283.w_out
  96.5 2.7 slice.285.w_down
  99.2 3.7 slice.284.w_up
  102.9 79.9 %ffn_forward.2 = (f32[2,64,1024]{2,1,0:T(8,128)}, bf16[4,2,64,1024]{3,2,1,0:T(8,128)(2,1)}, f32[4,2,64,1536]{3,2,1,0:T(8,128)}, bf16[4,2,64,768]{3,2,1,0:T(8,128...) custom-call(bf16[4,2,64,512]{3,2,1,0:T(8,128)(2,1)} %bitcast.163, bf16[1024,512]{1,0:T(8,128)(2,1)} %slice.283.w_out, ...), custom_call_target="tpu_custom_call" | custom-call | tf_op jit(solution)/shard_map/ffn_forward/pallas_call | solution.py:767
  182.8 6.1 fusion.29.qref.kref.vref.gref.pair_ref
  189.0 12.4 %delta_forward.3 = (bf16[512,512]{1,0:T(8,128)(2,1)S(1)}, f32[512,512]{1,0:T(8,128)S(1)}, f32[512,512]{1,0:T(8,128)S(1)}, f32[1,2,4,128,128]{4,3,2,1,0:T(8,128)S(1)}, f32[1,2,4,128,256]{4,3,2,1,0:T(8,128)S(1)}) custom-call(f32[512,1664]{1,0:T(8,128)} %fusion.29.qref.kref.vref.gref.pair_ref, f32[512,1664]{1,0:T(8,128)} %fusion.29.qref.kref.vref.gref.pair_ref, ...), custom_call_target="tpu_custom_call" | custom-call | tf_op jit(solution)/shard_map/delta_forward/pallas_call | solution.py:370
  206.0 2.3 slice.295.w_out
  208.2 2.6 slice.297.w_down
  210.9 3.8 slice.296.w_up
  214.7 61.7 %ffn_forward.3 = (f32[2,64,1024]{2,1,0:T(8,128)}, bf16[4,2,64,1024]{3,2,1,0:T(8,128)(2,1)}, f32[4,2,64,1536]{3,2,1,0:T(8,128)}, bf16[4,2,64,768]{3,2,1,0:T(8,128)(2,1)}, f32[2,64,1024]{2,1,0:T(8,128)}) custom-call(bf16[4,2,64,512]{3,2,1,0:T(8,128)(2,1)} %bitcast.165, bf16[1024,512]{1,0:T(8,128)(2,1)} %slice.295.w_out, bf16[1024,1536]{1,0:T(8,128)(2,1)} %slice.296.w_up, ...), custom_call_target="tpu_custom_call" | custom-call | tf_op jit(solution)/shard_map/ffn_forward/pallas_call | solution.py:767
  276.5 47.4 %ffn_backward.2 = (f32[4,2,64,512]{3,2,1,0:T(8,128)}, bf16[1024,2304]{1,0:T(8,128)(2,1)}, bf16[4,2,64,1024]{3,2,1,0:T(8,128)(2,1)}, f32[2,64,1024]{2,1,0:T(8,128)}, f32[1,1024]{1,0:T(1,128)}) custom-call(bf16[4,2,64,1024]{3,2,1,0:T(8,128)(2,1)} %get-tuple-element.79.cot, bf16[4,2,64,768]{3,2,1,0:T(8,128)(2,1)} %get-tuple-element.80.hidden, ...), custom_call_target="tpu_custom_call" | custom-call | tf_op jit(solution)/shard_map/ffn_backward/pallas_call | solution.py:767
  323.9 22.6 %delta_backward.2 = (bf16[512,1664]{1,0:T(8,128)(2,1)}, f32[1,2,4,256]{3,2,1,0:T(4,128)}, f32[1,4,512]{2,1,0:T(4,128)}, f32[1,2,8,128]{3,2,1,0:T(8,128)}, f32[1,2,1,256]{3,2,1,0:T(1,128)}) custom-call(f32[512,1664]{1,0:T(8,128)} %fusion.29.qref.kref.vref.gref.pair_ref, f32[512,1664]{1,0:T(8,128)} %fusion.29.qref.kref.vref.gref.pair_ref, ...), custom_call_target="tpu_custom_call" | custom-call | tf_op jit(solution)/shard_map/delta_backward/pallas_call | solution.py:399
  346.4 45.0 %mixer_backward.2 = (f32[2,64,1024]{2,1,0:T(8,128)}, f32[1,1024]{1,0:T(1,128)}, bf16[1024,2176]{1,0:T(8,128)(2,1)}, bf16[4,2,64,1024]{3,2,1,0:T(8,128)(2,1)}) custom-call(bf16[4,2,64,1664]{3,2,1,0:T(8,128)(2,1)} %bitcast.171, bf16[1024,1664]{1,0:T(8,128)(2,1)} %all-gather.9.cloned.1.call-done.w_in, bf16[4,2,64,1024]{3,2,1,0:T(8,128)(2,1)} %get-tuple-element.67.normed, ...), custom_call_target="tpu_custom_call" | custom-call | tf_op jit(solution)/shard_map/mixer_backward/pallas_call | solution.py:767
  391.6 47.0 %ffn_backward.3 = (f32[4,2,64,512]{3,2,1,0:T(8,128)}, bf16[1024,2304]{1,0:T(8,128)(2,1)}, bf16[4,2,64,1024]{3,2,1,0:T(8,128)(2,1)}, f32[2,64,1024]{2,1,0:T(8,128)}, f32[1,1024]{1,0:T(1,128)}) custom-call(bf16[4,2,64,1024]{3,2,1,0:T(8,128)(2,1)} %get-tuple-element.88.cot, bf16[4,2,64,768]{3,2,1,0:T(8,128)(2,1)} %get-tuple-element.89.hidden, ...), custom_call_target="tpu_custom_call" | custom-call | tf_op jit(solution)/shard_map/ffn_backward/pallas_call | solution.py:767
  438.6 22.8 %delta_backward.3 = (bf16[512,1664]{1,0:T(8,128)(2,1)}, f32[1,2,4,256]{3,2,1,0:T(4,128)}, f32[1,4,512]{2,1,0:T(4,128)}, f32[1,2,8,128]{3,2,1,0:T(8,128)}, f32[1,2,1,256]{3,2,1,0:T(1,128)}) custom-call(f32[512,1664]{1,0:T(8,128)} %fusion.28.qref.kref.vref.gref.pair_ref, f32[512,1664]{1,0:T(8,128)} %fusion.28.qref.kref.vref.gref.pair_ref, ...), custom_call_target="tpu_custom_call" | custom-call | tf_op jit(solution)/shard_map/delta_backward/pallas_call | solution.py:399
  463.2 2.1 convolution_convert_fusion
  465.3 2.4 pad_maximum_fusion
  469.3 26.3 %mixer_backward.3 = (f32[2,64,1024]{2,1,0:T(8,128)}, f32[1,1024]{1,0:T(1,128)}) custom-call(bf16[4,2,64,1664]{3,2,1,0:T(8,128)(2,1)} %bitcast.170, bf16[1024,1664]{1,0:T(8,128)(2,1)} %all-gather.5.cloned.1.call-done.w_in, bf16[4,2,64,1024]{3,2,1,0:T(8,128)(2,1)} %get-tuple-element.65.normed, bf16[4,2,64,512]{3,2,1,0:T(8,128)(2,1)} %bitcast.164, ...), custom_call_target="tpu_custom_call" | custom-call | tf_op jit(solution)/shard_map/mixer_backward/pallas_call | solution.py:767
  498.2 37.9 %all-reduce.11 = (f32[2,2,1024]{2,1,0:T(2,128)}, f32[2,256]{1,0:T(2,128)}) all-reduce(f32[2,2,1024]{2,1,0:T(2,128)S(1)} %pad_maximum_fusion.3, f32[2,256]{1,0:T(2,128)S(1)} %pad_maximum_fusion.5), channel_id=1, replica_groups=mesh['dp'=8,'tensor'=4] {'dp','tensor'}, use_global_device_ids=true, to_apply=%region_7.8 | all-reduce | flops 4608 | bytes 36864 | tf_op jit(solution)/shard_map/psum | solution.py:972
  536.2 25.1 %all-reduce.12 = (f32[2,2,4,256]{3,2,1,0:T(4,128)}, f32[2,4,512]{2,1,0:T(4,128)}, f32[2,2,2]{2,1,0:T(2,128)}) all-reduce(f32[2,2,4,256]{3,2,1,0:T(4,128)S(1)} %pad_maximum_fusion.1, f32[2,4,512]{2,1,0:T(4,128)S(1)} %pad_maximum_fusion.2, f32[2,2,2]{2,1,0:T(2,128)S(1)} %pad_maximum_fusion.4), channel_id=1, replica_groups=mesh['dp'=8,'tensor'=4] {'dp'}, use_global_device_ids=true, to_apply=%region_4.5 | all-reduce | flops 8200 | bytes 65600 | tf_op jit(solution)/shard_map/psum | solution.py:971
  569.6 8.9 %reduce-scatter.9.cloned.1.call-done = bf16[128,2304]{1,0:T(8,128)(2,1)} async-done(((bf16[1024,2304]{1,0:T(8,128)(2,1)}), bf16[128,2304]{1,0:T(8,128)(2,1)}) %reduce-scatter.9.cloned.1.call-update) | async-done | bytes 589840 | tf_op jit(solution)/shard_map/reduce_scatter | solution.py:882
  578.5 1.2 slice_bitcast_fusion.1
  579.7 56.6 %reduce-scatter.11.cloned.1.call-done = bf16[128,2304]{1,0:T(8,128)(2,1)} async-done(((bf16[1024,2304]{1,0:T(8,128)(2,1)}), bf16[128,2304]{1,0:T(8,128)(2,1)}) %reduce-scatter.11.cloned.1.call-update) | async-done | bytes 589840 | tf_op jit(solution)/shard_map/reduce_scatter | solution.py:882
  636.2 1.2 slice_bitcast_fusion
  637.5 1.1 copy.77
  638.7 1.1 copy.76
  639.9 1.1 copy.75
  (191 shorter events, 35.8 us)
Async XLA Ops:
  7.2 55.1 %all-gather.5.cloned.1.call-start = ((), (), s32[]{:S(2)}) async-start(), calls=%async_computation.4 | async-start | bytes 3833856 | tf_op jit(solution)/shard_map/all_gather | solution.py:879
  12.1 82.1 %all-gather.7.cloned.1.call-start = ((), (), s32[]{:S(2)}) async-start(), calls=%async_computation.5 | async-start | bytes 6488064 | tf_op jit(solution)/shard_map/all_gather | solution.py:879
  14.9 167.9 %all-gather.9.cloned.1.call-start = ((), (), s32[]{:S(2)}) async-start(), calls=%async_computation.6 | async-start | bytes 3833856 | tf_op jit(solution)/shard_map/all_gather | solution.py:879
  15.0 47.0 %copy-start.47 = (f32[2,2,2]{2,1,0:T(2,128)S(1)}, f32[2,2,2]{2,1,0:T(2,128)}, u32[]{:S(2)}) copy-start(f32[2,2,2]{2,1,0:T(2,128)} %param.30) | copy-start | bytes 100
  15.0 47.0 %copy-start.48 = (f32[2,256]{1,0:T(2,128)S(1)}, f32[2,256]{1,0:T(2,128)}, u32[]{:S(2)}) copy-start(f32[2,256]{1,0:T(2,128)} %param.32) | copy-start | bytes 6148
  15.0 47.1 %copy-start.36 = (f32[2,2,4,256]{3,2,1,0:T(4,128)S(1)}, f32[2,2,4,256]{3,2,1,0:T(4,128)}, u32[]{:S(2)}) copy-start(f32[2,2,4,256]{3,2,1,0:T(4,128)} %param.28) | copy-start | bytes 49156
  15.8 46.4 %copy-start.37 = (f32[2,4,512]{2,1,0:T(4,128)S(1)}, f32[2,4,512]{2,1,0:T(4,128)}, u32[]{:S(2)}) copy-start(f32[2,4,512]{2,1,0:T(4,128)} %param.29) | copy-start | bytes 49156
  15.8 190.2 %all-gather.11.cloned.1.call-start = ((), (), s32[]{:S(2)}) async-start(), calls=%async_computation.7 | async-start | bytes 6488064 | tf_op jit(solution)/shard_map/all_gather | solution.py:879
  16.8 544.5 %reduce-scatter.7.cloned.1.call-start = ((), (), s32[]{:S(2)}) async-start(), calls=%async_computation.9 | async-start | bytes 5013504 | tf_op jit(solution)/shard_map/reduce_scatter | solution.py:882
  18.7 170.3 %copy-start = (f32[1,512,8]{2,1,0:T(8,128)}, f32[1,512,8]{2,1,0:T(8,128)S(1)}, u32[]{:S(2)}) copy-start(f32[1,512,8]{2,1,0:T(8,128)S(1)} %copy.63.col_ref) | copy-start | bytes 49156
  62.0 126.9 %copy-start.12 = (f32[1,8,512]{2,1,0:T(8,128)}, f32[1,8,512]{2,1,0:T(8,128)S(1)}, u32[]{:S(2)}) copy-start(f32[1,8,512]{2,1,0:T(8,128)S(1)} %stack.181.row_ref) | copy-start | bytes 49156
  62.1 6.3 copy-start.17
  62.1 126.9 %copy-start.19 = (f32[2,2]{1,0:T(2,128)}, f32[2,2]{1,0:T(2,128)S(1)}, u32[]{:S(2)}) copy-start(f32[2,2]{1,0:T(2,128)S(1)} %get-tuple-element.211.head_table) | copy-start | bytes 52
  62.1 6.2 copy-start.18
  62.1 126.9 %copy-start.20 = (f32[1,256]{1,0:T(1,128)}, f32[1,256]{1,0:T(1,128)S(1)}, u32[]{:S(2)}) copy-start(f32[1,256]{1,0:T(1,128)S(1)} %get-tuple-element.209.gain) | copy-start | bytes 3076
  62.2 6.2 copy-start.13
  62.2 126.8 %copy-start.15 = (f32[2,4,256]{2,1,0:T(4,128)}, f32[2,4,256]{2,1,0:T(4,128)S(1)}, u32[]{:S(2)}) copy-start(f32[2,4,256]{2,1,0:T(4,128)S(1)} %get-tuple-element.207.tap_qk) | copy-start | bytes 24580
  62.2 126.8 %copy-start.16 = (f32[4,512]{1,0:T(4,128)}, f32[4,512]{1,0:T(4,128)S(1)}, u32[]{:S(2)}) copy-start(f32[4,512]{1,0:T(4,128)S(1)} %get-tuple-element.205.tap_v) | copy-start | bytes 24580
  391.5 170.7 %reduce-scatter.5.cloned.1.call-start = ((), (), s32[]{:S(2)}) async-start(), calls=%async_computation.8 | async-start | bytes 5013504 | tf_op jit(solution)/shard_map/reduce_scatter | solution.py:882
  438.6 22.8 %copy-start.2 = (bf16[512,512]{1,0:T(8,128)(2,1)S(1)}, bf16[512,512]{1,0:T(8,128)(2,1)}, u32[]{:S(2)}) copy-start(bf16[512,512]{1,0:T(8,128)(2,1)} %copy-done.1) | copy-start | bytes 1572868
  438.6 22.8 %copy-start.23 = (bf16[4,2,64,1024]{3,2,1,0:T(8,128)(2,1)S(1)}, bf16[4,2,64,1024]{3,2,1,0:T(8,128)(2,1)}, u32[]{:S(2)}) copy-start(bf16[4,2,64,1024]{3,2,1,0:T(8,128)(2,1)} %get-tuple-element.96.mixer_cot) | copy-start | bytes 3145732
  467.7 110.8 %reduce-scatter.9.cloned.1.call-start = ((), (), s32[]{:S(2)}) async-start(), calls=%async_computation.10 | async-start | bytes 5308416 | tf_op jit(solution)/shard_map/reduce_scatter | solution.py:882
  468.4 167.8 %reduce-scatter.11.cloned.1.call-start = ((), (), s32[]{:S(2)}) async-start(), calls=%async_computation.11 | async-start | bytes 5308416 | tf_op jit(solution)/shard_map/reduce_scatter | solution.py:882
  469.2 27.3 %copy-start.46 = (f32[1,2,1,256]{3,2,1,0:T(1,128)S(1)}, f32[1,2,1,256]{3,2,1,0:T(1,128)}, u32[]{:S(2)}) copy-start(f32[1,2,1,256]{3,2,1,0:T(1,128)} %get-tuple-element.112) | copy-start | bytes 6148
  469.2 27.3 %copy-start.45 = (f32[1,2,1,256]{3,2,1,0:T(1,128)S(1)}, f32[1,2,1,256]{3,2,1,0:T(1,128)}, u32[]{:S(2)}) copy-start(f32[1,2,1,256]{3,2,1,0:T(1,128)} %get-tuple-element.113) | copy-start | bytes 6148
  469.2 28.2 %copy-start.44 = (f32[1,1024]{1,0:T(1,128)S(1)}, f32[1,1024]{1,0:T(1,128)}, u32[]{:S(2)}) copy-start(f32[1,1024]{1,0:T(1,128)} %get-tuple-element.109) | copy-start | bytes 12292
  469.2 28.9 %copy-start.42 = (f32[1,1024]{1,0:T(1,128)S(1)}, f32[1,1024]{1,0:T(1,128)}, u32[]{:S(2)}) copy-start(f32[1,1024]{1,0:T(1,128)} %get-tuple-element.111) | copy-start | bytes 12292
  469.2 28.9 %copy-start.43 = (f32[1,1024]{1,0:T(1,128)S(1)}, f32[1,1024]{1,0:T(1,128)}, u32[]{:S(2)}) copy-start(f32[1,1024]{1,0:T(1,128)} %get-tuple-element.110) | copy-start | bytes 12292
  469.2 66.9 %copy-start.39 = (f32[1,2,4,256]{3,2,1,0:T(4,128)S(1)}, f32[1,2,4,256]{3,2,1,0:T(4,128)}, u32[]{:S(2)}) copy-start(f32[1,2,4,256]{3,2,1,0:T(4,128)} %get-tuple-element.103) | copy-start | bytes 24580
  469.2 66.9 %copy-start.41 = (f32[1,2,4,256]{3,2,1,0:T(4,128)S(1)}, f32[1,2,4,256]{3,2,1,0:T(4,128)}, u32[]{:S(2)}) copy-start(f32[1,2,4,256]{3,2,1,0:T(4,128)} %get-tuple-element.102) | copy-start | bytes 24580
  469.3 66.9 %copy-start.38 = (f32[1,4,512]{2,1,0:T(4,128)S(1)}, f32[1,4,512]{2,1,0:T(4,128)}, u32[]{:S(2)}) copy-start(f32[1,4,512]{2,1,0:T(4,128)} %get-tuple-element.105) | copy-start | bytes 24580
  469.3 66.9 %copy-start.40 = (f32[1,4,512]{2,1,0:T(4,128)S(1)}, f32[1,4,512]{2,1,0:T(4,128)}, u32[]{:S(2)}) copy-start(f32[1,4,512]{2,1,0:T(4,128)} %get-tuple-element.104) | copy-start | bytes 24580
  (25 other events, 49.3 us)
Sparse Core Ops, SparseCore 0:
  12.2 36.1 all-gather.4
  50.8 43.3 all-gather.6
  96.7 33.4 all-gather.8
  132.4 43.3 all-gather.10
  391.6 52.0 reduce-scatter.6
  467.8 52.7 reduce-scatter.4
  524.1 54.3 reduce-scatter.8
  582.3 53.8 reduce-scatter.10

commit v3 on v2

--- a/solution.py
+++ b/solution.py
@@ -15,12 +15,16 @@
 FLOOR = 0.01
 
 
+def cost(micros):
+    return pl.CostEstimate(flops=0, bytes_accessed=int(micros * 3.5e6), transcendentals=0)
+
+
 def split(x):
     high = x.astype(BF16)
     return high, (x - high.astype(F32)).astype(BF16)
 
 
-def mm(a, b, dims, passes=1):
+def mm(a, b, dims, passes=3):
     def one(p, q):
         return lax.dot_general(p, q, dims, preferred_element_type=F32)
 
@@ -77,8 +81,8 @@
         found = [x - mm(t, x, NN) for x, t in zip(found, half)]
         block *= 2
     for _ in range(refine):
-        rest = [(x - eye) + mm(part, x, NN, 3) for x, part in zip(found, lower)]
-        found = [x - mm(x, r, NN, 1) for x, r in zip(found, rest)]
+        rest = [(x - eye) + mm(part, x, NN) for x, part in zip(found, lower)]
+        found = [x - mm(x, r, NN) for x, r in zip(found, rest)]
     return found
 
 
@@ -384,6 +388,7 @@
             jax.ShapeDtypeStruct((seqs, heads, chunks, dk, dv), F32),
         ],
         compiler_params=pltpu.CompilerParams(vmem_limit_bytes=48 * 2**20),
+        cost_estimate=cost(15),
         name="delta_forward",
     )(proj, proj, proj, proj, proj, taps_qk, taps_v, head_table, gain, cols, rows)
 
@@ -421,6 +426,7 @@
             jax.ShapeDtypeStruct((seqs, heads, 1, dv), F32),
         ],
         compiler_params=pltpu.CompilerParams(vmem_limit_bytes=56 * 2**20),
+        cost_estimate=cost(25),
         name="delta_backward",
     )(proj, proj, proj, proj, proj, taps_qk, taps_v, head_table, gain, cols, rows, *saved, dmix)
 
@@ -440,10 +446,16 @@
         for m in range(4):
             @pl.when(self.me == m)
             def _():
-                others = [t for t in range(4) if t != m and {t, m} != {0, 3}]
-                for t in others:
-                    pl.semaphore_signal(barrier, inc=1, device_id={"tensor": t}, device_id_type=MESH)
-                pl.semaphore_wait(barrier, len(others))
+                for t in range(4):
+                    if t != m and {t, m} != {0, 3}:
+                        pl.semaphore_signal(barrier, inc=1, device_id={"tensor": t}, device_id_type=MESH)
+
+    def meet(self, others=0):
+        barrier = pltpu.get_barrier_semaphore()
+        for m in range(4):
+            @pl.when(self.me == m)
+            def _():
+                pl.semaphore_wait(barrier, others + (2 if m in (0, 3) else 3))
 
     def copy(self, phase, source, target, to, send_at, recv_at):
         return pltpu.make_async_remote_copy(
@@ -459,14 +471,18 @@
                     if t != m and {t, m} != {0, 3}:
                         self.copy(phase, blocks[m], blocks[m], t, t, m).start()
 
-    def gather_finish(self, phase, blocks):
+    def gather_forward(self, phase, blocks):
+        for m in (1, 2):
+            @pl.when(self.me == m)
+            def _():
+                far, to = (3, 0) if m == 1 else (0, 3)
+                self.copy(phase, blocks[far], blocks[far], to, m, far).wait_recv()
+                self.copy(phase, blocks[far], blocks[far], to, m, far).start()
+
+    def gather_wait(self, phase, blocks):
         for m in range(4):
             @pl.when(self.me == m)
             def _():
-                if m in (1, 2):
-                    far, to = (3, 0) if m == 1 else (0, 3)
-                    self.copy(phase, blocks[far], blocks[far], to, m, far).wait_recv()
-                    self.copy(phase, blocks[far], blocks[far], to, m, far).start()
                 for b in range(4):
                     if b != m and not (m in (1, 2) and b == (3 if m == 1 else 0)):
                         self.copy(phase, blocks[b], blocks[b], b, b, b).wait_recv()
@@ -530,6 +546,184 @@
                         self.copy(phase, parts[t], slots[m], t, t, m).wait_send()
 
 
+TURN_AT = 1
+
+
+class Turns:
+    def __init__(self, gate):
+        self.gate = gate
+        self.me = lax.axis_index("dp")
+        self.second = lax.rem(self.me, 2)
+        self.sibling = self.me + 1 - 2 * self.second
+
+    def greet(self):
+        pl.semaphore_signal(
+            pltpu.get_barrier_semaphore(), inc=1, device_id={"dp": self.sibling}, device_id_type=MESH
+        )
+
+    def wait(self):
+        @pl.when(self.second == 1)
+        def _():
+            pl.semaphore_wait(self.gate, 1)
+
+    def give(self):
+        @pl.when(self.second == 0)
+        def _():
+            pl.semaphore_signal(self.gate, inc=1, device_id={"dp": self.sibling}, device_id_type=MESH)
+
+
+class Sums:
+    def __init__(self, source, near, far, near_send, near_recv, far_send, far_recv):
+        self.source, self.near, self.far = source, near, far
+        self.near_send, self.near_recv, self.far_send, self.far_recv = near_send, near_recv, far_send, far_recv
+        self.pairs = source.shape[0]
+        self.group = self.pairs // 4
+        me = lax.axis_index("dp")
+        self.parity, self.mine = lax.rem(me, 2), lax.div(me, 2)
+
+    def greet(self):
+        barrier = pltpu.get_barrier_semaphore()
+        sibling = 2 * self.mine + 1 - self.parity
+        pl.semaphore_signal(barrier, inc=1, device_id={"dp": sibling}, device_id_type=MESH)
+
+        def signal(i, carry):
+            other = 2 * lax.rem(self.mine + i, self.pairs) + self.parity
+            pl.semaphore_signal(barrier, inc=1, device_id={"dp": other}, device_id_type=MESH)
+            return carry
+
+        lax.fori_loop(1, self.pairs, signal, 0)
+        return self.pairs
+
+    def near_copy(self, m):
+        span = pl.ds(m * self.group, self.group)
+        return pltpu.make_async_remote_copy(
+            src_ref=self.source.at[span, 1 - self.parity], dst_ref=self.near.at[span],
+            send_sem=self.near_send.at[m], recv_sem=self.near_recv.at[m],
+            device_id={"dp": 2 * self.mine + 1 - self.parity}, device_id_type=MESH,
+        )
+
+    def far_copy(self, j, slot, to):
+        return pltpu.make_async_remote_copy(
+            src_ref=self.near.at[j], dst_ref=self.far.at[slot], send_sem=self.far_send.at[j],
+            recv_sem=self.far_recv.at[slot], device_id={"dp": 2 * to + self.parity}, device_id_type=MESH,
+        )
+
+    def start(self, m):
+        self.near_copy(m).start()
+
+    def turn(self, m):
+        self.near_copy(m).wait_recv()
+        rows = self.near.shape[1]
+        step = 16
+
+        def add(i, carry):
+            j = m * self.group + lax.div(i, rows // step)
+            span = pl.ds(pl.multiple_of(lax.rem(i, rows // step) * step, step), step)
+            both = self.source[j, self.parity, span, :].astype(F32) + self.near[j, span, :].astype(F32)
+            self.near[j, span, :] = both.astype(BF16)
+            return carry
+
+        lax.fori_loop(0, self.group * (rows // step), add, 0)
+
+        def send(i, carry):
+            j = m * self.group + i
+
+            @pl.when(j != self.mine)
+            def _():
+                self.far_copy(j, self.mine, j).start()
+
+            return carry
+
+        lax.fori_loop(0, self.group, send, 0)
+
+    def finish(self, out):
+        def arrive(i, carry):
+            slot = lax.rem(self.mine + i, self.pairs)
+            self.far_copy(slot, slot, slot).wait_recv()
+            return carry
+
+        lax.fori_loop(1, self.pairs, arrive, 0)
+        rows = out.shape[0]
+        step = 16
+
+        def add(i, carry):
+            span = pl.ds(pl.multiple_of(i * step, step), step)
+            total = self.near[self.mine, span, :].astype(F32)
+
+            def more(j, value):
+                return value + self.far[lax.rem(self.mine + j, self.pairs), span, :].astype(F32)
+
+            if self.pairs <= 4:
+                for j in range(1, self.pairs):
+                    total = more(j, total)
+            else:
+                total = lax.fori_loop(1, self.pairs, more, total)
+            out[span, :] = total
+            return carry
+
+        lax.fori_loop(0, rows // step, add, 0)
+
+        def sent(i, carry):
+            slot = lax.rem(self.mine + i, self.pairs)
+            self.far_copy(slot, slot, slot).wait_send()
+            return carry
+
+        lax.fori_loop(1, self.pairs, sent, 0)
+        for m in range(4):
+            self.near_copy(m).wait_send()
+
+
+class Smalls:
+    def __init__(self, axis, land, send_sem, recv_sem):
+        self.axis, self.land, self.send_sem, self.recv_sem = axis, land, send_sem, recv_sem
+        self.me, self.count = lax.axis_index(axis), land.shape[0]
+
+    def other(self, i):
+        return lax.rem(self.me + i, self.count)
+
+    def greet(self):
+        barrier = pltpu.get_barrier_semaphore()
+
+        def signal(i, carry):
+            pl.semaphore_signal(barrier, inc=1, device_id={self.axis: self.other(i)}, device_id_type=MESH)
+            return carry
+
+        lax.fori_loop(1, self.count, signal, 0)
+        return self.count - 1
+
+    def copy(self, slot, to):
+        return pltpu.make_async_remote_copy(
+            src_ref=self.land.at[self.me], dst_ref=self.land.at[slot], send_sem=self.send_sem.at[to],
+            recv_sem=self.recv_sem.at[slot], device_id={self.axis: to}, device_id_type=MESH,
+        )
+
+    def start(self):
+        def send(i, carry):
+            self.copy(self.me, self.other(i)).start()
+            return carry
+
+        lax.fori_loop(1, self.count, send, 0)
+
+    def finish(self):
+        def arrive(i, carry):
+            self.copy(self.other(i), self.other(i)).wait_recv()
+            return carry
+
+        lax.fori_loop(1, self.count, arrive, 0)
+
+        def add(i, value):
+            return value + self.land[i]
+
+        total = lax.fori_loop(1, self.count, add, self.land[0])
+
+        def sent(i, carry):
+            self.copy(self.me, self.other(i)).wait_send()
+            return carry
+
+        lax.fori_loop(1, self.count, sent, 0)
+        return total
+
+
 def half_of(ref, h):
     value = ref[:, h]
     return value.reshape(value.shape[0] * value.shape[1], value.shape[2])
@@ -562,15 +756,19 @@
 def row_grads(left, right, out, column):
     rows = left.shape[0] * left.shape[1] * left.shape[2]
     width = right.shape[3]
+    pairs, _, own, _ = out.shape
+    group = pairs // 4
+    tall = group * 2 * own
 
     def piece(m):
-        m = pl.multiple_of(m * 256, 256)
-        turned = jnp.transpose(left[:, :, :, pl.ds(m, 256)].reshape(rows, 256))
+        start = pl.multiple_of(m * tall, tall)
+        turned = jnp.transpose(left[:, :, :, pl.ds(start, tall)].reshape(rows, tall))
         for n in range(0, width, 512):
             size = min(512, width - n)
             tile = right[:, :, :, n : n + size].reshape(rows, size)
             value = lax.dot_general(turned, tile, NN, preferred_element_type=F32)
-            out[pl.ds(m, 256), column + n : column + n + size] = value.astype(BF16)
+            span = pl.ds(m * group, group)
+            out[span, :, :, column + n : column + n + size] = value.astype(BF16).reshape(group, 2, own, size)
 
     return piece
 
@@ -597,37 +795,54 @@
 
 def start_kernel(rows, cot, gain, normed, cot_all, send_sem, recv_sem):
     line = Line(send_sem, recv_sem)
+    line.greet()
     for h in range(HALVES):
         normed[line.me, h] = rms(rows[h].astype(F32), gain[...]).astype(BF16)
         cot_all[line.me, h] = cot[h]
-    line.greet()
-    for k, ref in ((0, normed), (2, cot_all)):
-        for h in range(HALVES):
-            line.gather_start(k + h, blocks_of(ref, h))
-    for k, ref in ((0, normed), (2, cot_all)):
-        for h in range(HALVES):
-            line.gather_finish(k + h, blocks_of(ref, h))
-    for k, ref in ((0, normed), (2, cot_all)):
-        for h in range(HALVES):
-            line.gather_drain(k + h, blocks_of(ref, h))
-
-
-def ffn_forward_kernel(
-    last, mixer, w_out, w_up, w_down, rows, gain, gain_next, middle, normed, pre, hidden, out_rows, *rest
-):
+    line.meet()
+    both = [(k + h, blocks_of(ref, h)) for k, ref in ((0, normed), (2, cot_all)) for h in range(HALVES)]
+    for item in both:
+        line.gather_start(*item)
+    for item in both:
+        line.gather_forward(*item)
+    for item in both:
+        line.gather_wait(*item)
+    for item in both:
+        line.gather_drain(*item)
+
+
+def slices_of(weights, v_width, wide):
+    return (
+        weights.at[:, :v_width],
+        weights.at[:, v_width : v_width + 2 * wide],
+        weights.at[:, v_width + 2 * wide :],
+    )
+
+
+def ffn_forward_kernel(last, mixer, weights, rows, gain, gain_next, middle, normed, pre, hidden, out_rows, *rest):
     if last:
         part, slots, total, send_sem, recv_sem = rest
     else:
-        normed_next, part, slots, total, send_sem, recv_sem = rest
+        normed_next, part, slots, total, send_sem, recv_sem, gate = rest
     line = Line(send_sem, recv_sem)
-    wide = w_down.shape[1]
+    wide = hidden.shape[3]
+    w_out, w_up, w_down = slices_of(weights, mixer.shape[3], wide)
     block = rows.shape[1]
     line.greet()
-    for h in range(HALVES):
-        partial_sums(half_of(mixer, h), w_out, part, 0, h)
-        line.scatter_start(h, *parts_of(part, slots, 0, h))
-    for h in range(HALVES):
-        line.scatter_relay(h, *parts_of(part, slots, 0, h))
+    if last:
+        partial_sums(half_of(mixer, 0), w_out, part, 0, 0)
+        line.meet()
+    else:
+        turns = Turns(gate)
+        turns.greet()
+        partial_sums(half_of(mixer, 0), w_out, part, 0, 0)
+        line.meet(1)
+        turns.wait()
+    line.scatter_start(0, *parts_of(part, slots, 0, 0))
+    partial_sums(half_of(mixer, 1), w_out, part, 0, 1)
+    line.scatter_relay(0, *parts_of(part, slots, 0, 0))
+    line.scatter_start(1, *parts_of(part, slots, 0, 1))
+    line.scatter_relay(1, *parts_of(part, slots, 0, 1))
     for h in range(HALVES):
         both = parts_of(part, slots, 0, h)
         line.scatter_wait(h, *both)
@@ -636,8 +851,13 @@
         middle[h] = value
         normed[line.me, h] = rms(value, gain[...]).astype(BF16)
         line.gather_start(2 + h, blocks_of(normed, h))
+    line.gather_forward(2, blocks_of(normed, 0))
     for h in range(HALVES):
-        line.gather_finish(2 + h, blocks_of(normed, h))
+        if h == 1:
+            line.gather_forward(3, blocks_of(normed, 1))
+        line.gather_wait(2 + h, blocks_of(normed, h))
+        if h == TURN_AT and not last:
+            turns.give()
         left = half_of(normed, h)
 
         def step(n):
@@ -650,9 +870,10 @@
 
         for_tiles(wide, 256, step)
         partial_sums(half_of(hidden, h), w_down, part, 1, h)
+        if h == 1:
+            line.scatter_relay(4, *parts_of(part, slots, 1, 0))
         line.scatter_start(4 + h, *parts_of(part, slots, 1, h))
-    for h in range(HALVES):
-        line.scatter_relay(4 + h, *parts_of(part, slots, 1, h))
+    line.scatter_relay(5, *parts_of(part, slots, 1, 1))
     for h in range(HALVES):
         both = parts_of(part, slots, 1, h)
         line.scatter_wait(4 + h, *both)
@@ -664,7 +885,9 @@
             line.gather_start(6 + h, blocks_of(normed_next, h))
     if not last:
         for h in range(HALVES):
-            line.gather_finish(6 + h, blocks_of(normed_next, h))
+            line.gather_forward(6 + h, blocks_of(normed_next, h))
+        for h in range(HALVES):
+            line.gather_wait(6 + h, blocks_of(normed_next, h))
     for h in range(HALVES):
         line.scatter_drain(h, *parts_of(part, slots, 0, h))
         line.gather_drain(2 + h, blocks_of(normed, h))
@@ -674,13 +897,15 @@
 
 
 def ffn_backward_kernel(
-    cot, hidden, pre, normed, middle, grad, gain, w_down, w_up, w_out,
+    cot, hidden, pre, normed, middle, grad, gain, weights,
     d_mixer, grads, mixer_cot, grad_out, d_gain, d_pre, part, slots, total, send_sem, recv_sem,
 ):
     line = Line(send_sem, recv_sem)
-    wide = w_down.shape[1]
+    wide = hidden.shape[3]
+    w_out, w_up, w_down = slices_of(weights, d_mixer.shape[3], wide)
     block = middle.shape[1]
     line.greet()
+    line.meet()
     for h in range(HALVES):
         left = half_of(cot, h)
 
@@ -696,12 +921,12 @@
 
         for_tiles(wide, 256, step)
         partial_sums(half_of(d_pre, h), w_up, part, 0, h)
+        if h == 1:
+            line.scatter_relay(0, *parts_of(part, slots, 0, 0))
         line.scatter_start(h, *parts_of(part, slots, 0, h))
+    line.scatter_relay(1, *parts_of(part, slots, 0, 1))
     pieces = [row_grads(cot, hidden, grads, 0), row_grads(normed, d_pre, grads, wide)]
     run_pieces(pieces, 0, 2)
-    for h in range(HALVES):
-        line.scatter_relay(h, *parts_of(part, slots, 0, h))
-    run_pieces(pieces, 2, 4)
     d_gain[...] = jnp.zeros_like(d_gain)
     for h in range(HALVES):
         both = parts_of(part, slots, 0, h)
@@ -713,8 +938,12 @@
         grad_out[h] = value
         mixer_cot[line.me, h] = value.astype(BF16)
         line.gather_start(2 + h, blocks_of(mixer_cot, h))
+    run_pieces(pieces, 2, 3)
+    line.gather_forward(2, blocks_of(mixer_cot, 0))
+    line.gather_forward(3, blocks_of(mixer_cot, 1))
+    run_pieces(pieces, 3, 4)
     for h in range(HALVES):
-        line.gather_finish(2 + h, blocks_of(mixer_cot, h))
+        line.gather_wait(2 + h, blocks_of(mixer_cot, h))
         left = half_of(mixer_cot, h)
         for n in range(0, w_out.shape[1], 256):
             value = jnp.dot(left, w_out[:, n : n + 256], preferred_element_type=F32)
@@ -724,24 +953,22 @@
         line.gather_drain(2 + h, blocks_of(mixer_cot, h))
 
 
-def mixer_backward_kernel(last, d_proj, w_in, normed, mixer, mixer_cot, rows, grad, gain, grad_out, d_gain, *rest):
-    if last:
-        part, slots, total, send_sem, recv_sem = rest
-    else:
-        grads, cot, part, slots, total, send_sem, recv_sem = rest
+def mixer_backward_kernel(
+    d_proj, w_in, normed, mixer, mixer_cot, rows, grad, gain,
+    grad_out, d_gain, grads, cot, part, slots, total, send_sem, recv_sem,
+):
     line = Line(send_sem, recv_sem)
     line.greet()
-    for h in range(HALVES):
-        partial_sums(half_of(d_proj, h), w_in, part, 0, h)
-        line.scatter_start(h, *parts_of(part, slots, 0, h))
-    if not last:
-        width = mixer.shape[3]
-        pieces = [row_grads(mixer_cot, mixer, grads, 0), row_grads(normed, d_proj, grads, width)]
-        run_pieces(pieces, 0, 2)
-    for h in range(HALVES):
-        line.scatter_relay(h, *parts_of(part, slots, 0, h))
-    if not last:
-        run_pieces(pieces, 2, 4)
+    line.meet()
+    partial_sums(half_of(d_proj, 0), w_in, part, 0, 0)
+    line.scatter_start(0, *parts_of(part, slots, 0, 0))
+    partial_sums(half_of(d_proj, 1), w_in, part, 0, 1)
+    line.scatter_relay(0, *parts_of(part, slots, 0, 0))
+    line.scatter_start(1, *parts_of(part, slots, 0, 1))
+    line.scatter_relay(1, *parts_of(part, slots, 0, 1))
+    width = mixer.shape[3]
+    pieces = [row_grads(mixer_cot, mixer, grads, 0), row_grads(normed, d_proj, grads, width)]
+    run_pieces(pieces, 0, 2)
     d_gain[...] = jnp.zeros_like(d_gain)
     for h in range(HALVES):
         both = parts_of(part, slots, 0, h)
@@ -751,86 +978,194 @@
         d_gain[...] += gain_part
         value = grad[h] + back
         grad_out[h] = value
-        if not last:
-            cot[line.me, h] = value.astype(BF16)
-            line.gather_start(2 + h, blocks_of(cot, h))
-    if not last:
-        for h in range(HALVES):
-            line.gather_finish(2 + h, blocks_of(cot, h))
+        cot[line.me, h] = value.astype(BF16)
+        line.gather_start(2 + h, blocks_of(cot, h))
+    run_pieces(pieces, 2, 3)
+    line.gather_forward(2, blocks_of(cot, 0))
+    line.gather_forward(3, blocks_of(cot, 1))
+    run_pieces(pieces, 3, 4)
+    for h in range(HALVES):
+        line.gather_wait(2 + h, blocks_of(cot, h))
     for h in range(HALVES):
         line.scatter_drain(h, *parts_of(part, slots, 0, h))
-        if not last:
-            line.gather_drain(2 + h, blocks_of(cot, h))
-
-
-def line_call(kernel, operands, outs, scratch, phases, number, name):
+        line.gather_drain(2 + h, blocks_of(cot, h))
+
+
+def last_kernel(gain_at, norm_rows, d_proj, w_in, normed, mixer, mixer_cot, rows, grad, gain, taps, norms,
+                grad_out, summed, taps_out, norms_out,
+                d_gain, grads, taps_land, line_land, norms_land,
+                taps_send, taps_recv, line_send, line_recv, norms_send, norms_recv,
+                part, slots, total, send_sem, recv_sem, *sum_refs):
+    line = Line(send_sem, recv_sem)
+    sums = Sums(grads, *sum_refs)
+    small_taps = Smalls("dp", taps_land, taps_send, taps_recv)
+    small_line = Smalls("tensor", line_land, line_send, line_recv)
+    small_norms = Smalls("dp", norms_land, norms_send, norms_recv)
+    line.greet()
+    others = sums.greet() + small_taps.greet() + small_line.greet()
+    taps_land[small_taps.me] = taps[...]
+    partial_sums(half_of(d_proj, 0), w_in, part, 0, 0)
+    line.meet(others)
+    line.scatter_start(0, *parts_of(part, slots, 0, 0))
+    small_taps.start()
+    width = mixer.shape[3]
+    pieces = [row_grads(mixer_cot, mixer, grads, 0), row_grads(normed, d_proj, grads, width)]
+    run_pieces(pieces, 0, 1)
+    sums.start(0)
+    line.scatter_relay(0, *parts_of(part, slots, 0, 0))
+    partial_sums(half_of(d_proj, 1), w_in, part, 0, 1)
+    line.scatter_start(1, *parts_of(part, slots, 0, 1))
+    for m in range(1, 4):
+        run_pieces(pieces, m, m + 1)
+        sums.start(m)
+        sums.turn(m - 1)
+    line.scatter_relay(1, *parts_of(part, slots, 0, 1))
+    sums.turn(3)
+    d_gain[...] = jnp.zeros_like(d_gain)
+    for h in range(HALVES):
+        both = parts_of(part, slots, 0, h)
+        line.scatter_wait(h, *both)
+        line.scatter_sum(total, *both)
+        back, gain_part = rms_back(rows[h].astype(F32), gain[...], total[...])
+        d_gain[...] += gain_part
+        grad_out[h] = grad[h] + back
+    line_land[line.me] = norms[...]
+    for i in range(norm_rows):
+        line_land[line.me, gain_at + i : gain_at + i + 1, :] = d_gain[:, 128 * i : 128 * (i + 1)]
+    small_line.start()
+    norms_land[small_norms.me] = small_line.finish()
+    small_norms.start()
+    taps_out[...] = small_taps.finish()
+    for h in range(HALVES):
+        line.scatter_drain(h, *parts_of(part, slots, 0, h))
+    sums.finish(summed)
+    norms_out[...] = small_norms.finish()
+
+
+DMA = pltpu.SemaphoreType.DMA
+
+
+def line_call(kernel, operands, outs, scratch, number, name, micros):
     return pl.pallas_call(
         kernel,
         in_specs=[pl.BlockSpec(memory_space=pltpu.VMEM)] * len(operands),
         out_specs=[pl.BlockSpec(memory_space=pltpu.VMEM)] * len(outs),
         out_shape=[jax.ShapeDtypeStruct(*out) for out in outs],
-        scratch_shapes=[pltpu.VMEM(*item) for item in scratch]
-        + [pltpu.SemaphoreType.DMA((phases, 4)), pltpu.SemaphoreType.DMA((phases, 5))],
+        scratch_shapes=scratch,
         compiler_params=pltpu.CompilerParams(
             collective_id=number, has_side_effects=True, vmem_limit_bytes=VMEM_LIMIT
         ),
+        cost_estimate=cost(micros),
         name=name,
     )(*operands)
 
 
-def exchange_scratch(sums, block, width):
+def line_scratch(sums, block, width, phases):
     return [
-        ((sums, HALVES, 4, block, width), BF16),
-        ((sums, HALVES, 5, block, width), BF16),
-        ((block, width), F32),
+        pltpu.VMEM((sums, HALVES, 4, block, width), BF16),
+        pltpu.VMEM((sums, HALVES, 5, block, width), BF16),
+        pltpu.VMEM((block, width), F32),
+        DMA((phases, 4)),
+        DMA((phases, 5)),
+    ]
+
+
+def sums_scratch(shape):
+    pairs, _, own, width = shape
+    return [
+        pltpu.VMEM((pairs, own, width), BF16), pltpu.VMEM((pairs, own, width), BF16),
+        DMA((4,)), DMA((4,)), DMA((pairs,)), DMA((pairs,)),
     ]
 
 
 def start_call(rows, cot, gain):
     _, block, width = rows.shape
     whole = ((4, HALVES, block, width), BF16)
-    return line_call(start_kernel, (rows, cot, gain), [whole, whole], [], 4, 1, "start")
-
-
-def ffn_forward_call(mixer, w_out, w_up, w_down, rows, gain, gain_next, layer, last):
+    return line_call(start_kernel, (rows, cot, gain), [whole, whole], [DMA((4, 4)), DMA((4, 5))], 1, "start", 35)
+
+
+def ffn_forward_call(mixer, weights, rows, gain, gain_next, layer, last):
     _, block, width = rows.shape
-    wide = w_down.shape[1]
+    wide = (weights.shape[1] - mixer.shape[3]) // 3
     own, whole = ((HALVES, block, width), F32), ((4, HALVES, block, width), BF16)
     outs = [own, whole, ((4, HALVES, block, 2 * wide), F32), ((4, HALVES, block, wide), BF16), own]
     if not last:
         outs.append(whole)
     return line_call(
-        functools.partial(ffn_forward_kernel, last),
-        (mixer, w_out, w_up, w_down, rows, gain, gain_next), outs,
-        exchange_scratch(2, block, width), 8, 2 + layer, "ffn_forward",
+        functools.partial(ffn_forward_kernel, last), (mixer, weights, rows, gain, gain_next), outs,
+        line_scratch(2, block, width, 8) + ([] if last else [pltpu.SemaphoreType.REGULAR]), 2 + layer, "ffn_forward", 65,
     )
 
 
-def ffn_backward_call(cot, hidden, pre, normed, middle, grad, gain, w_down, w_up, w_out, layer):
+def ffn_backward_call(cot, hidden, pre, normed, middle, grad, gain, weights, v_width, grads_shape, layer):
     _, block, width = middle.shape
-    wide = w_down.shape[1]
+    wide = hidden.shape[3]
     whole = ((4, HALVES, block, width), BF16)
     outs = [
-        ((4, HALVES, block, w_out.shape[1]), F32), ((width, 3 * wide), BF16), whole,
+        ((4, HALVES, block, v_width), F32), (grads_shape + (3 * wide,), BF16), whole,
         ((HALVES, block, width), F32), ((1, width), F32),
     ]
-    scratch = [((4, HALVES, block, 2 * wide), BF16)] + exchange_scratch(1, block, width)
+    scratch = [pltpu.VMEM((4, HALVES, block, 2 * wide), BF16)] + line_scratch(1, block, width, 4)
     return line_call(
-        ffn_backward_kernel, (cot, hidden, pre, normed, middle, grad, gain, w_down, w_up, w_out), outs,
-        scratch, 4, 4 + layer, "ffn_backward",
+        ffn_backward_kernel, (cot, hidden, pre, normed, middle, grad, gain, weights), outs, scratch,
+        4 + layer, "ffn_backward", 40,
     )
 
 
-def mixer_backward_call(d_proj, w_in, normed, mixer, mixer_cot, rows, grad, gain, layer, last):
+def mixer_backward_call(d_proj, w_in, normed, mixer, mixer_cot, rows, grad, gain, grads_shape, layer):
     _, block, width = rows.shape
-    outs = [((HALVES, block, width), F32), ((1, width), F32)]
-    if not last:
-        outs += [((width, mixer.shape[3] + w_in.shape[1]), BF16), ((4, HALVES, block, width), BF16)]
+    outs = [
+        ((HALVES, block, width), F32), ((1, width), F32),
+        (grads_shape + (mixer.shape[3] + w_in.shape[1],), BF16), ((4, HALVES, block, width), BF16),
+    ]
     return line_call(
-        functools.partial(mixer_backward_kernel, last),
-        (d_proj, w_in, normed, mixer, mixer_cot, rows, grad, gain), outs,
-        exchange_scratch(1, block, width), 4, 6 + layer, "mixer_backward",
+        mixer_backward_kernel, (d_proj, w_in, normed, mixer, mixer_cot, rows, grad, gain), outs,
+        line_scratch(1, block, width, 4), 6 + layer, "mixer_backward", 40,
     )
+
+
+def last_call(d_proj, w_in, normed, mixer, mixer_cot, rows, grad, gain, taps, norms, grads_shape, gain_at):
+    _, block, width = rows.shape
+    dp = 2 * grads_shape[0]
+    shape = grads_shape + (mixer.shape[3] + w_in.shape[1],)
+    outs = [((HALVES, block, width), F32), (shape[2:], F32), (taps.shape, F32), (norms.shape, F32)]
+    scratch = [
+        pltpu.VMEM((1, width), F32), pltpu.VMEM(shape, BF16), pltpu.VMEM((dp,) + taps.shape, F32),
+        pltpu.VMEM((4,) + norms.shape, F32), pltpu.VMEM((dp,) + norms.shape, F32),
+        DMA((dp,)), DMA((dp,)), DMA((4,)), DMA((4,)), DMA((dp,)), DMA((dp,)),
+    ]
+    return line_call(
+        functools.partial(last_kernel, gain_at, width // 128),
+        (d_proj, w_in, normed, mixer, mixer_cot, rows, grad, gain, taps, norms), outs,
+        scratch + line_scratch(1, block, width, 2) + sums_scratch(shape), 8, "last", 40,
+    )
+
+
+def finish_kernel(places, *refs):
+    sources, outs = refs[: 2 * LAYERS], refs[2 * LAYERS : 2 * LAYERS + len(places)]
+    held, sems = refs[2 * LAYERS + len(places) : -1], refs[-1]
+    for i, (kind, width, start) in enumerate(places):
+        for l in range(LAYERS):
+            source = sources[kind * LAYERS + l]
+            held[i][l] = source[:, start : start + width].astype(F32)
+        pltpu.make_async_copy(held[i], outs[i], sems.at[i]).start()
+    for i in range(len(places)):
+        pltpu.make_async_copy(held[i], outs[i], sems.at[i]).wait()
+
+
+def finish_call(mixer_grads, ffn_grads, places):
+    operands = list(mixer_grads) + list(ffn_grads)
+    own = operands[0].shape[0]
+    shapes = [(LAYERS, own, width) for _, width, _ in places]
+    return pl.pallas_call(
+        functools.partial(finish_kernel, places),
+        in_specs=[pl.BlockSpec(memory_space=pltpu.VMEM)] * len(operands),
+        out_specs=[pl.BlockSpec(memory_space=pl.ANY)] * len(places),
+        out_shape=[jax.ShapeDtypeStruct(shape, F32) for shape in shapes],
+        scratch_shapes=[pltpu.VMEM(shape, F32) for shape in shapes] + [DMA((len(places),))],
+        compiler_params=pltpu.CompilerParams(vmem_limit_bytes=VMEM_LIMIT),
+        name="finish",
+    )(*operands)
 
 
 LAYERS = 2
@@ -838,8 +1173,21 @@
 REFINE = 1
 
 
-def over_rows(left, right):
-    return lax.dot_general(left, right, TN, preferred_element_type=F32)
+def packed(arrays):
+    flat = []
+    for array in arrays:
+        flat.append(jnp.pad(array.reshape(-1), (0, -array.size % 128)))
+    flat = jnp.concatenate(flat)
+    return jnp.pad(flat, (0, -flat.size % 1024)).reshape(-1, 128)
+
+
+def unpacked(rows, like):
+    found, start = [], 0
+    for array in like:
+        count = -(-array.size // 128)
+        found.append(rows[start : start + count].reshape(-1)[: array.size].reshape(array.shape))
+        start += count
+    return tuple(found)
 
 
 def padded(matrix, width):
@@ -890,9 +1238,7 @@
             [low(out_weight), padded(low(swiglu_gate), hidden_pad), padded(low(swiglu_up), hidden_pad),
              padded(low(swiglu_down), hidden_pad)], axis=1
         ))
-        return (
-            first, second[:, :v_width], second[:, v_width : v_width + 2 * hidden_pad], second[:, v_width + 2 * hidden_pad :]
-        )
+        return first, second
 
     def split_rows(matrix):
         return matrix.reshape(HALVES, block, matrix.shape[1])
@@ -912,15 +1258,15 @@
     normed, cot = start_call(rows, cot_rows, gain_of(0, 0))
     kept = []
     for l in range(LAYERS):
-        w_in, w_out, w_up, w_down = weights[l]
+        w_in, w_rest = weights[l]
         last = l == LAYERS - 1
         proj = jnp.dot(merged(normed), w_in, preferred_element_type=F32)
         small = (conv_query_key[l], conv_value[l], head_params[l], out_gain[l][None])
         mixer, *saved = delta_forward(proj, *small, tables, seqs, heads, CHUNK, REFINE)
         mixer = split_all(mixer)
-        following = gain_of(min(l + 1, LAYERS - 1), 0)
+        gain_next = gain_of(min(l + 1, LAYERS - 1), 0)
         middle, normed_ffn, pre, hidden, out_rows, *following = ffn_forward_call(
-            mixer, w_out, w_up, w_down, rows, gain_of(l, 1), following, l, last
+            mixer, w_rest, rows, gain_of(l, 1), gain_next, l, last
         )
         kept.append((rows, normed, proj, small, mixer, saved, middle, normed_ffn, pre, hidden))
         rows = out_rows
@@ -928,50 +1274,47 @@
             normed = following[0]
     output = rows.reshape(local_rows, width)
     grad = cot_rows
+    dp = lax.axis_size("dp")
+    grads_shape = (dp // 2, 2, width // dp)
     ffn_grads, mixer_grads, tap_grads, norm_grads, gain_grads = ([None] * LAYERS for _ in range(5))
     for l in reversed(range(LAYERS)):
-        w_in, w_out, w_up, w_down = weights[l]
+        w_in, w_rest = weights[l]
         rows, normed, proj, small, mixer, saved, middle, normed_ffn, pre, hidden = kept[l]
-        last = l == 0
+        if l < LAYERS - 1:
+            cot, ffn_grads[l + 1] = lax.optimization_barrier((cot, ffn_grads[l + 1]))
         d_mixer, ffn_grad, mixer_cot, grad, second_gain = ffn_backward_call(
-            cot, hidden, pre, normed_ffn, middle, grad, gain_of(l, 1), w_down, w_up, w_out, l
+            cot, hidden, pre, normed_ffn, middle, grad, gain_of(l, 1), w_rest, v_width, grads_shape, l
         )
-        ffn_grads[l] = reduced(ffn_grad)
+        ffn_grads[l] = reduced(ffn_grad.reshape(width, 3 * hidden_pad))
         d_proj, d_qk, d_v, d_head, d_gain = delta_backward(
             proj, *small, tables, saved, merged(d_mixer), seqs, heads, CHUNK
         )
-        if last:
-            mixer_grad = jnp.concatenate(
-                [over_rows(merged(mixer_cot), merged(mixer)), over_rows(merged(normed), d_proj)], axis=1
-            ).astype(BF16)
-            mixer_grads[l] = reduced(mixer_grad)
-        grad, first_gain, *others = mixer_backward_call(
-            split_all(d_proj), w_in, normed, mixer, mixer_cot, rows, grad, gain_of(l, 0), l, last
-        )
-        if not last:
-            mixer_grads[l] = reduced(others[0])
-            cot = others[1]
         tap_grads[l] = (d_qk.sum(0), d_v.sum(0), d_head.sum(0)[:, :2, 0].T)
-        norm_grads[l] = jnp.concatenate([first_gain, second_gain], axis=0)
         gain_grads[l] = d_gain.sum((0, 1, 2))
-
-    def columns(parts, start, size):
-        return jnp.stack([part[:, start : start + size] for part in parts]).astype(F32)
-
-    start = v_width
-    in_grads = []
-    for size in (qk_width, qk_width, v_width, v_width, pair_width):
-        in_grads.append(columns(mixer_grads, start, size))
-        start += size
-    out_grad = columns(mixer_grads, 0, v_width)
-    down_grad = columns(ffn_grads, 0, hidden_width)
-    gate_grad = columns(ffn_grads, hidden_pad, hidden_width)
-    up_grad = columns(ffn_grads, 2 * hidden_pad, hidden_width)
+        d_proj = split_all(d_proj)
+        if l > 0:
+            grad, first_gain, mixer_grad, cot = mixer_backward_call(
+                d_proj, w_in, normed, mixer, mixer_cot, rows, grad, gain_of(l, 0), grads_shape, l
+            )
+            mixer_grads[l] = reduced(mixer_grad.reshape(width, mixer_grad.shape[3]))
+            norm_grads[l] = jnp.concatenate([first_gain, second_gain], axis=0)
+    norm_grads[0] = jnp.concatenate([jnp.zeros_like(second_gain), second_gain], axis=0)
     taps = tuple(jnp.stack([tap_grads[l][i] for l in range(LAYERS)]) for i in range(3))
-    taps = lax.psum(taps, "dp")
-    norms = lax.psum((jnp.stack(norm_grads), jnp.stack(gain_grads)), ("dp", "tensor"))
+    norms = (jnp.stack(norm_grads), jnp.stack(gain_grads))
+    d_proj, mixer_grads[1] = lax.optimization_barrier((d_proj, mixer_grads[1]))
+    grad, mixer_grads[0], *small_sums = last_call(
+        d_proj, w_in, normed, mixer, mixer_cot, rows, grad, gain_of(0, 0), packed(taps), packed(norms), grads_shape, 0
+    )
+    taps, norms = unpacked(small_sums[0], taps), unpacked(small_sums[1], norms)
+
+    weight_grads = finish_call(
+        mixer_grads, ffn_grads,
+        [(0, qk_width, v_width), (0, qk_width, v_width + qk_width), (0, v_width, v_width + 2 * qk_width),
+         (0, v_width, 2 * v_width + 2 * qk_width), (0, pair_width, 3 * v_width + 2 * qk_width), (0, v_width, 0),
+         (1, hidden_width, hidden_pad), (1, hidden_width, 2 * hidden_pad), (1, hidden_width, 0)],
+    )
     return (
-        output, grad.reshape(local_rows, width), *in_grads, out_grad, gate_grad, up_grad, down_grad, *taps, *norms
+        output, grad.reshape(local_rows, width), *weight_grads, *taps, *norms
     )
 
 

time: 659 us -> 514 us (0.78)
  blocking collectives: 63.1 us -> 0 us
  waiting for transfers between devices: 76 us -> 14.8 us
  local copies, waits for them, and re-layouts: 45.2 us -> 31 us
    psum x2 -> x0, blocking collectives: 63.1 us -> none  [the longest x1 37.9 us: body(): lax.psum((jnp.stack(norm_grads), jnp.stack(gain_grads)), ('dp', 'tensor'))]
    reduce_scatter x4 -> x3, waiting for transfers between devices: 65.5 us -> 8.71 us  [reduced(): return lax.psum_scatter(matrix, 'dp', scatter_dimension=0, tiled=True)]
    slice x6 -> x4, local copies, waits for them, and re-layouts: 17.5 us -> 2.83 us  [unpacked(): rows[start:start + count].reshape(-1)[:array.size].reshape(array.shape)]
    pallas_call x7, Pallas kernels: 350 us -> 336 us  [line_call(): pl.pallas_call(kernel, in_specs=[pl.BlockSpec(memory_space=pltpu.VMEM)] *...]
    unnamed x112 -> x103, local copies, waits for them, and re-layouts: 18.2 us -> 20.8 us
  transfers between devices with their start and end apart: 8 -> 7, of which waited for: 3 -> 3; matrix products, arithmetic and copies ran while one was open for 7% -> 6% of each run, Pallas kernels for 37% -> 64%
where the time goes in v3:
time: 514 us; the launch traced here: 504 us
  Pallas kernels  421 us (82%)
  local copies, waits for them, and re-layouts  31 us (6%)
  between operations  15.1 us (3%)
  waiting for transfers between devices  14.8 us (3%)
  matrix products  12.2 us (2%)
  other arithmetic  9.59 us (2%)
    pallas_call x7, Pallas kernels, line_call(): pl.pallas_call(kernel, in_specs=[pl.BlockSpec(memory_space=pltpu.VMEM)] *...  336 us
    pallas_call x2, Pallas kernels, delta_backward(): pl.pallas_call(functools.partial(backward_kernel, chunk, heads), grid=(se...  50.3 us
    pallas_call x2, Pallas kernels, delta_forward(): pl.pallas_call(functools.partial(forward_kernel, chunk, refine), grid=(se...  30.6 us
    unnamed x103, local copies, waits for them, and re-layouts  20.8 us
    dot_general x2, matrix products, body(): proj = jnp.dot(merged(normed), w_in, preferred_element_type=F32)  12.2 us
  transfers between devices with their start and end apart: 7, of which 3 were waited for; matrix products, arithmetic and copies ran while one was open for 6% of the time, Pallas kernels for 64%

profile of v3, /device:TPU:0, one launch (start us, length us, event | category | flops | bytes accessed | tf_op | source)
XLA Modules:
  0.0 503.9 jit_solution(10987678247451509245)
XLA Ops:
  8.1 1.0 convert.41
  9.1 1.0 convert.42
  10.1 1.1 convert.43
  12.2 1.1 convert.46
  14.0 0.9 fusion.10
  19.4 42.5 %start.1 = (bf16[4,2,64,1024]{3,2,1,0:T(8,128)(2,1)}, bf16[4,2,64,1024]{3,2,1,0:T(8,128)(2,1)}) custom-call(bf16[2,64,1024]{2,1,0:T(8,128)(2,1)} %bitcast.147, bf16[2,64,1024]{2,1,0:T(8,128)(2,1)} %bitcast.155, f32[1,1024]{1,0:T(1,128)} %get-tuple-element.214.gain), custom_call_target="tpu_custom_call" | custom-call | bytes 122500000 | tf_op jit(solution)/shard_map/start/pallas_call | solution.py:1049
  62.2 6.1 %fusion.30.qref.kref.vref.gref.pair_ref = f32[512,1664]{1,0:T(8,128)} fusion(bf16[512,1024]{1,0:T(8,128)(2,1)} %bitcast.152, bf16[1024,1664]{1,0:T(8,128)(2,1)} %all-gather.5.cloned.1.call-done.w_in), kind=kOutput, calls=%fused_computation.91 | convolution fusion | flops 1744830464 | bytes 7864320 | tf_op jit(solution)/shard_map/dot_general | solution.py:1263
  68.4 15.3 %delta_forward.2 = (bf16[512,512]{1,0:T(8,128)(2,1)S(1)}, f32[512,512]{1,0:T(8,128)S(1)}, f32[512,512]{1,0:T(8,128)S(1)}, f32[1,2,4,128,128]{4,3,2,1,0:T(8,128)S(1)}, f32[1,2,4,128,256]{4,3,2,1,0:T(8,128)S(1)}) custom-call(f32[512,1664]{1,0:T(8,128)} %fusion.30.qref.kref.vref.gref.pair_ref, f32[512,1664]{1,0:T(8,128)} %fusion.30.qref.kref.vref.gref.pair_ref, ...), custom_call_target="tpu_custom_call" | custom-call | bytes 52500000 | tf_op jit(solution)/shard_map/delta_forward/pallas_call | solution.py:374
  84.5 1.0 copy-done.3
  85.5 1.0 copy-done.4
  86.4 1.0 copy-done.5
  88.2 5.9 %all-gather.7.cloned.1.call-done.weights = bf16[1024,2816]{1,0:T(8,128)(2,1)} async-done(((bf16[128,2816]{1,0:T(8,128)(2,1)}), bf16[1024,2816]{1,0:T(8,128)(2,1)}) %all-gather.7.cloned.1.call-update) | async-done | bytes 5767184 | tf_op jit(solution)/shard_map/all_gather | solution.py:1227
  94.2 65.3 %ffn_forward.2 = (f32[2,64,1024]{2,1,0:T(8,128)}, bf16[4,2,64,1024]{3,2,1,0:T(8,128)(2,1)}, f32[4,2,64,1536]{3,2,1,0:T(8,128)}, bf16[4,2,64,768]{3,2,1,0:T(8,128...) custom-call(bf16[4,2,64,512]{3,2,1,0:T(8,128)(2,1)} %bitcast.140, ...), custom_call_target="tpu_custom_call" | custom-call | bytes 227500000 | tf_op jit(solution)/shard_map/ffn_forward/pallas_call | solution.py:1049
  159.5 6.1 %fusion.31.qref.kref.vref.gref.pair_ref = f32[512,1664]{1,0:T(8,128)} fusion(bf16[512,1024]{1,0:T(8,128)(2,1)} %bitcast.157, bf16[1024,1664]{1,0:T(8,128)(2,1)} %all-gather.9.cloned.1.call-done.w_in), kind=kOutput, calls=%fused_computation.92 | convolution fusion | flops 1744830464 | bytes 7864320 | tf_op jit(solution)/shard_map/dot_general | solution.py:1263
  165.6 15.3 %delta_forward.3 = (bf16[512,512]{1,0:T(8,128)(2,1)S(1)}, f32[512,512]{1,0:T(8,128)S(1)}, f32[512,512]{1,0:T(8,128)S(1)}, f32[1,2,4,128,128]{4,3,2,1,0:T(8,128)S(1)}, f32[1,2,4,128,256]{4,3,2,1,0:T(8,128)S(1)}) custom-call(f32[512,1664]{1,0:T(8,128)} %fusion.31.qref.kref.vref.gref.pair_ref, f32[512,1664]{1,0:T(8,128)} %fusion.31.qref.kref.vref.gref.pair_ref, ...), custom_call_target="tpu_custom_call" | custom-call | bytes 52500000 | tf_op jit(solution)/shard_map/delta_forward/pallas_call | solution.py:374
  181.7 1.0 copy-done.6
  182.7 1.0 copy-done.7
  183.7 1.0 copy-done.8
  185.5 57.2 %ffn_forward.3 = (f32[2,64,1024]{2,1,0:T(8,128)}, bf16[4,2,64,1024]{3,2,1,0:T(8,128)(2,1)}, f32[4,2,64,1536]{3,2,1,0:T(8,128)}, bf16[4,2,64,768]{3,2,1,0:T(8,128)(2,1)}, f32[2,64,1024]{2,1,0:T(8,128)}) custom-call(bf16[4,2,64,512]{3,2,1,0:T(8,128)(2,1)} %bitcast.142, bf16[1024,2816]{1,0:T(8,128)(2,1)} %all-gather.11.cloned.1.call-done.weights, ...), custom_call_target="tpu_custom_call" | custom-call | bytes 227500000 | tf_op jit(solution)/shard_map/ffn_forward/pallas_call | solution.py:1049
  242.7 35.7 %ffn_backward.2 = (f32[4,2,64,512]{3,2,1,0:T(8,128)}, bf16[4,2,128,2304]{3,2,1,0:T(8,128)(2,1)}, bf16[4,2,64,1024]{3,2,1,0:T(8,128)(2,1)}, f32[2,64,1024]{2,1,0:T(8,128)}, f32[1,1024]{1,0:T(1,128)}) custom-call(bf16[4,2,64,1024]{3,2,1,0:T(8,128)(2,1)} %get-tuple-element.94.cot, bf16[4,2,64,768]{3,2,1,0:T(8,128)(2,1)} %get-tuple-element.95.hidden, ...), custom_call_target="tpu_custom_call" | custom-call | bytes 140000000 | tf_op jit(solution)/shard_map/ffn_backward/pallas_call | solution.py:1049
  278.5 25.1 %delta_backward.2 = (bf16[512,1664]{1,0:T(8,128)(2,1)}, f32[1,2,4,256]{3,2,1,0:T(4,128)}, f32[1,4,512]{2,1,0:T(4,128)}, f32[1,2,8,128]{3,2,1,0:T(8,128)}, f32[1,2,1,256]{3,2,1,0:T(1,128)}) custom-call(f32[512,1664]{1,0:T(8,128)} %fusion.31.qref.kref.vref.gref.pair_ref, f32[512,1664]{1,0:T(8,128)} %fusion.31.qref.kref.vref.gref.pair_ref, ...), custom_call_target="tpu_custom_call" | custom-call | bytes 87500000 | tf_op jit(solution)/shard_map/delta_backward/pallas_call | solution.py:404
  303.6 37.1 %mixer_backward.1 = (f32[2,64,1024]{2,1,0:T(8,128)}, f32[1,1024]{1,0:T(1,128)}, bf16[4,2,128,2176]{3,2,1,0:T(8,128)(2,1)}, bf16[4,2,64,1024]{3,2,1,0:T(8,128)(2,1)}) custom-call(bf16[4,2,64,1664]{3,2,1,0:T(8,128)(2,1)} %bitcast.151, bf16[1024,1664]{1,0:T(8,128)(2,1)} %all-gather.9.cloned.1.call-done.w_in, bf16[4,2,64,1024]{3,2,1,0:T(8,128)(2,1)} %get-tuple-element.82.normed, ...), custom_call_target="tpu_custom_call" | custom-call | bytes 140000000 | tf_op jit(solution)/shard_map/mixer_backward/pallas_call | solution.py:1049
  340.9 7.6 %reduce-scatter.4.cloned.1.call-done.refs_3_ = bf16[128,2304]{1,0:T(8,128)(2,1)} async-done(((bf16[1024,2304]{1,0:T(8,128)(2,1)}), bf16[128,2304]{1,0:T(8,128)(2,1)}) %reduce-scatter.4.cloned.1.call-update) | async-done | bytes 589840 | tf_op jit(solution)/shard_map/reduce_scatter | solution.py:1230
  348.4 46.7 %ffn_backward.3 = (f32[4,2,64,512]{3,2,1,0:T(8,128)}, bf16[4,2,128,2304]{3,2,1,0:T(8,128)(2,1)}, bf16[4,2,64,1024]{3,2,1,0:T(8,128)(2,1)}, f32[2,64,1024]{2,1,0:T(8,128)}, f32[1,1024]{1,0:T(1,128)}) custom-call(bf16[4,2,64,1024]{3,2,1,0:T(8,128)(2,1)} %get-tuple-element.105.cot, bf16[4,2,64,768]{3,2,1,0:T(8,128)(2,1)} %get-tuple-element.106.hidden, ...), custom_call_target="tpu_custom_call" | custom-call | bytes 140000000 | tf_op jit(solution)/shard_map/ffn_backward/pallas_call | solution.py:1049
  396.8 25.2 %delta_backward.3 = (bf16[512,1664]{1,0:T(8,128)(2,1)}, f32[1,2,4,256]{3,2,1,0:T(4,128)}, f32[1,4,512]{2,1,0:T(4,128)}, f32[1,2,8,128]{3,2,1,0:T(8,128)}, f32[1,2,1,256]{3,2,1,0:T(1,128)}) custom-call(f32[512,1664]{1,0:T(8,128)} %fusion.30.qref.kref.vref.gref.pair_ref, f32[512,1664]{1,0:T(8,128)} %fusion.30.qref.kref.vref.gref.pair_ref, ...), custom_call_target="tpu_custom_call" | custom-call | bytes 87500000 | tf_op jit(solution)/shard_map/delta_backward/pallas_call | solution.py:404
  426.5 51.5 %last.1 = (f32[2,64,1024]{2,1,0:T(8,128)}, f32[128,2176]{1,0:T(8,128)}, f32[72,128]{1,0:T(8,128)}, f32[40,128]{1,0:T(8,128)}) custom-call(bf16[4,2,64,1664]{3,2,1,0:T(8,128)(2,1)} %bitcast.150, bf16[1024,1664]{1,0:T(8,128)(2,1)} %all-gather.5.cloned.1.call-done.w_in, bf16[4,2,64,1024]{3,2,1,0:T(8,128)(2,1)} %get-tuple-element.80.normed, ...), custom_call_target="tpu_custom_call" | custom-call | bytes 140000000 | tf_op jit(solution)/shard_map/last/pallas_call | solution.py:1049
  483.9 1.1 reduce-scatter.8.cloned.1.call-done.refs_2_
  485.0 4.0 finish.1
  489.0 1.6 copy.70
  490.6 2.3 copy.71
  493.0 1.1 copy.72
  494.1 1.1 copy.73
  (163 shorter events, 23.8 us)
Async XLA Ops:
  7.2 4.0 copy-start.27
  7.2 55.0 %all-gather.5.cloned.1.call-start = ((), (), s32[]{:S(2)}) async-start(), calls=%async_computation.3 | async-start | bytes 3833856 | tf_op jit(solution)/shard_map/all_gather | solution.py:1227
  11.2 2.1 copy-start.22
  11.3 2.2 copy-start.23
  12.1 82.1 %all-gather.7.cloned.1.call-start = ((), (), s32[]{:S(2)}) async-start(), calls=%async_computation.4 | async-start | bytes 6488064 | tf_op jit(solution)/shard_map/all_gather | solution.py:1227
  14.9 2.0 copy-start.30
  14.9 144.5 %all-gather.9.cloned.1.call-start = ((), (), s32[]{:S(2)}) async-start(), calls=%async_computation.5 | async-start | bytes 3833856 | tf_op jit(solution)/shard_map/all_gather | solution.py:1227
  15.0 3.7 copy-start.31
  15.8 169.7 %all-gather.11.cloned.1.call-start = ((), (), s32[]{:S(2)}) async-start(), calls=%async_computation.6 | async-start | bytes 6488064 | tf_op jit(solution)/shard_map/all_gather | solution.py:1227
  15.9 46.1 %copy-start.40 = (f32[2,2,2]{2,1,0:T(2,128)S(1)}, f32[2,2,2]{2,1,0:T(2,128)}, u32[]{:S(2)}) copy-start(f32[2,2,2]{2,1,0:T(2,128)} %param.30) | copy-start | bytes 100
  15.9 46.1 %copy-start.41 = (f32[2,256]{1,0:T(2,128)S(1)}, f32[2,256]{1,0:T(2,128)}, u32[]{:S(2)}) copy-start(f32[2,256]{1,0:T(2,128)} %param.32) | copy-start | bytes 6148
  15.9 46.2 %copy-start.32 = (f32[2,2,4,256]{3,2,1,0:T(4,128)S(1)}, f32[2,2,4,256]{3,2,1,0:T(4,128)}, u32[]{:S(2)}) copy-start(f32[2,2,4,256]{3,2,1,0:T(4,128)} %param.28) | copy-start | bytes 49156
  15.9 46.2 %copy-start.33 = (f32[2,4,512]{2,1,0:T(4,128)S(1)}, f32[2,4,512]{2,1,0:T(4,128)}, u32[]{:S(2)}) copy-start(f32[2,4,512]{2,1,0:T(4,128)} %param.29) | copy-start | bytes 49156
  16.8 331.6 %reduce-scatter.4.cloned.1.call-start = ((), (), s32[]{:S(2)}) async-start(), calls=%async_computation.7 | async-start | bytes 5308416 | tf_op jit(solution)/shard_map/reduce_scatter | solution.py:1230
  18.7 146.8 %copy-start = (f32[1,512,8]{2,1,0:T(8,128)}, f32[1,512,8]{2,1,0:T(8,128)S(1)}, u32[]{:S(2)}) copy-start(f32[1,512,8]{2,1,0:T(8,128)S(1)} %copy.61.col_ref) | copy-start | bytes 49156
  62.0 103.6 %copy-start.11 = (f32[1,8,512]{2,1,0:T(8,128)}, f32[1,8,512]{2,1,0:T(8,128)S(1)}, u32[]{:S(2)}) copy-start(f32[1,8,512]{2,1,0:T(8,128)S(1)} %stack.100.row_ref) | copy-start | bytes 49156
  62.0 6.3 %copy-start.16 = (f32[2,2]{1,0:T(2,128)}, f32[2,2]{1,0:T(2,128)S(1)}, u32[]{:S(2)}) copy-start(f32[2,2]{1,0:T(2,128)S(1)} %get-tuple-element.223.head_table) | copy-start | bytes 52
  62.0 103.5 %copy-start.18 = (f32[2,2]{1,0:T(2,128)}, f32[2,2]{1,0:T(2,128)S(1)}, u32[]{:S(2)}) copy-start(f32[2,2]{1,0:T(2,128)S(1)} %get-tuple-element.222.head_table) | copy-start | bytes 52
  62.1 6.3 %copy-start.17 = (f32[1,256]{1,0:T(1,128)}, f32[1,256]{1,0:T(1,128)S(1)}, u32[]{:S(2)}) copy-start(f32[1,256]{1,0:T(1,128)S(1)} %get-tuple-element.221.gain) | copy-start | bytes 3076
  62.1 103.5 %copy-start.19 = (f32[1,256]{1,0:T(1,128)}, f32[1,256]{1,0:T(1,128)S(1)}, u32[]{:S(2)}) copy-start(f32[1,256]{1,0:T(1,128)S(1)} %get-tuple-element.220.gain) | copy-start | bytes 3076
  62.1 6.2 %copy-start.12 = (f32[2,4,256]{2,1,0:T(4,128)}, f32[2,4,256]{2,1,0:T(4,128)S(1)}, u32[]{:S(2)}) copy-start(f32[2,4,256]{2,1,0:T(4,128)S(1)} %get-tuple-element.219.tap_qk) | copy-start | bytes 24580
  62.1 103.5 %copy-start.14 = (f32[2,4,256]{2,1,0:T(4,128)}, f32[2,4,256]{2,1,0:T(4,128)S(1)}, u32[]{:S(2)}) copy-start(f32[2,4,256]{2,1,0:T(4,128)S(1)} %get-tuple-element.218.tap_qk) | copy-start | bytes 24580
  62.1 6.2 %copy-start.13 = (f32[4,512]{1,0:T(4,128)}, f32[4,512]{1,0:T(4,128)S(1)}, u32[]{:S(2)}) copy-start(f32[4,512]{1,0:T(4,128)S(1)} %get-tuple-element.217.tap_v) | copy-start | bytes 24580
  62.2 103.4 %copy-start.15 = (f32[4,512]{1,0:T(4,128)}, f32[4,512]{1,0:T(4,128)S(1)}, u32[]{:S(2)}) copy-start(f32[4,512]{1,0:T(4,128)S(1)} %get-tuple-element.216.tap_v) | copy-start | bytes 24580
  278.5 143.5 %reduce-scatter.6.cloned.1.call-start = ((), (), s32[]{:S(2)}) async-start(), calls=%async_computation.8 | async-start | bytes 5013504 | tf_op jit(solution)/shard_map/reduce_scatter | solution.py:1230
  340.8 144.2 %reduce-scatter.8.cloned.1.call-start = ((), (), s32[]{:S(2)}) async-start(), calls=%async_computation.9 | async-start | bytes 5308416 | tf_op jit(solution)/shard_map/reduce_scatter | solution.py:1230
  396.8 26.9 %copy-start.35 = (f32[1,2,4,256]{3,2,1,0:T(4,128)S(1)}, f32[1,2,4,256]{3,2,1,0:T(4,128)}, u32[]{:S(2)}) copy-start(f32[1,2,4,256]{3,2,1,0:T(4,128)} %get-tuple-element.118) | copy-start | bytes 24580
  396.8 27.6 %copy-start.34 = (f32[1,4,512]{2,1,0:T(4,128)S(1)}, f32[1,4,512]{2,1,0:T(4,128)}, u32[]{:S(2)}) copy-start(f32[1,4,512]{2,1,0:T(4,128)} %get-tuple-element.120) | copy-start | bytes 24580
  396.8 28.4 %copy-start.36 = (f32[1,1024]{1,0:T(1,128)S(1)}, f32[1,1024]{1,0:T(1,128)}, u32[]{:S(2)}) copy-start(f32[1,1024]{1,0:T(1,128)} %get-tuple-element.123) | copy-start | bytes 12292
  489.0 4.0 copy-start.21
  490.6 3.5 copy-start.20
  493.0 2.3 copy-start.28
  (17 other events, 18.0 us)
Sparse Core Ops, SparseCore 0:
  12.2 36.1 all-gather.4
  50.8 43.3 all-gather.6
  96.7 33.4 all-gather.8
  132.4 43.3 all-gather.10
  278.6 69.7 reduce-scatter.3
  352.1 54.1 reduce-scatter.5
  409.8 75.1 reduce-scatter.7

commit v4 on v3

--- a/solution.py
+++ b/solution.py
@@ -77,12 +77,12 @@
     block = 2
     while block < size:
         mask = off(block)
-        half = [mm(x, part * mask, NN) for x, part in zip(found, lower)]
-        found = [x - mm(t, x, NN) for x, t in zip(found, half)]
+        half = [mm(x, part * mask, NN, 1) for x, part in zip(found, lower)]
+        found = [x - mm(t, x, NN, 1) for x, t in zip(found, half)]
         block *= 2
     for _ in range(refine):
         rest = [(x - eye) + mm(part, x, NN) for x, part in zip(found, lower)]
-        found = [x - mm(x, r, NN) for x, r in zip(found, rest)]
+        found = [x - mm(x, r, NN, 1) for x, r in zip(found, rest)]
     return found
 
 
@@ -382,10 +382,10 @@
         ],
         out_shape=[
             jax.ShapeDtypeStruct((tokens, heads * dv), BF16),
-            jax.ShapeDtypeStruct((tokens, heads * dv), F32),
-            jax.ShapeDtypeStruct((tokens, heads * dv), F32),
-            jax.ShapeDtypeStruct((seqs, heads, chunks, chunk, chunk), F32),
-            jax.ShapeDtypeStruct((seqs, heads, chunks, dk, dv), F32),
+            pltpu.HBM((tokens, heads * dv), F32),
+            pltpu.HBM((tokens, heads * dv), F32),
+            pltpu.HBM((seqs, heads, chunks, chunk, chunk), F32),
+            pltpu.HBM((seqs, heads, chunks, dk, dv), F32),
         ],
         compiler_params=pltpu.CompilerParams(vmem_limit_bytes=48 * 2**20),
         cost_estimate=cost(15),
@@ -434,6 +434,7 @@
 MESH = pl.DeviceIdType.MESH
 VMEM_LIMIT = 58 * 2**20
 HALVES = 2
+LAYERS = 2
 
 
 class Line:
@@ -594,6 +595,41 @@
         lax.fori_loop(1, self.pairs, signal, 0)
         return self.pairs
 
+    def greet_late(self, gate):
+        self.gate = gate
+        barrier = pltpu.get_barrier_semaphore()
+        sibling = 2 * self.mine + 1 - self.parity
+
+        @pl.when(self.parity == 0)
+        def _():
+            pl.semaphore_signal(barrier, inc=1, device_id={"dp": sibling}, device_id_type=MESH)
+
+        def signal(i, carry):
+            other = 2 * lax.rem(self.mine + i, self.pairs) + self.parity
+            pl.semaphore_signal(barrier, inc=1, device_id={"dp": other}, device_id_type=MESH)
+            return carry
+
+        lax.fori_loop(1, self.pairs, signal, 0)
+
+    def meet_late(self, line):
+        @pl.when(self.parity == 0)
+        def _():
+            line.meet(self.pairs - 1)
+
+        @pl.when(self.parity == 1)
+        def _():
+            line.meet(self.pairs)
+            pl.semaphore_signal(self.gate, inc=1, device_id={"dp": 2 * self.mine}, device_id_type=MESH)
+            for m in range(4):
+                self.start(m)
+
+    def start_late(self):
+        @pl.when(self.parity == 0)
+        def _():
+            pl.semaphore_wait(self.gate, 1)
+            for m in range(4):
+                self.start(m)
+
     def near_copy(self, m):
         span = pl.ds(m * self.group, self.group)
         return pltpu.make_async_remote_copy(
@@ -671,6 +707,67 @@
         lax.fori_loop(1, self.pairs, sent, 0)
         for m in range(4):
             self.near_copy(m).wait_send()
+
+
+class Spread:
+    def __init__(self, whole, far_send, far_recv, near_send, near_recv):
+        self.whole = whole
+        self.far_send, self.far_recv, self.near_send, self.near_recv = far_send, far_recv, near_send, near_recv
+        self.pairs = whole.shape[0] // 2
+        self.me = lax.axis_index("dp")
+        self.parity, self.mine = lax.rem(self.me, 2), lax.div(self.me, 2)
+
+    def greet(self):
+        barrier = pltpu.get_barrier_semaphore()
+        sibling = self.me + 1 - 2 * self.parity
+        pl.semaphore_signal(barrier, inc=1, device_id={"dp": sibling}, device_id_type=MESH)
+
+        def signal(i, carry):
+            other = 2 * lax.rem(self.mine + i, self.pairs) + self.parity
+            pl.semaphore_signal(barrier, inc=1, device_id={"dp": other}, device_id_type=MESH)
+            return carry
+
+        lax.fori_loop(1, self.pairs, signal, 0)
+        return self.pairs
+
+    def far_copy(self, block, to, slot):
+        return pltpu.make_async_remote_copy(
+            src_ref=self.whole.at[block], dst_ref=self.whole.at[block], send_sem=self.far_send.at[to],
+            recv_sem=self.far_recv.at[slot], device_id={"dp": 2 * to + self.parity}, device_id_type=MESH,
+        )
+
+    def near_copy(self, j, parity):
+        block = 2 * j + parity
+        return pltpu.make_async_remote_copy(
+            src_ref=self.whole.at[block], dst_ref=self.whole.at[block], send_sem=self.near_send.at[j],
+            recv_sem=self.near_recv.at[j], device_id={"dp": self.me + 1 - 2 * self.parity}, device_id_type=MESH,
+        )
+
+    def over_others(self, step):
+        def run(i, carry):
+            step(lax.rem(self.mine + i, self.pairs))
+            return carry
+
+        lax.fori_loop(1, self.pairs, run, 0)
+
+    def start(self):
+        self.over_others(lambda j: self.far_copy(self.me, j, self.mine).start())
+        self.near_copy(self.mine, self.parity).start()
+
+    def forward(self):
+        def step(j):
+            self.far_copy(2 * j + self.parity, j, j).wait_recv()
+            self.near_copy(j, self.parity).start()
+
+        self.over_others(step)
+
+    def finish(self):
+        other = 1 - self.parity
+        self.over_others(lambda j: self.near_copy(j, other).wait_recv())
+        self.near_copy(self.mine, other).wait_recv()
+        self.over_others(lambda j: self.far_copy(self.me, j, self.mine).wait_send())
+        self.over_others(lambda j: self.near_copy(j, self.parity).wait_send())
+        self.near_copy(self.mine, self.parity).wait_send()
 
 
 class Smalls:
@@ -793,22 +890,107 @@
     return back, jnp.sum(value * scale * grad, axis=0, keepdims=True)
 
 
-def start_kernel(rows, cot, gain, normed, cot_all, send_sem, recv_sem):
+def is_turned(shape):
+    return shape[1] % 128 == 0 and shape[2] % 128 != 0
+
+
+def turn(array):
+    return jnp.swapaxes(array, 1, 2) if is_turned(array.shape) else array
+
+
+def fetch_start(sources, held, sems, l):
+    for i, source in enumerate(sources):
+        pltpu.make_async_copy(source.at[l], held[i], sems.at[i]).start()
+
+
+def cast_into(out, sources, held, sems, l, places):
+    start = 0
+    for i, (turned, width, padded) in enumerate(places):
+        pltpu.make_async_copy(sources[i].at[l], held[i], sems.at[i]).wait()
+        value = held[i][...]
+        if turned:
+            tall = -(-width // 128) * 128
+            if tall > width:
+                value = jnp.concatenate([value, jnp.zeros((tall - width, value.shape[1]), F32)], axis=0)
+            value = jnp.transpose(value)
+            width = tall
+        out[:, start : start + width] = value.astype(BF16)
+        if padded > width:
+            out[:, start + width : start + padded] = jnp.zeros((value.shape[0], padded - width), BF16)
+        start += padded
+
+
+def cast_places(weights, units):
+    return [(is_turned(w.shape), w.shape[2], -(-w.shape[2] // u) * u) for w, u in zip(weights, units)]
+
+
+def cast_scratch(weights):
+    return [pltpu.VMEM(held_shape(w), F32) for w in weights] + [DMA((len(weights),))]
+
+
+def held_shape(w):
+    _, own, width = w.shape
+    return (width, own) if is_turned(w.shape) else (own, width)
+
+
+def cast_kernel(l, places, *refs):
+    count = len(places)
+    sources, out, held, sems = refs[:count], refs[count], refs[count + 1 : -1], refs[-1]
+    fetch_start(sources, held, sems, l)
+    cast_into(out, sources, held, sems, l, places)
+
+
+def cast_call(weights, units, l):
+    places = cast_places(weights, units)
+    return pl.pallas_call(
+        functools.partial(cast_kernel, l, places),
+        in_specs=[pl.BlockSpec(memory_space=pl.ANY)] * len(weights),
+        out_specs=pl.BlockSpec(memory_space=pltpu.VMEM),
+        out_shape=jax.ShapeDtypeStruct((weights[0].shape[1], sum(p[2] for p in places)), BF16),
+        scratch_shapes=cast_scratch(weights),
+        compiler_params=pltpu.CompilerParams(vmem_limit_bytes=VMEM_LIMIT),
+        cost_estimate=cost(2),
+        name="cast",
+    )(*[turn(w) for w in weights])
+
+
+def start_kernel(in_places, rest_places, rows, cot, gain, *refs):
+    first, second = len(in_places), len(rest_places)
+    sources, refs = refs[: first + second], refs[first + second :]
+    (normed, cot_all, w_in), refs = refs[:3], refs[3:]
+    low, refs = refs[: 2 * (LAYERS - 1)], refs[2 * (LAYERS - 1) :]
+    held, (in_sems, rest_sems, send_sem, recv_sem, *spread_sems) = refs[: first + second], refs[first + second :]
+    in_refs = sources[:first], held[:first], in_sems
+    rest_refs = sources[first:], held[first:], rest_sems
     line = Line(send_sem, recv_sem)
+    spread = Spread(w_in, *spread_sems)
+    fetch_start(*in_refs, 0)
     line.greet()
+    others = spread.greet()
+    cast_into(w_in.at[spread.me], *in_refs, 0, in_places)
     for h in range(HALVES):
         normed[line.me, h] = rms(rows[h].astype(F32), gain[...]).astype(BF16)
         cot_all[line.me, h] = cot[h]
-    line.meet()
+    line.meet(others)
+    spread.start()
     both = [(k + h, blocks_of(ref, h)) for k, ref in ((0, normed), (2, cot_all)) for h in range(HALVES)]
     for item in both:
         line.gather_start(*item)
-    for item in both:
+    for l in range(1, LAYERS):
+        fetch_start(*in_refs, l)
+        fetch_start(*rest_refs, l)
+        cast_into(low[2 * l - 2], *in_refs, l, in_places)
+        cast_into(low[2 * l - 1], *rest_refs, l, rest_places)
+    for item in both[:2]:
+        line.gather_forward(*item)
+    spread.forward()
+    for item in both[2:]:
         line.gather_forward(*item)
     for item in both:
         line.gather_wait(*item)
     for item in both:
         line.gather_drain(*item)
+    spread.finish()
 
 
 def slices_of(weights, v_width, wide):
@@ -896,16 +1078,26 @@
             line.gather_drain(6 + h, blocks_of(normed_next, h))
 
 
-def ffn_backward_kernel(
-    cot, hidden, pre, normed, middle, grad, gain, weights,
-    d_mixer, grads, mixer_cot, grad_out, d_gain, d_pre, part, slots, total, send_sem, recv_sem,
-):
+def ffn_backward_kernel(owes, cot, hidden, pre, normed, middle, grad, gain, weights, *rest):
+    if owes:
+        owed, d_mixer, grads, mixer_cot, grad_out, d_gain, summed, *rest = rest
+    else:
+        d_mixer, grads, mixer_cot, grad_out, d_gain, *rest = rest
+    d_pre, part, slots, total, send_sem, recv_sem, *rest = rest
+    sums = None
+    if owes:
+        near, far, near_send, near_recv, far_send, far_recv, gate = rest
+        sums = Sums(owed, near, far, near_send, near_recv, far_send, far_recv)
     line = Line(send_sem, recv_sem)
     wide = hidden.shape[3]
     w_out, w_up, w_down = slices_of(weights, d_mixer.shape[3], wide)
     block = middle.shape[1]
     line.greet()
-    line.meet()
+    if owes:
+        sums.greet_late(gate)
+        sums.meet_late(line)
+    else:
+        line.meet()
     for h in range(HALVES):
         left = half_of(cot, h)
 
@@ -924,9 +1116,17 @@
         if h == 1:
             line.scatter_relay(0, *parts_of(part, slots, 0, 0))
         line.scatter_start(h, *parts_of(part, slots, 0, h))
+    if owes:
+        @pl.when(sums.parity == 1)
+        def _():
+            for m in range(4):
+                sums.turn(m)
+
     line.scatter_relay(1, *parts_of(part, slots, 0, 1))
     pieces = [row_grads(cot, hidden, grads, 0), row_grads(normed, d_pre, grads, wide)]
     run_pieces(pieces, 0, 2)
+    if owes:
+        sums.start_late()
     d_gain[...] = jnp.zeros_like(d_gain)
     for h in range(HALVES):
         both = parts_of(part, slots, 0, h)
@@ -938,6 +1138,12 @@
         grad_out[h] = value
         mixer_cot[line.me, h] = value.astype(BF16)
         line.gather_start(2 + h, blocks_of(mixer_cot, h))
+        if owes:
+            @pl.when(sums.parity == 0)
+            def _():
+                sums.turn(2 * h)
+                sums.turn(2 * h + 1)
+
     run_pieces(pieces, 2, 3)
     line.gather_forward(2, blocks_of(mixer_cot, 0))
     line.gather_forward(3, blocks_of(mixer_cot, 1))
@@ -951,6 +1157,8 @@
     for h in range(HALVES):
         line.scatter_drain(h, *parts_of(part, slots, 0, h))
         line.gather_drain(2 + h, blocks_of(mixer_cot, h))
+    if owes:
+        sums.finish(summed)
 
 
 def mixer_backward_kernel(
@@ -991,11 +1199,14 @@
         line.gather_drain(2 + h, blocks_of(cot, h))
 
 
-def last_kernel(gain_at, norm_rows, d_proj, w_in, normed, mixer, mixer_cot, rows, grad, gain, taps, norms,
-                grad_out, summed, taps_out, norms_out,
-                d_gain, grads, taps_land, line_land, norms_land,
-                taps_send, taps_recv, line_send, line_recv, norms_send, norms_recv,
-                part, slots, total, send_sem, recv_sem, *sum_refs):
+def last_kernel(heads, d_proj, w_in, normed, mixer, mixer_cot, rows, grad, gain, *refs):
+    smalls, refs = refs[: 5 * LAYERS + LAYERS - 1], refs[5 * LAYERS + LAYERS - 1 :]
+    per_layer = [smalls[5 * l : 5 * l + 5] for l in range(LAYERS)]
+    first_gains = smalls[5 * LAYERS :]
+    (grad_out, summed, taps_out, norms_out,
+     d_gain, grads, taps_land, line_land, norms_land,
+     taps_send, taps_recv, line_send, line_recv, norms_send, norms_recv,
+     part, slots, total, send_sem, recv_sem, *sum_refs) = refs
     line = Line(send_sem, recv_sem)
     sums = Sums(grads, *sum_refs)
     small_taps = Smalls("dp", taps_land, taps_send, taps_recv)
@@ -1003,7 +1214,26 @@
     small_norms = Smalls("dp", norms_land, norms_send, norms_recv)
     line.greet()
     others = sums.greet() + small_taps.greet() + small_line.greet()
-    taps_land[small_taps.me] = taps[...]
+    taps_land[small_taps.me] = jnp.zeros(taps_land.shape[1:], F32)
+    line_land[line.me] = jnp.zeros(line_land.shape[1:], F32)
+    for l, (d_qk, d_v, d_head, d_out_gain, second_gain) in enumerate(per_layer):
+        top = TAP_ROWS * l
+        seqs = d_qk.shape[0]
+        for i in range(2):
+            taps_land[small_taps.me, top + 4 * i : top + 4 * i + 4, : d_qk.shape[3]] = sum(d_qk[s, i] for s in range(seqs))
+        taps_land[small_taps.me, top + 8 : top + 12, : d_v.shape[2]] = sum(d_v[s] for s in range(seqs))
+        lane = iota((1, 128), 1)
+        row = jnp.zeros((1, 128), F32)
+        for kind in range(2):
+            for h in range(heads):
+                value = sum(d_head[s, h, kind : kind + 1, :] for s in range(seqs))
+                row = row + jnp.where(lane == kind * heads + h, value, 0.0)
+        taps_land[small_taps.me, top + 12 : top + 13, :128] = row
+        line_land[line.me, 2 * l + 1 : 2 * l + 2, :] = second_gain[...]
+        value = sum(d_out_gain[s, h] for s in range(seqs) for h in range(heads))
+        line_land[line.me, 2 * LAYERS + l : 2 * LAYERS + l + 1, : value.shape[1]] = value
+        if l > 0:
+            line_land[line.me, 2 * l : 2 * l + 1, :] = first_gains[l - 1][...]
     partial_sums(half_of(d_proj, 0), w_in, part, 0, 0)
     line.meet(others)
     line.scatter_start(0, *parts_of(part, slots, 0, 0))
@@ -1029,9 +1259,7 @@
         back, gain_part = rms_back(rows[h].astype(F32), gain[...], total[...])
         d_gain[...] += gain_part
         grad_out[h] = grad[h] + back
-    line_land[line.me] = norms[...]
-    for i in range(norm_rows):
-        line_land[line.me, gain_at + i : gain_at + i + 1, :] = d_gain[:, 128 * i : 128 * (i + 1)]
+    line_land[line.me, 0:1, :] = d_gain[...]
     small_line.start()
     norms_land[small_norms.me] = small_line.finish()
     small_norms.start()
@@ -1042,13 +1270,14 @@
     norms_out[...] = small_norms.finish()
 
 
+TAP_ROWS = 16
 DMA = pltpu.SemaphoreType.DMA
 
 
-def line_call(kernel, operands, outs, scratch, number, name, micros):
+def line_call(kernel, operands, outs, scratch, number, name, micros, spaces=None):
     return pl.pallas_call(
         kernel,
-        in_specs=[pl.BlockSpec(memory_space=pltpu.VMEM)] * len(operands),
+        in_specs=[pl.BlockSpec(memory_space=s) for s in spaces or [pltpu.VMEM] * len(operands)],
         out_specs=[pl.BlockSpec(memory_space=pltpu.VMEM)] * len(outs),
         out_shape=[jax.ShapeDtypeStruct(*out) for out in outs],
         scratch_shapes=scratch,
@@ -1078,10 +1307,25 @@
     ]
 
 
-def start_call(rows, cot, gain):
+def start_call(rows, cot, gain, in_weights, rest_weights, rest_units, dp):
     _, block, width = rows.shape
+    in_places = cast_places(in_weights, (128,) * len(in_weights))
+    rest_places = cast_places(rest_weights, rest_units)
+    own = in_weights[0].shape[1]
+    in_width, rest_width = (sum(p[2] for p in places) for places in (in_places, rest_places))
     whole = ((4, HALVES, block, width), BF16)
-    return line_call(start_kernel, (rows, cot, gain), [whole, whole], [DMA((4, 4)), DMA((4, 5))], 1, "start", 35)
+    outs = [whole, whole, ((dp, own, in_width), BF16)]
+    outs += [((own, in_width), BF16), ((own, rest_width), BF16)] * (LAYERS - 1)
+    half = dp // 2
+    scratch = [pltpu.VMEM(held_shape(w), F32) for w in in_weights + rest_weights] + [
+        DMA((len(in_weights),)), DMA((len(rest_weights),)),
+        DMA((4, 4)), DMA((4, 5)), DMA((half,)), DMA((half,)), DMA((half,)), DMA((half,)),
+    ]
+    return line_call(
+        functools.partial(start_kernel, in_places, rest_places),
+        (rows, cot, gain, *[turn(w) for w in in_weights + rest_weights]), outs, scratch, 1, "start", 35,
+        [pltpu.VMEM] * 3 + [pl.ANY] * len(in_weights + rest_weights),
+    )
 
 
 def ffn_forward_call(mixer, weights, rows, gain, gain_next, layer, last):
@@ -1097,7 +1341,7 @@
     )
 
 
-def ffn_backward_call(cot, hidden, pre, normed, middle, grad, gain, weights, v_width, grads_shape, layer):
+def ffn_backward_call(cot, hidden, pre, normed, middle, grad, gain, weights, v_width, grads_shape, owed, layer):
     _, block, width = middle.shape
     wide = hidden.shape[3]
     whole = ((4, HALVES, block, width), BF16)
@@ -1106,8 +1350,13 @@
         ((HALVES, block, width), F32), ((1, width), F32),
     ]
     scratch = [pltpu.VMEM((4, HALVES, block, 2 * wide), BF16)] + line_scratch(1, block, width, 4)
+    operands = [cot, hidden, pre, normed, middle, grad, gain, weights]
+    if owed is not None:
+        operands.append(owed)
+        outs.append((owed.shape[2:], F32))
+        scratch += sums_scratch(owed.shape) + [pltpu.SemaphoreType.REGULAR]
     return line_call(
-        ffn_backward_kernel, (cot, hidden, pre, normed, middle, grad, gain, weights), outs, scratch,
+        functools.partial(ffn_backward_kernel, owed is not None), operands, outs, scratch,
         4 + layer, "ffn_backward", 40,
     )
 
@@ -1124,74 +1373,85 @@
     )
 
 
-def last_call(d_proj, w_in, normed, mixer, mixer_cot, rows, grad, gain, taps, norms, grads_shape, gain_at):
+def last_call(d_proj, w_in, normed, mixer, mixer_cot, rows, grad, gain, smalls, first_gains, grads_shape, heads):
     _, block, width = rows.shape
     dp = 2 * grads_shape[0]
     shape = grads_shape + (mixer.shape[3] + w_in.shape[1],)
-    outs = [((HALVES, block, width), F32), (shape[2:], F32), (taps.shape, F32), (norms.shape, F32)]
+    taps_width = max(smalls[0][0].shape[3], smalls[0][1].shape[2])
+    taps_shape, norms_shape = (TAP_ROWS * LAYERS, taps_width), (8, width)
+    outs = [((HALVES, block, width), F32), (shape[2:], F32), (taps_shape, F32), (norms_shape, F32)]
     scratch = [
-        pltpu.VMEM((1, width), F32), pltpu.VMEM(shape, BF16), pltpu.VMEM((dp,) + taps.shape, F32),
-        pltpu.VMEM((4,) + norms.shape, F32), pltpu.VMEM((dp,) + norms.shape, F32),
+        pltpu.VMEM((1, width), F32), pltpu.VMEM(shape, BF16), pltpu.VMEM((dp,) + taps_shape, F32),
+        pltpu.VMEM((4,) + norms_shape, F32), pltpu.VMEM((dp,) + norms_shape, F32),
         DMA((dp,)), DMA((dp,)), DMA((4,)), DMA((4,)), DMA((dp,)), DMA((dp,)),
     ]
+    flat = [array for layer in smalls for array in layer] + list(first_gains)
     return line_call(
-        functools.partial(last_kernel, gain_at, width // 128),
-        (d_proj, w_in, normed, mixer, mixer_cot, rows, grad, gain, taps, norms), outs,
+        functools.partial(last_kernel, heads),
+        (d_proj, w_in, normed, mixer, mixer_cot, rows, grad, gain, *flat), outs,
         scratch + line_scratch(1, block, width, 2) + sums_scratch(shape), 8, "last", 40,
     )
 
 
-def finish_kernel(places, *refs):
-    sources, outs = refs[: 2 * LAYERS], refs[2 * LAYERS : 2 * LAYERS + len(places)]
-    held, sems = refs[2 * LAYERS + len(places) : -1], refs[-1]
-    for i, (kind, width, start) in enumerate(places):
+def finish_kernel(places, heads, *refs):
+    sources, refs = refs[: 2 * LAYERS + 4], refs[2 * LAYERS + 4 :]
+    rows, grad, taps, norms = sources[2 * LAYERS :]
+    outs, refs = refs[: len(places) + 2], refs[len(places) + 2 :]
+    (conv_qk, conv_v, head, norm_gains, out_gain), refs = refs[:5], refs[5:]
+    held, sems = refs[:-1], refs[-1]
+    copies = [
+        pltpu.make_async_copy(rows, outs[len(places)], sems.at[len(places)]),
+        pltpu.make_async_copy(grad, outs[len(places) + 1], sems.at[len(places) + 1]),
+    ]
+    for copy in copies:
+        copy.start()
+    for i, (kind, width, start, turned) in enumerate(places):
         for l in range(LAYERS):
             source = sources[kind * LAYERS + l]
-            held[i][l] = source[:, start : start + width].astype(F32)
-        pltpu.make_async_copy(held[i], outs[i], sems.at[i]).start()
-    for i in range(len(places)):
-        pltpu.make_async_copy(held[i], outs[i], sems.at[i]).wait()
-
-
-def finish_call(mixer_grads, ffn_grads, places):
-    operands = list(mixer_grads) + list(ffn_grads)
-    own = operands[0].shape[0]
-    shapes = [(LAYERS, own, width) for _, width, _ in places]
-    return pl.pallas_call(
-        functools.partial(finish_kernel, places),
+            if turned:
+                tall = -(-width // 128) * 128
+                held[i][l] = jnp.transpose(source[:, start : start + tall].astype(F32))[:width]
+            else:
+                held[i][l] = source[:, start : start + width].astype(F32)
+        copies.append(pltpu.make_async_copy(held[i], outs[i], sems.at[i]))
+        copies[-1].start()
+    for l in range(LAYERS):
+        top = TAP_ROWS * l
+        for i in range(2):
+            conv_qk[l, i] = taps[top + 4 * i : top + 4 * i + 4, : conv_qk.shape[3]]
+            head[l, i : i + 1, :] = taps[top + 12 : top + 13, i * heads : (i + 1) * heads]
+            norm_gains[l, i : i + 1, :] = norms[2 * l + i : 2 * l + i + 1, :]
+        conv_v[l] = taps[top + 8 : top + 12, : conv_v.shape[2]]
+        out_gain[l : l + 1, :] = norms[2 * LAYERS + l : 2 * LAYERS + l + 1, : out_gain.shape[1]]
+    for copy in copies:
+        copy.wait()
+
+
+def finish_call(mixer_grads, ffn_grads, rows, grad, taps, norms, places, like):
+    operands = list(mixer_grads) + list(ffn_grads) + [rows, grad, taps, norms]
+    own = mixer_grads[0].shape[0]
+    heads = like[2].shape[2]
+    full = [(LAYERS, own, width) for _, width, _ in places]
+    turned = [is_turned(shape) for shape in full]
+    shapes = [(s[0], s[2], s[1]) if t else s for s, t in zip(full, turned)]
+    places = [p + (t,) for p, t in zip(places, turned)]
+    count = len(places)
+    outs = pl.pallas_call(
+        functools.partial(finish_kernel, places, heads),
         in_specs=[pl.BlockSpec(memory_space=pltpu.VMEM)] * len(operands),
-        out_specs=[pl.BlockSpec(memory_space=pl.ANY)] * len(places),
-        out_shape=[jax.ShapeDtypeStruct(shape, F32) for shape in shapes],
-        scratch_shapes=[pltpu.VMEM(shape, F32) for shape in shapes] + [DMA((len(places),))],
+        out_specs=[pl.BlockSpec(memory_space=pl.ANY)] * (count + 2) + [pl.BlockSpec(memory_space=pltpu.VMEM)] * 5,
+        out_shape=[jax.ShapeDtypeStruct(shape, F32) for shape in shapes + [rows.shape, grad.shape]]
+        + [jax.ShapeDtypeStruct(array.shape, F32) for array in like],
+        scratch_shapes=[pltpu.VMEM(shape, F32) for shape in shapes] + [DMA((count + 2,))],
         compiler_params=pltpu.CompilerParams(vmem_limit_bytes=VMEM_LIMIT),
         name="finish",
     )(*operands)
-
-
-LAYERS = 2
+    weight_grads = [jnp.swapaxes(o, 1, 2) if t else o for o, t in zip(outs[:count], turned)]
+    return outs[count], outs[count + 1], weight_grads, outs[count + 2 :]
+
+
 CHUNK = 128
-REFINE = 1
-
-
-def packed(arrays):
-    flat = []
-    for array in arrays:
-        flat.append(jnp.pad(array.reshape(-1), (0, -array.size % 128)))
-    flat = jnp.concatenate(flat)
-    return jnp.pad(flat, (0, -flat.size % 1024)).reshape(-1, 128)
-
-
-def unpacked(rows, like):
-    found, start = [], 0
-    for array in like:
-        count = -(-array.size // 128)
-        found.append(rows[start : start + count].reshape(-1)[: array.size].reshape(array.shape))
-        start += count
-    return tuple(found)
-
-
-def padded(matrix, width):
-    return jnp.pad(matrix, ((0, 0), (0, width - matrix.shape[1])))
+REFINE = 2
 
 
 def body(
@@ -1229,16 +1489,9 @@
     def reduced(matrix):
         return lax.psum_scatter(matrix, "dp", scatter_dimension=0, tiled=True)
 
-    def layer_weights(l):
-        low = lambda m: m[l].astype(BF16)
-        first = gathered(jnp.concatenate(
-            [low(query_weight), low(key_weight), low(value_weight), low(gate_weight), padded(low(decay_weight), 128)], axis=1
-        ))
-        second = gathered(jnp.concatenate(
-            [low(out_weight), padded(low(swiglu_gate), hidden_pad), padded(low(swiglu_up), hidden_pad),
-             padded(low(swiglu_down), hidden_pad)], axis=1
-        ))
-        return first, second
+    in_weights = (query_weight, key_weight, value_weight, gate_weight, decay_weight)
+    rest_weights = (out_weight, swiglu_gate, swiglu_up, swiglu_down)
+    rest_units = (128, 256, 256, 256)
 
     def split_rows(matrix):
         return matrix.reshape(HALVES, block, matrix.shape[1])
@@ -1252,70 +1505,63 @@
     def gain_of(l, i):
         return norm_gains[l, i][None]
 
-    weights = [layer_weights(l) for l in range(LAYERS)]
+    dp = lax.axis_size("dp")
     rows = split_rows(tokens)
     cot_rows = split_rows(cotangent)
-    normed, cot = start_call(rows, cot_rows, gain_of(0, 0))
+    w_rest = [gathered(cast_call(rest_weights, rest_units, 0))]
+    normed, cot, w_in, *low = start_call(rows, cot_rows, gain_of(0, 0), in_weights, rest_weights, rest_units, dp)
+    w_in = [w_in.reshape(width, w_in.shape[2])] + [gathered(part) for part in low[::2]]
+    w_rest += [gathered(part) for part in low[1::2]]
     kept = []
     for l in range(LAYERS):
-        w_in, w_rest = weights[l]
         last = l == LAYERS - 1
-        proj = jnp.dot(merged(normed), w_in, preferred_element_type=F32)
+        proj = jnp.dot(merged(normed), w_in[l], preferred_element_type=F32)
         small = (conv_query_key[l], conv_value[l], head_params[l], out_gain[l][None])
         mixer, *saved = delta_forward(proj, *small, tables, seqs, heads, CHUNK, REFINE)
         mixer = split_all(mixer)
         gain_next = gain_of(min(l + 1, LAYERS - 1), 0)
         middle, normed_ffn, pre, hidden, out_rows, *following = ffn_forward_call(
-            mixer, w_rest, rows, gain_of(l, 1), gain_next, l, last
+            mixer, w_rest[l], rows, gain_of(l, 1), gain_next, l, last
         )
         kept.append((rows, normed, proj, small, mixer, saved, middle, normed_ffn, pre, hidden))
         rows = out_rows
         if not last:
             normed = following[0]
-    output = rows.reshape(local_rows, width)
+    output = rows
     grad = cot_rows
-    dp = lax.axis_size("dp")
     grads_shape = (dp // 2, 2, width // dp)
-    ffn_grads, mixer_grads, tap_grads, norm_grads, gain_grads = ([None] * LAYERS for _ in range(5))
+    ffn_grads, mixer_grads, smalls, first_gains = ([None] * LAYERS for _ in range(4))
+    owed = None
     for l in reversed(range(LAYERS)):
-        w_in, w_rest = weights[l]
         rows, normed, proj, small, mixer, saved, middle, normed_ffn, pre, hidden = kept[l]
+        d_mixer, ffn_grad, mixer_cot, grad, second_gain, *summed = ffn_backward_call(
+            cot, hidden, pre, normed_ffn, middle, grad, gain_of(l, 1), w_rest[l], v_width, grads_shape, owed, l
+        )
+        if summed:
+            mixer_grads[l + 1] = summed[0]
+        ffn_grads[l] = reduced(ffn_grad.reshape(width, 3 * hidden_pad))
         if l < LAYERS - 1:
-            cot, ffn_grads[l + 1] = lax.optimization_barrier((cot, ffn_grads[l + 1]))
-        d_mixer, ffn_grad, mixer_cot, grad, second_gain = ffn_backward_call(
-            cot, hidden, pre, normed_ffn, middle, grad, gain_of(l, 1), w_rest, v_width, grads_shape, l
-        )
-        ffn_grads[l] = reduced(ffn_grad.reshape(width, 3 * hidden_pad))
+            d_mixer, ffn_grads[l + 1] = lax.optimization_barrier((d_mixer, ffn_grads[l + 1]))
         d_proj, d_qk, d_v, d_head, d_gain = delta_backward(
             proj, *small, tables, saved, merged(d_mixer), seqs, heads, CHUNK
         )
-        tap_grads[l] = (d_qk.sum(0), d_v.sum(0), d_head.sum(0)[:, :2, 0].T)
-        gain_grads[l] = d_gain.sum((0, 1, 2))
+        smalls[l] = (d_qk, d_v, d_head, d_gain, second_gain)
         d_proj = split_all(d_proj)
         if l > 0:
-            grad, first_gain, mixer_grad, cot = mixer_backward_call(
-                d_proj, w_in, normed, mixer, mixer_cot, rows, grad, gain_of(l, 0), grads_shape, l
+            grad, first_gains[l], owed, cot = mixer_backward_call(
+                d_proj, w_in[l], normed, mixer, mixer_cot, rows, grad, gain_of(l, 0), grads_shape, l
             )
-            mixer_grads[l] = reduced(mixer_grad.reshape(width, mixer_grad.shape[3]))
-            norm_grads[l] = jnp.concatenate([first_gain, second_gain], axis=0)
-    norm_grads[0] = jnp.concatenate([jnp.zeros_like(second_gain), second_gain], axis=0)
-    taps = tuple(jnp.stack([tap_grads[l][i] for l in range(LAYERS)]) for i in range(3))
-    norms = (jnp.stack(norm_grads), jnp.stack(gain_grads))
-    d_proj, mixer_grads[1] = lax.optimization_barrier((d_proj, mixer_grads[1]))
-    grad, mixer_grads[0], *small_sums = last_call(
-        d_proj, w_in, normed, mixer, mixer_cot, rows, grad, gain_of(0, 0), packed(taps), packed(norms), grads_shape, 0
+    grad, mixer_grads[0], taps, norms = last_call(
+        d_proj, w_in[0], normed, mixer, mixer_cot, rows, grad, gain_of(0, 0), smalls, first_gains[1:], grads_shape, heads
     )
-    taps, norms = unpacked(small_sums[0], taps), unpacked(small_sums[1], norms)
-
-    weight_grads = finish_call(
-        mixer_grads, ffn_grads,
+    output, grad, weight_grads, others = finish_call(
+        mixer_grads, ffn_grads, output, grad, taps, norms,
         [(0, qk_width, v_width), (0, qk_width, v_width + qk_width), (0, v_width, v_width + 2 * qk_width),
          (0, v_width, 2 * v_width + 2 * qk_width), (0, pair_width, 3 * v_width + 2 * qk_width), (0, v_width, 0),
          (1, hidden_width, hidden_pad), (1, hidden_width, 2 * hidden_pad), (1, hidden_width, 0)],
+        (conv_query_key, conv_value, head_params, norm_gains, out_gain),
     )
-    return (
-        output, grad.reshape(local_rows, width), *weight_grads, *taps, *norms
-    )
+    return (output.reshape(local_rows, width), grad.reshape(local_rows, width), *weight_grads, *others)
 
 
 def solution(mesh):

time: 514 us -> 475 us (0.924)
  the two profiles are of different devices: /device:TPU:0 before, /device:TPU:23 now
where the time goes in v4:
time: 475 us; the launch traced here: 467 us
  Pallas kernels  437 us (92%)
  between operations  14.4 us (3%)
  matrix products  8.76 us (2%)
    pallas_call x7, Pallas kernels, line_call(): pl.pallas_call(kernel, in_specs=[pl.BlockSpec(memory_space=s) for s in sp...  351 us
    pallas_call x2, Pallas kernels, delta_backward(): pl.pallas_call(functools.partial(backward_kernel, chunk, heads), grid=(se...  50.2 us
    pallas_call x2, Pallas kernels, delta_forward(): pl.pallas_call(functools.partial(forward_kernel, chunk, refine), grid=(se...  28.9 us
  transfers between devices with their start and end apart: 5, of which 0 were waited for; matrix products, arithmetic and copies ran while one was open for 3% of the time, Pallas kernels for 73%

profile of v4, /device:TPU:23, one launch (start us, length us, event | category | flops | bytes accessed | tf_op | source)
XLA Modules:
  0.0 466.6 jit_solution(10637319402393135643)
XLA Ops:
  7.2 0.0 all-gather.4.cloned.1.call-start
  7.2 2.4 cast.1
  9.7 0.0 all-gather.6.cloned.1.call-start
  9.8 0.6 slice_bitcast_fusion.4
  10.4 42.9 %start.1 = (bf16[4,2,64,1024]{3,2,1,0:T(8,128)(2,1)}, bf16[4,2,64,1024]{3,2,1,0:T(8,128)(2,1)}, bf16[8,128,1664]{2,1,0:T(8,128)(2,1)}, bf16[128,1664]{1,0:T(8,128)(2,1)}, bf16[128,2816]{1,0:T(8,128)(2,1)}) custom-call(bf16[2,64,1024]{2,1,0:T(8,128)(2,1)} %bitcast.83, bf16[2,64,1024]{2,1,0:T(8,128)(2,1)} %bitcast.90, f32[1,1024]{1,0:T(1,128)} %get-tuple-element.164.gain, ...), custom_call_target="tpu_custom_call" | custom-call | bytes 122500000 | tf_op jit(solution)/shard_map/start/pallas_call | solution.py:1278
  53.3 0.0 all-gather.8.cloned.1.call-start
  53.3 0.7 all-gather.8.cloned.1.call-update
  54.0 0.0 reduce-scatter.3.cloned.1.call-start
  54.1 0.5 slice.69
  54.6 0.1 slice.70
  54.7 0.1 copy.44
  54.7 0.7 add_bitcast_fusion
  55.5 0.1 eq.40
  55.5 0.1 eq.43
  55.6 0.1 fusion.1
  55.7 0.8 copy.43.col_ref
  56.8 4.4 fusion.6.qref.kref.vref.gref.pair_ref
  61.3 14.5 %delta_forward.2 = (bf16[512,512]{1,0:T(8,128)(2,1)S(1)}, f32[512,512]{1,0:T(8,128)}, f32[512,512]{1,0:T(8,128)}, f32[1,2,4,128,128]{4,3,2,1,0:T(8,128)}, f32[1,2,4,128,256]{4,3,2,1,0:T(8,128)}) custom-call(f32[512,1664]{1,0:T(8,128)S(1)} %fusion.6.qref.kref.vref.gref.pair_ref, f32[512,1664]{1,0:T(8,128)S(1)} %fusion.6.qref.kref.vref.gref.pair_ref, ...), custom_call_target="tpu_custom_call" | custom-call | bytes 52500000 | tf_op jit(solution)/shard_map/delta_forward/pallas_call | solution.py:374
  75.8 0.8 copy-done.4
  76.5 90.0 %ffn_forward.2 = (f32[2,64,1024]{2,1,0:T(8,128)}, bf16[4,2,64,1024]{3,2,1,0:T(8,128)(2,1)}, f32[4,2,64,1536]{3,2,1,0:T(8,128)}, bf16[4,2,64,768]{3,2,1,0:T(8,128...) custom-call(bf16[4,2,64,512]{3,2,1,0:T(8,128)(2,1)} %bitcast.69, ...), custom_call_target="tpu_custom_call" | custom-call | bytes 227500000 | tf_op jit(solution)/shard_map/ffn_forward/pallas_call | solution.py:1278
  166.6 4.4 fusion.7.qref.kref.vref.gref.pair_ref
  171.0 14.4 %delta_forward.3 = (bf16[512,512]{1,0:T(8,128)(2,1)S(1)}, f32[512,512]{1,0:T(8,128)}, f32[512,512]{1,0:T(8,128)}, f32[1,2,4,128,128]{4,3,2,1,0:T(8,128)}, f32[1,2,4,128,256]{4,3,2,1,0:T(8,128)}) custom-call(f32[512,1664]{1,0:T(8,128)S(1)} %fusion.7.qref.kref.vref.gref.pair_ref, f32[512,1664]{1,0:T(8,128)S(1)} %fusion.7.qref.kref.vref.gref.pair_ref, ...), custom_call_target="tpu_custom_call" | custom-call | bytes 52500000 | tf_op jit(solution)/shard_map/delta_forward/pallas_call | solution.py:374
  185.5 0.8 copy-done.5
  186.3 54.8 %ffn_forward.3 = (f32[2,64,1024]{2,1,0:T(8,128)}, bf16[4,2,64,1024]{3,2,1,0:T(8,128)(2,1)}, f32[4,2,64,1536]{3,2,1,0:T(8,128)}, bf16[4,2,64,768]{3,2,1,0:T(8,128)(2,1)}, f32[2,64,1024]{2,1,0:T(8,128)}) custom-call(bf16[4,2,64,512]{3,2,1,0:T(8,128)(2,1)} %bitcast.71, bf16[1024,2816]{1,0:T(8,128)(2,1)} %all-gather.8.cloned.1.call-done.weights, ...), custom_call_target="tpu_custom_call" | custom-call | bytes 227500000 | tf_op jit(solution)/shard_map/ffn_forward/pallas_call | solution.py:1278
  241.0 33.2 %ffn_backward.2 = (f32[4,2,64,512]{3,2,1,0:T(8,128)}, bf16[4,2,128,2304]{3,2,1,0:T(8,128)(2,1)}, bf16[4,2,64,1024]{3,2,1,0:T(8,128)(2,1)}, f32[2,64,1024]{2,1,0:T(8,128)}, f32[1,1024]{1,0:T(1,128)}) custom-call(bf16[4,2,64,1024]{3,2,1,0:T(8,128)(2,1)} %get-tuple-element.102.cot, bf16[4,2,64,768]{3,2,1,0:T(8,128)(2,1)} %get-tuple-element.106.hidden, ...), custom_call_target="tpu_custom_call" | custom-call | bytes 140000000 | tf_op jit(solution)/shard_map/ffn_backward/pallas_call | solution.py:1278
  274.3 0.0 reduce-scatter.5.cloned.1.call-start
  274.3 25.1 %delta_backward.2 = (bf16[512,1664]{1,0:T(8,128)(2,1)}, f32[1,2,4,256]{3,2,1,0:T(4,128)}, f32[1,4,512]{2,1,0:T(4,128)}, f32[1,2,8,128]{3,2,1,0:T(8,128)}, f32[1,2,1,256]{3,2,1,0:T(1,128)}) custom-call(f32[512,1664]{1,0:T(8,128)} %copy-done.1, f32[512,1664]{1,0:T(8,128)} %copy-done.1, f32[512,1664]{1,0:T(8,128)} %copy-done.1, f32[512,1664]{1,0:T(8,128)} %copy-done.1, ...), custom_call_target="tpu_custom_call" | custom-call | bytes 87500000 | tf_op jit(solution)/shard_map/delta_backward/pallas_call | solution.py:404
  299.4 30.7 %mixer_backward.1 = (f32[2,64,1024]{2,1,0:T(8,128)}, f32[1,1024]{1,0:T(1,128)}, bf16[4,2,128,2176]{3,2,1,0:T(8,128)(2,1)}, bf16[4,2,64,1024]{3,2,1,0:T(8,128)(2,1)}) custom-call(bf16[4,2,64,1664]{3,2,1,0:T(8,128)(2,1)} %bitcast.87, bf16[1024,1664]{1,0:T(8,128)(2,1)} %all-gather.6.cloned.1.call-done.w_in, bf16[4,2,64,1024]{3,2,1,0:T(8,128)(2,1)} %get-tuple-element.96.normed, ...), custom_call_target="tpu_custom_call" | custom-call | bytes 140000000 | tf_op jit(solution)/shard_map/mixer_backward/pallas_call | solution.py:1278
  330.2 43.1 %ffn_backward.3 = (f32[4,2,64,512]{3,2,1,0:T(8,128)}, bf16[4,2,128,2304]{3,2,1,0:T(8,128)(2,1)}, bf16[4,2,64,1024]{3,2,1,0:T(8,128)(2,1)}, f32[2,64,1024]{2,1,0:...) custom-call(bf16[4,2,64,1024]{3,2,1,0:T(8,128)(2,1)} %get-tuple-element.114.cot, ...), custom_call_target="tpu_custom_call" | custom-call | bytes 140000000 | tf_op jit(solution)/shard_map/ffn_backward/pallas_call | solution.py:1278
  373.3 25.1 %delta_backward.3 = (bf16[512,1664]{1,0:T(8,128)(2,1)}, f32[1,2,4,256]{3,2,1,0:T(4,128)}, f32[1,4,512]{2,1,0:T(4,128)}, f32[1,2,8,128]{3,2,1,0:T(8,128)}, f32[1,2,1,256]{3,2,1,0:T(1,128)}) custom-call(f32[512,1664]{1,0:T(8,128)} %copy-done, f32[512,1664]{1,0:T(8,128)} %copy-done, f32[512,1664]{1,0:T(8,128)} %copy-done, f32[512,1664]{1,0:T(8,128)} %copy-done, ...), custom_call_target="tpu_custom_call" | custom-call | bytes 87500000 | tf_op jit(solution)/shard_map/delta_backward/pallas_call | solution.py:404
  398.5 56.0 %last.1 = (f32[2,64,1024]{2,1,0:T(8,128)}, f32[128,2176]{1,0:T(8,128)}, f32[32,512]{1,0:T(8,128)}, f32[8,1024]{1,0:T(8,128)}) custom-call(bf16[4,2,64,1664]{3,2,1,0:T(8,128)(2,1)} %bitcast.86, bf16[1024,1664]{1,0:T(8,128)(2,1)} %bitcast.76, bf16[4,2,64,1024]{3,2,1,0:T(8,128)(2,1)} %get-tuple-element.89.normed, bf16[4,2,64,512]{3,2,1,0:T(8,128)(2,1)} %bitcast.70, ...), custom_call_target="tpu_custom_call" | custom-call | bytes 140000000 | tf_op jit(solution)/shard_map/last/pallas_call | solution.py:1278
  454.5 5.3 %finish.1 = (f32[2,128,256]{2,1,0:T(8,128)}, f32[2,128,256]{2,1,0:T(8,128)}, f32[2,128,512]{2,1,0:T(8,128)}, f32[2,128,512]{2,1,0:T(8,128)}, f32[2,4,128]{2,1,0:...) custom-call(f32[128,2176]{1,0:T(8,128)} %get-tuple-element.138.refs_, ...), custom_call_target="tpu_custom_call" | custom-call | tf_op jit(solution)/shard_map/finish/pallas_call | solution.py:1439
  (59 shorter events, 0.3 us)
Async XLA Ops:
  7.2 2.6 copy-start.16
  7.2 69.4 %all-gather.4.cloned.1.call-start = ((), (), s32[]{:S(2)}) async-start(), calls=%async_computation.2 | async-start | bytes 6488064 | tf_op jit(solution)/shard_map/all_gather | solution.py:1487
  9.6 44.4 %copy-start.15 = (s32[1,512]{1,0:T(1,128)S(1)}, s32[1,512]{1,0:T(1,128)}, u32[]{:S(2)}) copy-start(s32[1,512]{1,0:T(1,128)} %param.18) | copy-start | bytes 6148
  9.6 47.0 %copy-start.19 = (f32[2,2,2]{2,1,0:T(2,128)S(1)}, f32[2,2,2]{2,1,0:T(2,128)}, u32[]{:S(2)}) copy-start(f32[2,2,2]{2,1,0:T(2,128)} %param.30) | copy-start | bytes 100
  9.6 47.0 %copy-start.20 = (f32[2,256]{1,0:T(2,128)S(1)}, f32[2,256]{1,0:T(2,128)}, u32[]{:S(2)}) copy-start(f32[2,256]{1,0:T(2,128)} %param.32) | copy-start | bytes 6148
  9.7 47.0 %copy-start.17 = (f32[2,2,4,256]{3,2,1,0:T(4,128)S(1)}, f32[2,2,4,256]{3,2,1,0:T(4,128)}, u32[]{:S(2)}) copy-start(f32[2,2,4,256]{3,2,1,0:T(4,128)} %param.28) | copy-start | bytes 49156
  9.7 47.0 %copy-start.18 = (f32[2,4,512]{2,1,0:T(4,128)S(1)}, f32[2,4,512]{2,1,0:T(4,128)}, u32[]{:S(2)}) copy-start(f32[2,4,512]{2,1,0:T(4,128)} %param.29) | copy-start | bytes 49156
  9.7 156.8 %all-gather.6.cloned.1.call-start = ((), (), s32[]{:S(2)}) async-start(), calls=%async_computation.3 | async-start | bytes 3833856 | tf_op jit(solution)/shard_map/all_gather | solution.py:1487
  53.3 133.0 %all-gather.8.cloned.1.call-start = ((), (), s32[]{:S(2)}) async-start(), calls=%async_computation.4 | async-start | bytes 6488064 | tf_op jit(solution)/shard_map/all_gather | solution.py:1487
  54.0 319.3 %reduce-scatter.3.cloned.1.call-start = ((), (), s32[]{:S(2)}) async-start(), calls=%async_computation.5 | async-start | bytes 5308416 | tf_op jit(solution)/shard_map/reduce_scatter | solution.py:1490
  56.6 114.3 %copy-start.6 = (f32[1,8,512]{2,1,0:T(8,128)}, f32[1,8,512]{2,1,0:T(8,128)S(1)}, u32[]{:S(2)}) copy-start(f32[1,8,512]{2,1,0:T(8,128)S(1)} %stack.63.row_ref) | copy-start | bytes 49156
  56.7 4.6 copy-start.11
  56.7 114.3 %copy-start.13 = (f32[2,2]{1,0:T(2,128)}, f32[2,2]{1,0:T(2,128)S(1)}, u32[]{:S(2)}) copy-start(f32[2,2]{1,0:T(2,128)S(1)} %get-tuple-element.172.head_table) | copy-start | bytes 52
  56.7 4.5 copy-start.12
  56.7 114.3 %copy-start.14 = (f32[1,256]{1,0:T(1,128)}, f32[1,256]{1,0:T(1,128)S(1)}, u32[]{:S(2)}) copy-start(f32[1,256]{1,0:T(1,128)S(1)} %get-tuple-element.170.gain) | copy-start | bytes 3076
  56.7 4.5 copy-start.7
  56.8 114.2 %copy-start.9 = (f32[2,4,256]{2,1,0:T(4,128)}, f32[2,4,256]{2,1,0:T(4,128)S(1)}, u32[]{:S(2)}) copy-start(f32[2,4,256]{2,1,0:T(4,128)S(1)} %get-tuple-element.168.tap_qk) | copy-start | bytes 24580
  56.8 4.5 copy-start.8
  56.8 114.2 %copy-start.10 = (f32[4,512]{1,0:T(4,128)}, f32[4,512]{1,0:T(4,128)S(1)}, u32[]{:S(2)}) copy-start(f32[4,512]{1,0:T(4,128)S(1)} %get-tuple-element.166.tap_v) | copy-start | bytes 24580
  56.8 4.4 copy-start.2
  61.2 14.5 %copy-start = (f32[512,1664]{1,0:T(8,128)}, f32[512,1664]{1,0:T(8,128)S(1)}, u32[]{:S(2)}) copy-start(f32[512,1664]{1,0:T(8,128)S(1)} %fusion.6.qref.kref.vref.gref.pair_ref) | copy-start | bytes 10223620
  75.8 0.8 copy-start.4
  166.6 4.5 copy-start.3
  171.0 14.5 %copy-start.1 = (f32[512,1664]{1,0:T(8,128)}, f32[512,1664]{1,0:T(8,128)S(1)}, u32[]{:S(2)}) copy-start(f32[512,1664]{1,0:T(8,128)S(1)} %fusion.7.qref.kref.vref.gref.pair_ref) | copy-start | bytes 10223620
  185.5 0.8 copy-start.5
  274.3 180.2 %reduce-scatter.5.cloned.1.call-start = ((), (), s32[]{:S(2)}) async-start(), calls=%async_computation.6 | async-start | bytes 5308416 | tf_op jit(solution)/shard_map/reduce_scatter | solution.py:1490
Sparse Core Ops, SparseCore 0:
  10.5 53.5 all-gather.3
  65.9 33.4 all-gather.5
  101.3 43.3 all-gather.7
  274.4 54.5 reduce-scatter.2
  373.4 80.9 reduce-scatter.4

commit v5 on v4

--- a/solution.py
+++ b/solution.py
@@ -105,10 +105,14 @@
     out["q"] = out["act_q"] * out["inv_q"] * dk ** (-0.5)
     out["k"] = out["act_k"] * out["inv_k"]
     out["v"] = out["act_v"]
-    pair = jnp.transpose(pair_ref[...])
-    picked = iota(pair.shape, 0)
-    a_row = jnp.sum(jnp.where(picked == 2 * head, pair, 0.0), axis=0, keepdims=True)
-    b_row = jnp.sum(jnp.where(picked == 2 * head + 1, pair, 0.0), axis=0, keepdims=True)
+    picked = (iota((8, 128), 1) == 2 * head + iota((8, 128), 0)).astype(BF16)
+    pair = jnp.zeros((8, length), F32)
+    rest = pair_ref[...]
+    for _ in range(3):
+        high = rest.astype(BF16)
+        rest = rest - high.astype(F32)
+        pair = pair + lax.dot_general(picked, high, NT, preferred_element_type=F32)
+    a_row, b_row = pair[0:1], pair[1:2]
     rate = jnp.exp(jnp.full((1, length), head_table[0, head], F32))
     a_row = a_row + head_table[1, head]
     softplus = jnp.maximum(a_row, 0.0) + jnp.log1p(jnp.exp(-jnp.abs(a_row)))
@@ -123,13 +127,18 @@
     for i in range(1, chunks):
         last = jnp.where(place >= i * chunk, ends[i], jnp.broadcast_to(last, (1, length)))
     tail = jnp.exp(last - total) * row_info[1:2]
-    rows = jnp.concatenate([beta, total, entry, tail, jnp.zeros((124, length), F32)], axis=0)
+    rows = jnp.concatenate([beta, total, entry, tail, a_row, decay, jnp.zeros((2, length), F32)], axis=0)
     cols = jnp.transpose(rows)
-    out.update(
-        a_row=a_row, rate=rate, decay=decay, beta_row=beta, total_row=total, entry_row=entry, tail_row=tail,
+    out.update(rows=rows, cols=cols)
+    out.update(named_parts(rows, cols))
+    return out
+
+
+def named_parts(rows, cols):
+    return dict(
+        total_row=rows[1:2], entry_row=rows[2:3],
         beta=cols[:, 0:1], total=cols[:, 1:2], entry=cols[:, 2:3], tail=cols[:, 3:4],
     )
-    return out
 
 
 def chunk_parts(pre, i, chunk, col_info, row_info):
@@ -149,15 +158,26 @@
     )
 
 
+def silu_grad(pre, sig):
+    return sig * (1.0 + pre * (1.0 - sig))
+
+
 def forward_kernel(
     chunk, refine, qref, kref, vref, gref, pair_ref, tap_qk, tap_v, head_table, gain, col_ref, row_ref,
-    mix_ref, rec_ref, fix_ref, inv_ref, state_ref,
+    mix_ref, rec_ref, fix_ref, inv_ref, state_ref, act_ref, slope_ref, cols_ref, rows_ref,
 ):
     head = pl.program_id(1)
     col_info, row_info = col_ref[0], row_ref[0]
     pre = prepared(head, chunk, qref, kref, vref, pair_ref, tap_qk, tap_v, head_table, col_info, row_info)
     length, dk = qref.shape
     dv = vref.shape[1]
+    for name, start, width in (("q", 0, dk), ("k", dk, dk), ("v", 2 * dk, dv)):
+        act_ref[:, start : start + width] = pre[name]
+        slope_ref[:, start : start + width] = silu_grad(pre["pre_" + name], pre["sig_" + name]).astype(BF16)
+    cols_ref[0, 0] = pre["cols"]
+    cols_ref[0, 0, :, 4:5] = pre["inv_q"]
+    cols_ref[0, 0, :, 5:6] = pre["inv_k"]
+    rows_ref[0, 0] = pre["rows"]
     chunks = length // chunk
     parts = [chunk_parts(pre, i, chunk, col_info, row_info) for i in range(chunks)]
     inverses = unit_lower_inverse([p["lower"] for p in parts], refine)
@@ -187,20 +207,20 @@
         mix_ref[s, :] = (normal * gain_row * (gate * lax.logistic(gate))).astype(BF16)
 
 
-def silu_grad(pre, sig):
-    return sig * (1.0 + pre * (1.0 - sig))
-
-
 def backward_kernel(
     chunk, heads, qref, kref, vref, gref, pair_ref, tap_qk, tap_v, head_table, gain, col_ref, row_ref,
-    rec_ref, fix_ref, inv_ref, state_ref, dmix_ref,
+    rec_ref, fix_ref, inv_ref, state_ref, act_ref, slope_ref, cols_ref, rows_ref, dmix_ref,
     dproj_ref, dtap_qk, dtap_v, dhead_ref, dgain_ref,
 ):
     seq, head = pl.program_id(0), pl.program_id(1)
     col_info, row_info = col_ref[0], row_ref[0]
-    pre = prepared(head, chunk, qref, kref, vref, pair_ref, tap_qk, tap_v, head_table, col_info, row_info)
     length, dk = qref.shape
     dv = vref.shape[1]
+    rows, cols = rows_ref[0, 0], cols_ref[0, 0]
+    pre = dict(q=act_ref[:, :dk], k=act_ref[:, dk : 2 * dk], v=act_ref[:, 2 * dk :], **named_parts(rows, cols))
+    rate = jnp.exp(jnp.full((1, length), head_table[0, head], F32))
+    masks = [jnp.broadcast_to(col_info[:, j : j + 1], (length, dk)) for j in range(3)]
+    wide = [jnp.concatenate([m] * (dv // dk), axis=1) for m in masks]
     chunks = length // chunk
     parts = [chunk_parts(pre, i, chunk, col_info, row_info) for i in range(chunks)]
     gain_row = gain[...]
@@ -236,7 +256,7 @@
     for p in reversed(parts):
         p["dstate"] = dstate
         dstate = p["exit"] * dstate - mm(p["ahead"], dstate, NN) + p["given"]
-    cols = iota((chunk, 8), 1)
+    lane = iota((chunk, 8), 1)
     col_parts, row_parts, dqs, dks, dvs = [], [], [], [], []
     for i, p in enumerate(parts):
         s = p["rows"]
@@ -272,18 +292,17 @@
         end = end + jnp.sum(dtail, axis=0, keepdims=True)
         dtotal = dtotal + jnp.where(iota((chunk, 1), 0) == chunk - 1, end, 0.0)
         row_parts.append(jnp.sum(high, axis=0, keepdims=True))
-        col_parts.append(jnp.where(cols == 0, dtotal, jnp.where(cols == 1, dbeta, 0.0)))
-    lanes = jnp.concatenate(col_parts, axis=0)
-    lanes = jnp.concatenate([lanes, jnp.zeros((length, 120), F32)], axis=1)
-    turned = jnp.transpose(lanes)
+        col_parts.append(jnp.where(lane == 0, dtotal, jnp.where(lane == 1, dbeta, 0.0)))
+    turned = jnp.transpose(jnp.concatenate(col_parts, axis=0))
     dtotal_row = turned[0:1] - jnp.concatenate(row_parts, axis=1)
     dbeta_row = turned[1:2]
     ddecay = chunk_scan(dtotal_row, chunk, backward=True)
-    da = -ddecay * pre["rate"] * lax.logistic(pre["a_row"])
-    db = dbeta_row * pre["beta_row"] * (1.0 - pre["beta_row"])
-    spread = iota((128, length), 0)
-    dpair = jnp.where(spread == 2 * head, da, jnp.where(spread == 2 * head + 1, db, 0.0))
-    dpair = jnp.transpose(dpair).astype(BF16)
+    da = -ddecay * rate * lax.logistic(rows[4:5])
+    db = dbeta_row * rows[0:1] * (1.0 - rows[0:1])
+    which = iota((8, length), 0)
+    both = jnp.transpose(jnp.where(which == 0, da, jnp.where(which == 1, db, 0.0)))
+    spread = iota((length, 128), 1)
+    dpair = jnp.where(spread == 2 * head, both[:, 0:1], jnp.where(spread == 2 * head + 1, both[:, 1:2], 0.0)).astype(BF16)
 
     @pl.when(head == 0)
     def _():
@@ -293,29 +312,30 @@
     def _():
         dproj_ref[:, p_at:] = dproj_ref[:, p_at:] + dpair
 
-    dscale = jnp.sum(ddecay * pre["decay"], axis=1, keepdims=True)
+    dscale = jnp.sum(ddecay * rows[5:6], axis=1, keepdims=True)
     dbias = jnp.sum(da, axis=1, keepdims=True)
     which = iota((8, 128), 0)
     dhead = jnp.where(which == 0, dscale, jnp.where(which == 1, dbias, 0.0))
     dq, dk_all, dv_all = (jnp.concatenate(x, axis=0) for x in (dqs, dks, dvs))
 
-    def through_norm(grad, act, inv, factor):
-        return factor * (inv * grad - act * (inv * inv * inv) * jnp.sum(grad * act, axis=1, keepdims=True))
-
-    dq = through_norm(dq, pre["act_q"], pre["inv_q"], dk ** (-0.5))
-    dk_all = through_norm(dk_all, pre["act_k"], pre["inv_k"], 1.0)
+    def through_norm(grad, unit, inv, factor):
+        along = jnp.sum(grad * unit, axis=1, keepdims=True) * factor ** (-2)
+        return (factor * inv) * (grad - unit * along)
+
+    dq = through_norm(dq, pre["q"], cols[:, 4:5], dk ** (-0.5))
+    dk_all = through_norm(dk_all, pre["k"], cols[:, 5:6], 1.0)
     taps_out = []
-    for grad, name, src, taps, masks, at in (
-        (dq, "q", qref, tap_qk[0], pre["masks"], head * dk),
-        (dk_all, "k", kref, tap_qk[1], pre["masks"], heads * dk + head * dk),
-        (dv_all, "v", vref, tap_v[...], pre["wide"], v_at + head * dv),
+    for grad, where, src, taps, kept, at in (
+        (dq, 0, qref, tap_qk[0], masks, head * dk),
+        (dk_all, dk, kref, tap_qk[1], masks, heads * dk + head * dk),
+        (dv_all, 2 * dk, vref, tap_v[...], wide, v_at + head * dv),
     ):
-        dpre = grad * silu_grad(pre["pre_" + name], pre["sig_" + name])
+        dpre = grad * slope_ref[:, where : where + grad.shape[1]].astype(F32)
         signal = src[...]
         dsignal = dpre * taps[0:1]
         dtaps = [jnp.sum(dpre * signal, axis=0, keepdims=True)]
         for j in range(1, 4):
-            masked = dpre * masks[j - 1]
+            masked = dpre * kept[j - 1]
             dsignal = dsignal + shifted_rows(masked, -j) * taps[j : j + 1]
             dtaps.append(jnp.sum(masked * shifted_rows(signal, j), axis=0, keepdims=True))
         width = grad.shape[1]
@@ -345,25 +365,6 @@
     ]
 
 
-def segment_tables(segment_ids, chunk):
-    seqs, length = segment_ids.shape
-    place = jnp.arange(length)
-    conv_masks = []
-    for j in range(1, 4):
-        earlier = jnp.pad(segment_ids, ((0, 0), (j, 0)), constant_values=-1)[:, :length]
-        conv_masks.append(earlier == segment_ids)
-    blocks = segment_ids.reshape(seqs, length // chunk, chunk)
-    finals = blocks[:, :, -1]
-    before = jnp.concatenate([segment_ids[:, :1], finals[:, :-1]], axis=1)
-    carried = (blocks == before[:, :, None]).reshape(seqs, length)
-    tailed = (blocks == finals[:, :, None]).reshape(seqs, length)
-    zero = jnp.zeros((seqs, length), F32)
-    ids = segment_ids.astype(F32)
-    rows = jnp.stack([carried.astype(F32), tailed.astype(F32), ids] + [zero] * 5, axis=1)
-    cols = jnp.stack([m.astype(F32) for m in conv_masks] + [ids] + [zero] * 4, axis=2)
-    return cols, rows
-
-
 def delta_forward(proj, taps_qk, taps_v, head_table, gain, tables, seqs, heads, chunk, refine):
     cols, rows = tables
     length = cols.shape[1]
@@ -379,6 +380,10 @@
             column, column, column,
             pl.BlockSpec((1, 1, chunks, chunk, chunk), lambda s, h: (s, h, 0, 0, 0)),
             pl.BlockSpec((1, 1, chunks, dk, dv), lambda s, h: (s, h, 0, 0, 0)),
+            pl.BlockSpec((length, 2 * dk + dv), lambda s, h: (s, h)),
+            pl.BlockSpec((length, 2 * dk + dv), lambda s, h: (s, h)),
+            pl.BlockSpec((1, 1, length, 8), lambda s, h: (s, h, 0, 0)),
+            pl.BlockSpec((1, 1, 8, length), lambda s, h: (s, h, 0, 0)),
         ],
         out_shape=[
             jax.ShapeDtypeStruct((tokens, heads * dv), BF16),
@@ -386,6 +391,10 @@
             pltpu.HBM((tokens, heads * dv), F32),
             pltpu.HBM((seqs, heads, chunks, chunk, chunk), F32),
             pltpu.HBM((seqs, heads, chunks, dk, dv), F32),
+            pltpu.HBM((tokens, heads * (2 * dk + dv)), F32),
+            pltpu.HBM((tokens, heads * (2 * dk + dv)), BF16),
+            pltpu.HBM((seqs, heads, length, 8), F32),
+            pltpu.HBM((seqs, heads, 8, length), F32),
         ],
         compiler_params=pltpu.CompilerParams(vmem_limit_bytes=48 * 2**20),
         cost_estimate=cost(15),
@@ -409,6 +418,10 @@
             column, column,
             pl.BlockSpec((1, 1, chunks, chunk, chunk), lambda s, h: (s, h, 0, 0, 0)),
             pl.BlockSpec((1, 1, chunks, dk, dv), lambda s, h: (s, h, 0, 0, 0)),
+            pl.BlockSpec((length, 2 * dk + dv), lambda s, h: (s, h)),
+            pl.BlockSpec((length, 2 * dk + dv), lambda s, h: (s, h)),
+            pl.BlockSpec((1, 1, length, 8), lambda s, h: (s, h, 0, 0)),
+            pl.BlockSpec((1, 1, 8, length), lambda s, h: (s, h, 0, 0)),
             column,
         ],
         out_specs=[
@@ -644,10 +657,14 @@
             recv_sem=self.far_recv.at[slot], device_id={"dp": 2 * to + self.parity}, device_id_type=MESH,
         )
 
-    def start(self, m):
-        self.near_copy(m).start()
-
-    def turn(self, m):
+    def order(self, i):
+        return lax.rem(lax.div(self.mine, self.group) + 1 + i, 4)
+
+    def start(self, i):
+        self.near_copy(self.order(i)).start()
+
+    def turn(self, i):
+        m = self.order(i)
         self.near_copy(m).wait_recv()
         rows = self.near.shape[1]
         step = 16
@@ -762,9 +779,15 @@
         self.over_others(step)
 
     def finish(self):
+        self.receive()
+        self.drain()
+
+    def receive(self):
         other = 1 - self.parity
         self.over_others(lambda j: self.near_copy(j, other).wait_recv())
         self.near_copy(self.mine, other).wait_recv()
+
+    def drain(self):
         self.over_others(lambda j: self.far_copy(self.me, j, self.mine).wait_send())
         self.over_others(lambda j: self.near_copy(j, self.parity).wait_send())
         self.near_copy(self.mine, self.parity).wait_send()
@@ -848,6 +871,18 @@
         part[k, h, :, :, pl.ds(n, 256)] = value.astype(BF16).reshape(4, left.shape[0] // 4, 256)
 
     for_tiles(weight.shape[0], 256, step)
+
+
+def partial_sums_of(left, weight, start, part, k, h):
+    devices, own, _ = weight.shape
+    stop = start + left.shape[1]
+
+    def step(n):
+        tile = weight[pl.ds(lax.div(n, own), 256 // own), :, start:stop].reshape(256, stop - start)
+        value = lax.dot_general(left, tile, NT, preferred_element_type=F32)
+        part[k, h, :, :, pl.ds(n, 256)] = value.astype(BF16).reshape(4, left.shape[0] // 4, 256)
+
+    for_tiles(devices * own, 256, step)
 
 
 def row_grads(left, right, out, column):
@@ -954,17 +989,38 @@
     )(*[turn(w) for w in weights])
 
 
-def start_kernel(in_places, rest_places, rows, cot, gain, *refs):
+def tables_into(segments, chunk, cols, rows):
+    length = segments.shape[1]
+    place = iota((1, length), 1)
+    for s in range(segments.shape[0]):
+        ids = segments[s : s + 1, :].astype(F32)
+        masks = [
+            jnp.where((pltpu.roll(ids, j, 1) == ids) & (place >= j), 1.0, 0.0) for j in range(1, 4)
+        ]
+        before, final = ids[:, :1], ids[:, chunk - 1 : chunk]
+        before, final = (jnp.broadcast_to(x, (1, length)) for x in (before, final))
+        for i in range(1, length // chunk):
+            before = jnp.where(place >= i * chunk, ids[:, i * chunk - 1 : i * chunk], before)
+            final = jnp.where(place >= i * chunk, ids[:, (i + 1) * chunk - 1 : (i + 1) * chunk], final)
+        carried, tailed = (jnp.where(ids == x, 1.0, 0.0) for x in (before, final))
+        rows[s] = jnp.concatenate([carried, tailed, ids, jnp.zeros((5, length), F32)], axis=0)
+        cols[s] = jnp.transpose(jnp.concatenate(masks + [ids, jnp.zeros((4, length), F32)], axis=0))
+
+
+def start_kernel(chunk, in_places, rest_places, rows, cot, gain, segments, *refs):
     first, second = len(in_places), len(rest_places)
     sources, refs = refs[: first + second], refs[first + second :]
     (normed, cot_all, w_in), refs = refs[:3], refs[3:]
-    low, refs = refs[: 2 * (LAYERS - 1)], refs[2 * (LAYERS - 1) :]
-    held, (in_sems, rest_sems, send_sem, recv_sem, *spread_sems) = refs[: first + second], refs[first + second :]
+    (low_down, table_cols, table_rows), refs = refs[:3], refs[3:]
+    low, refs = refs[: 2 * LAYERS - 2], refs[2 * LAYERS - 2 :]
+    held, (in_sems, rest_sems, down_sem, send_sem, recv_sem, *spread_sems) = refs[: first + second], refs[first + second :]
     in_refs = sources[:first], held[:first], in_sems
     rest_refs = sources[first:], held[first:], rest_sems
     line = Line(send_sem, recv_sem)
     spread = Spread(w_in, *spread_sems)
+    down_refs = sources[-1:], held[-1:], down_sem
     fetch_start(*in_refs, 0)
+    fetch_start(*down_refs, 0)
     line.greet()
     others = spread.greet()
     cast_into(w_in.at[spread.me], *in_refs, 0, in_places)
@@ -976,6 +1032,8 @@
     both = [(k + h, blocks_of(ref, h)) for k, ref in ((0, normed), (2, cot_all)) for h in range(HALVES)]
     for item in both:
         line.gather_start(*item)
+    tables_into(segments, chunk, table_cols, table_rows)
+    cast_into(low_down, *down_refs, 0, rest_places[-1:])
     for l in range(1, LAYERS):
         fetch_start(*in_refs, l)
         fetch_start(*rest_refs, l)
@@ -994,37 +1052,45 @@
 
 
 def slices_of(weights, v_width, wide):
-    return (
-        weights.at[:, :v_width],
-        weights.at[:, v_width : v_width + 2 * wide],
-        weights.at[:, v_width + 2 * wide :],
-    )
-
-
-def ffn_forward_kernel(last, mixer, weights, rows, gain, gain_next, middle, normed, pre, hidden, out_rows, *rest):
+    return weights.at[:, :v_width], weights.at[:, v_width : v_width + 2 * wide]
+
+
+def ffn_forward_kernel(last, reads, writes, mixer, weights, rows, gain, gain_next, down, middle, normed, pre, hidden, out_rows, *rest):
     if last:
         part, slots, total, send_sem, recv_sem = rest
     else:
-        normed_next, part, slots, total, send_sem, recv_sem, gate = rest
+        normed_next, whole_down, part, slots, total, send_sem, recv_sem, *spread_sems, gate = rest
     line = Line(send_sem, recv_sem)
     wide = hidden.shape[3]
-    w_out, w_up, w_down = slices_of(weights, mixer.shape[3], wide)
+    w_out, w_up = slices_of(weights, mixer.shape[3], wide)
     block = rows.shape[1]
     line.greet()
+    for copy in reads[:2]:
+        copy.wait()
     if last:
         partial_sums(half_of(mixer, 0), w_out, part, 0, 0)
         line.meet()
     else:
         turns = Turns(gate)
-        turns.greet()
+        spread = Spread(whole_down, *spread_sems)
+        others = spread.greet()
+        whole_down[spread.me] = down[...]
         partial_sums(half_of(mixer, 0), w_out, part, 0, 0)
-        line.meet(1)
+        line.meet(others)
+        spread.start()
+
+        @pl.when(turns.second == 1)
+        def _():
+            spread.forward()
+
         turns.wait()
     line.scatter_start(0, *parts_of(part, slots, 0, 0))
     partial_sums(half_of(mixer, 1), w_out, part, 0, 1)
     line.scatter_relay(0, *parts_of(part, slots, 0, 0))
     line.scatter_start(1, *parts_of(part, slots, 0, 1))
     line.scatter_relay(1, *parts_of(part, slots, 0, 1))
+    for copy in reads[2:]:
+        copy.wait()
     for h in range(HALVES):
         both = parts_of(part, slots, 0, h)
         line.scatter_wait(h, *both)
@@ -1033,6 +1099,7 @@
         middle[h] = value
         normed[line.me, h] = rms(value, gain[...]).astype(BF16)
         line.gather_start(2 + h, blocks_of(normed, h))
+    writes[0].start()
     line.gather_forward(2, blocks_of(normed, 0))
     for h in range(HALVES):
         if h == 1:
@@ -1051,10 +1118,22 @@
             hidden[:, h, :, pl.ds(n, 256)] = value.astype(BF16).reshape(4, block, 256)
 
         for_tiles(wide, 256, step)
-        partial_sums(half_of(hidden, h), w_down, part, 1, h)
+        if last:
+            partial_sums_of(half_of(hidden, h), down, down.shape[2] - wide, part, 1, h)
+        else:
+            if h == 0:
+                @pl.when(turns.second == 0)
+                def _():
+                    spread.forward()
+
+                spread.receive()
+                writes[6].start()
+            partial_sums_of(half_of(hidden, h), whole_down, 0, part, 1, h)
         if h == 1:
             line.scatter_relay(4, *parts_of(part, slots, 1, 0))
         line.scatter_start(4 + h, *parts_of(part, slots, 1, h))
+    for copy in writes[1:4]:
+        copy.start()
     line.scatter_relay(5, *parts_of(part, slots, 1, 1))
     for h in range(HALVES):
         both = parts_of(part, slots, 1, h)
@@ -1068,17 +1147,23 @@
     if not last:
         for h in range(HALVES):
             line.gather_forward(6 + h, blocks_of(normed_next, h))
+        writes[4].start()
         for h in range(HALVES):
             line.gather_wait(6 + h, blocks_of(normed_next, h))
+        writes[5].start()
+    else:
+        writes[4].start()
     for h in range(HALVES):
         line.scatter_drain(h, *parts_of(part, slots, 0, h))
         line.gather_drain(2 + h, blocks_of(normed, h))
         line.scatter_drain(4 + h, *parts_of(part, slots, 1, h))
         if not last:
             line.gather_drain(6 + h, blocks_of(normed_next, h))
-
-
-def ffn_backward_kernel(owes, cot, hidden, pre, normed, middle, grad, gain, weights, *rest):
+    if not last:
+        spread.drain()
+
+
+def ffn_backward_kernel(owes, reads, writes, cot, hidden, pre, normed, middle, grad, gain, weights, down, *rest):
     if owes:
         owed, d_mixer, grads, mixer_cot, grad_out, d_gain, summed, *rest = rest
     else:
@@ -1090,19 +1175,25 @@
         sums = Sums(owed, near, far, near_send, near_recv, far_send, far_recv)
     line = Line(send_sem, recv_sem)
     wide = hidden.shape[3]
-    w_out, w_up, w_down = slices_of(weights, d_mixer.shape[3], wide)
+    w_out, w_up = slices_of(weights, d_mixer.shape[3], wide)
+    down_at = down.shape[2] - wide
     block = middle.shape[1]
     line.greet()
     if owes:
         sums.greet_late(gate)
+        reads[8].wait()
         sums.meet_late(line)
     else:
         line.meet()
+    for copy in reads[:2]:
+        copy.wait()
     for h in range(HALVES):
+        reads[2 + h].wait()
         left = half_of(cot, h)
 
         def step(n):
-            d_hidden = jnp.dot(left, w_down[:, pl.ds(n, 256)], preferred_element_type=F32)
+            tile = down[:, :, pl.ds(down_at + n, 256)].reshape(left.shape[1], 256)
+            d_hidden = jnp.dot(left, tile, preferred_element_type=F32)
             gate = pre[:, h, :, pl.ds(n, 256)].reshape(4 * block, 256)
             up = pre[:, h, :, pl.ds(n + wide, 256)].reshape(4 * block, 256)
             sig = lax.logistic(gate)
@@ -1112,10 +1203,14 @@
             d_pre[:, h, :, pl.ds(n + wide, 256)] = d_up.astype(BF16).reshape(4, block, 256)
 
         for_tiles(wide, 256, step)
+        if h == 0:
+            reads[4].wait()
         partial_sums(half_of(d_pre, h), w_up, part, 0, h)
         if h == 1:
             line.scatter_relay(0, *parts_of(part, slots, 0, 0))
         line.scatter_start(h, *parts_of(part, slots, 0, h))
+    for copy in reads[5:8]:
+        copy.wait()
     if owes:
         @pl.when(sums.parity == 1)
         def _():
@@ -1148,12 +1243,16 @@
     line.gather_forward(2, blocks_of(mixer_cot, 0))
     line.gather_forward(3, blocks_of(mixer_cot, 1))
     run_pieces(pieces, 3, 4)
+    writes[0].start()
+    writes[1].start()
     for h in range(HALVES):
         line.gather_wait(2 + h, blocks_of(mixer_cot, h))
         left = half_of(mixer_cot, h)
         for n in range(0, w_out.shape[1], 256):
             value = jnp.dot(left, w_out[:, n : n + 256], preferred_element_type=F32)
             d_mixer[:, h, :, n : n + 256] = value.reshape(4, block, 256)
+        writes[2 + h].start()
+    writes[4].start()
     for h in range(HALVES):
         line.scatter_drain(h, *parts_of(part, slots, 0, h))
         line.gather_drain(2 + h, blocks_of(mixer_cot, h))
@@ -1162,20 +1261,25 @@
 
 
 def mixer_backward_kernel(
-    d_proj, w_in, normed, mixer, mixer_cot, rows, grad, gain,
+    reads, writes, d_proj, w_in, normed, mixer, mixer_cot, rows, grad, gain,
     grad_out, d_gain, grads, cot, part, slots, total, send_sem, recv_sem,
 ):
     line = Line(send_sem, recv_sem)
     line.greet()
     line.meet()
+    reads[0].wait()
+    reads[1].wait()
     partial_sums(half_of(d_proj, 0), w_in, part, 0, 0)
     line.scatter_start(0, *parts_of(part, slots, 0, 0))
+    reads[2].wait()
     partial_sums(half_of(d_proj, 1), w_in, part, 0, 1)
     line.scatter_relay(0, *parts_of(part, slots, 0, 0))
     line.scatter_start(1, *parts_of(part, slots, 0, 1))
     line.scatter_relay(1, *parts_of(part, slots, 0, 1))
     width = mixer.shape[3]
     pieces = [row_grads(mixer_cot, mixer, grads, 0), row_grads(normed, d_proj, grads, width)]
+    for copy in reads[3:]:
+        copy.wait()
     run_pieces(pieces, 0, 2)
     d_gain[...] = jnp.zeros_like(d_gain)
     for h in range(HALVES):
@@ -1192,14 +1296,17 @@
     line.gather_forward(2, blocks_of(cot, 0))
     line.gather_forward(3, blocks_of(cot, 1))
     run_pieces(pieces, 3, 4)
+    writes[0].start()
+    writes[1].start()
     for h in range(HALVES):
         line.gather_wait(2 + h, blocks_of(cot, h))
+    writes[2].start()
     for h in range(HALVES):
         line.scatter_drain(h, *parts_of(part, slots, 0, h))
         line.gather_drain(2 + h, blocks_of(cot, h))
 
 
-def last_kernel(heads, d_proj, w_in, normed, mixer, mixer_cot, rows, grad, gain, *refs):
+def last_kernel(heads, reads, writes, d_proj, w_in, normed, mixer, mixer_cot, rows, grad, gain, *refs):
     smalls, refs = refs[: 5 * LAYERS + LAYERS - 1], refs[5 * LAYERS + LAYERS - 1 :]
     per_layer = [smalls[5 * l : 5 * l + 5] for l in range(LAYERS)]
     first_gains = smalls[5 * LAYERS :]
@@ -1234,19 +1341,25 @@
         line_land[line.me, 2 * LAYERS + l : 2 * LAYERS + l + 1, : value.shape[1]] = value
         if l > 0:
             line_land[line.me, 2 * l : 2 * l + 1, :] = first_gains[l - 1][...]
+    reads[0].wait()
+    reads[1].wait()
     partial_sums(half_of(d_proj, 0), w_in, part, 0, 0)
     line.meet(others)
     line.scatter_start(0, *parts_of(part, slots, 0, 0))
     small_taps.start()
     width = mixer.shape[3]
     pieces = [row_grads(mixer_cot, mixer, grads, 0), row_grads(normed, d_proj, grads, width)]
-    run_pieces(pieces, 0, 1)
+    for copy in reads[2:]:
+        copy.wait()
+    for piece in pieces:
+        piece(sums.order(0))
     sums.start(0)
     line.scatter_relay(0, *parts_of(part, slots, 0, 0))
     partial_sums(half_of(d_proj, 1), w_in, part, 0, 1)
     line.scatter_start(1, *parts_of(part, slots, 0, 1))
     for m in range(1, 4):
-        run_pieces(pieces, m, m + 1)
+        for piece in pieces:
+            piece(sums.order(m))
         sums.start(m)
         sums.turn(m - 1)
     line.scatter_relay(1, *parts_of(part, slots, 0, 1))
@@ -1274,19 +1387,70 @@
 DMA = pltpu.SemaphoreType.DMA
 
 
-def line_call(kernel, operands, outs, scratch, number, name, micros, spaces=None):
+def line_call(kernel, operands, outs, scratch, number, name, micros, spaces=None, fetches=(), puts=()):
+    staged_in = sorted({i for i, _ in fetches})
+    staged_out = sorted({i for i, _ in puts})
+    count_in, count_out, count = len(operands), len(outs), len(scratch)
+    held = [pltpu.VMEM(operands[i].shape, operands[i].dtype) for i in staged_in]
+    held += [pltpu.VMEM(*outs[i]) for i in staged_out]
+    if fetches or puts:
+        held += [DMA((len(fetches),)), DMA((len(puts),))]
+
+    def staged(*refs):
+        ins, results = list(refs[:count_in]), list(refs[count_in : count_in + count_out])
+        own = refs[count_in + count_out : count_in + count_out + count]
+        *arrays, in_sems, out_sems = refs[count_in + count_out + count :]
+        sources, targets = list(ins), list(results)
+        for i, ref in zip(staged_in, arrays):
+            ins[i] = ref
+        for i, ref in zip(staged_out, arrays[len(staged_in) :]):
+            results[i] = ref
+        reads = [
+            pltpu.make_async_copy(cut(sources[i]), cut(ins[i]), in_sems.at[j]) for j, (i, cut) in enumerate(fetches)
+        ]
+        writes = [
+            pltpu.make_async_copy(cut(results[i]), cut(targets[i]), out_sems.at[j]) for j, (i, cut) in enumerate(puts)
+        ]
+        for copy in reads:
+            copy.start()
+        kernel(reads, writes, *ins, *results, *own)
+        for copy in writes:
+            copy.wait()
+
+    spaces = list(spaces or [pltpu.VMEM] * count_in)
+    out_spaces = [pltpu.VMEM] * count_out
+    for i in staged_in:
+        spaces[i] = pl.ANY
+    for i in staged_out:
+        out_spaces[i] = pl.ANY
     return pl.pallas_call(
-        kernel,
-        in_specs=[pl.BlockSpec(memory_space=s) for s in spaces or [pltpu.VMEM] * len(operands)],
-        out_specs=[pl.BlockSpec(memory_space=pltpu.VMEM)] * len(outs),
+        staged if fetches or puts else kernel,
+        in_specs=[pl.BlockSpec(memory_space=s) for s in spaces],
+        out_specs=[pl.BlockSpec(memory_space=s) for s in out_spaces],
         out_shape=[jax.ShapeDtypeStruct(*out) for out in outs],
-        scratch_shapes=scratch,
+        scratch_shapes=list(scratch) + held,
         compiler_params=pltpu.CompilerParams(
             collective_id=number, has_side_effects=True, vmem_limit_bytes=VMEM_LIMIT
         ),
         cost_estimate=cost(micros),
         name=name,
     )(*operands)
+
+
+def every(ref):
+    return ref
+
+
+def columns_cut(start, stop):
+    return lambda ref: ref.at[:, start:stop]
+
+
+def last_cut(start):
+    return lambda ref: ref.at[:, :, start:]
+
+
+def half_cut(h):
+    return lambda ref: ref.at[:, h]
 
 
 def line_scratch(sums, block, width, phases):
@@ -1307,41 +1471,49 @@
     ]
 
 
-def start_call(rows, cot, gain, in_weights, rest_weights, rest_units, dp):
+def start_call(rows, cot, gain, segments, chunk, in_weights, rest_weights, rest_units, dp):
     _, block, width = rows.shape
     in_places = cast_places(in_weights, (128,) * len(in_weights))
     rest_places = cast_places(rest_weights, rest_units)
     own = in_weights[0].shape[1]
     in_width, rest_width = (sum(p[2] for p in places) for places in (in_places, rest_places))
     whole = ((4, HALVES, block, width), BF16)
-    outs = [whole, whole, ((dp, own, in_width), BF16)]
+    outs = [whole, whole, ((dp, own, in_width), BF16), ((own, rest_places[-1][2]), BF16)]
+    seqs, length = segments.shape
+    outs += [((seqs, length, 8), F32), ((seqs, 8, length), F32)]
     outs += [((own, in_width), BF16), ((own, rest_width), BF16)] * (LAYERS - 1)
     half = dp // 2
     scratch = [pltpu.VMEM(held_shape(w), F32) for w in in_weights + rest_weights] + [
-        DMA((len(in_weights),)), DMA((len(rest_weights),)),
+        DMA((len(in_weights),)), DMA((len(rest_weights),)), DMA((1,)),
         DMA((4, 4)), DMA((4, 5)), DMA((half,)), DMA((half,)), DMA((half,)), DMA((half,)),
     ]
     return line_call(
-        functools.partial(start_kernel, in_places, rest_places),
-        (rows, cot, gain, *[turn(w) for w in in_weights + rest_weights]), outs, scratch, 1, "start", 35,
-        [pltpu.VMEM] * 3 + [pl.ANY] * len(in_weights + rest_weights),
+        functools.partial(start_kernel, chunk, in_places, rest_places),
+        (rows, cot, gain, segments, *[turn(w) for w in in_weights + rest_weights]), outs, scratch, 1, "start", 35,
+        [pltpu.VMEM] * 4 + [pl.ANY] * len(in_weights + rest_weights),
     )
 
 
-def ffn_forward_call(mixer, weights, rows, gain, gain_next, layer, last):
+def ffn_forward_call(mixer, weights, down, rows, gain, gain_next, layer, last, dp, wide):
     _, block, width = rows.shape
-    wide = (weights.shape[1] - mixer.shape[3]) // 3
+    up_at = mixer.shape[3]
     own, whole = ((HALVES, block, width), F32), ((4, HALVES, block, width), BF16)
     outs = [own, whole, ((4, HALVES, block, 2 * wide), F32), ((4, HALVES, block, wide), BF16), own]
-    if not last:
-        outs.append(whole)
+    scratch = line_scratch(2, block, width, 8)
+    fetches = [(0, every), (1, columns_cut(0, up_at)), (2, every), (1, columns_cut(up_at, up_at + 2 * wide))]
+    if last:
+        fetches.append((5, last_cut(down.shape[2] - wide)))
+    else:
+        outs += [whole, ((dp,) + down.shape, BF16)]
+        half = dp // 2
+        scratch += [DMA((half,)), DMA((half,)), DMA((half,)), DMA((half,)), pltpu.SemaphoreType.REGULAR]
     return line_call(
-        functools.partial(ffn_forward_kernel, last), (mixer, weights, rows, gain, gain_next), outs,
-        line_scratch(2, block, width, 8) + ([] if last else [pltpu.SemaphoreType.REGULAR]), 2 + layer, "ffn_forward", 65,
+        functools.partial(ffn_forward_kernel, last), (mixer, weights, rows, gain, gain_next, down), outs,
+        scratch, 2 + layer, "ffn_forward", 65, None, fetches, [(i, every) for i in range(len(outs))],
     )
 
 
-def ffn_backward_call(cot, hidden, pre, normed, middle, grad, gain, weights, v_width, grads_shape, owed, layer):
+def ffn_backward_call(cot, hidden, pre, normed, middle, grad, gain, weights, down, v_width, grads_shape, owed, layer):
     _, block, width = middle.shape
     wide = hidden.shape[3]
     whole = ((4, HALVES, block, width), BF16)
@@ -1350,14 +1522,23 @@
         ((HALVES, block, width), F32), ((1, width), F32),
     ]
     scratch = [pltpu.VMEM((4, HALVES, block, 2 * wide), BF16)] + line_scratch(1, block, width, 4)
-    operands = [cot, hidden, pre, normed, middle, grad, gain, weights]
+    operands = [cot, hidden, pre, normed, middle, grad, gain, weights, down]
     if owed is not None:
         operands.append(owed)
         outs.append((owed.shape[2:], F32))
         scratch += sums_scratch(owed.shape) + [pltpu.SemaphoreType.REGULAR]
+    up_at = v_width
+    down_at = up_at + 2 * wide
+    fetches = [
+        (8, last_cut(down.shape[2] - wide)), (0, every), (2, half_cut(0)), (2, half_cut(1)),
+        (7, columns_cut(up_at, down_at)), (1, every), (3, every), (7, columns_cut(0, up_at)),
+    ]
+    if owed is not None:
+        fetches.append((9, every))
     return line_call(
         functools.partial(ffn_backward_kernel, owed is not None), operands, outs, scratch,
-        4 + layer, "ffn_backward", 40,
+        4 + layer, "ffn_backward", 40, None, fetches,
+        [(1, every), (3, every), (0, half_cut(0)), (0, half_cut(1)), (2, every)],
     )
 
 
@@ -1369,7 +1550,9 @@
     ]
     return line_call(
         mixer_backward_kernel, (d_proj, w_in, normed, mixer, mixer_cot, rows, grad, gain), outs,
-        line_scratch(1, block, width, 4), 6 + layer, "mixer_backward", 40,
+        line_scratch(1, block, width, 4), 6 + layer, "mixer_backward", 40, None,
+        [(1, every), (0, half_cut(0)), (0, half_cut(1)), (4, every), (3, every), (2, every)],
+        [(2, every), (0, every), (3, every)],
     )
 
 
@@ -1389,25 +1572,15 @@
     return line_call(
         functools.partial(last_kernel, heads),
         (d_proj, w_in, normed, mixer, mixer_cot, rows, grad, gain, *flat), outs,
-        scratch + line_scratch(1, block, width, 2) + sums_scratch(shape), 8, "last", 40,
+        scratch + line_scratch(1, block, width, 2) + sums_scratch(shape), 8, "last", 40, None,
+        [(1, every), (0, half_cut(0)), (0, half_cut(1)), (4, every), (3, every), (2, every)],
     )
 
 
-def finish_kernel(places, heads, *refs):
-    sources, refs = refs[: 2 * LAYERS + 4], refs[2 * LAYERS + 4 :]
-    rows, grad, taps, norms = sources[2 * LAYERS :]
-    outs, refs = refs[: len(places) + 2], refs[len(places) + 2 :]
-    (conv_qk, conv_v, head, norm_gains, out_gain), refs = refs[:5], refs[5:]
-    held, sems = refs[:-1], refs[-1]
-    copies = [
-        pltpu.make_async_copy(rows, outs[len(places)], sems.at[len(places)]),
-        pltpu.make_async_copy(grad, outs[len(places) + 1], sems.at[len(places) + 1]),
-    ]
-    for copy in copies:
-        copy.start()
-    for i, (kind, width, start, turned) in enumerate(places):
-        for l in range(LAYERS):
-            source = sources[kind * LAYERS + l]
+def cut_grads(places, sources, outs, held, sems):
+    copies = []
+    for i, (width, start, turned) in enumerate(places):
+        for l, source in enumerate(sources):
             if turned:
                 tall = -(-width // 128) * 128
                 held[i][l] = jnp.transpose(source[:, start : start + tall].astype(F32))[:width]
@@ -1415,39 +1588,60 @@
                 held[i][l] = source[:, start : start + width].astype(F32)
         copies.append(pltpu.make_async_copy(held[i], outs[i], sems.at[i]))
         copies[-1].start()
-    for l in range(LAYERS):
-        top = TAP_ROWS * l
-        for i in range(2):
-            conv_qk[l, i] = taps[top + 4 * i : top + 4 * i + 4, : conv_qk.shape[3]]
-            head[l, i : i + 1, :] = taps[top + 12 : top + 13, i * heads : (i + 1) * heads]
-            norm_gains[l, i : i + 1, :] = norms[2 * l + i : 2 * l + i + 1, :]
-        conv_v[l] = taps[top + 8 : top + 12, : conv_v.shape[2]]
-        out_gain[l : l + 1, :] = norms[2 * LAYERS + l : 2 * LAYERS + l + 1, : out_gain.shape[1]]
+    return copies
+
+
+def finish_kernel(places, heads, *refs):
+    sources, refs = refs[:LAYERS], refs[LAYERS:]
+    count = len(places)
+    if heads:
+        (rows, grad, taps, norms), refs = refs[:4], refs[4:]
+        outs, refs = refs[: count + 2], refs[count + 2 :]
+        (conv_qk, conv_v, head, norm_gains, out_gain), refs = refs[:5], refs[5:]
+        copies = [
+            pltpu.make_async_copy(rows, outs[count], refs[-1].at[count]),
+            pltpu.make_async_copy(grad, outs[count + 1], refs[-1].at[count + 1]),
+        ]
+        for copy in copies:
+            copy.start()
+    else:
+        outs, refs, copies = refs[:count], refs[count:], []
+    copies += cut_grads(places, sources, outs, refs[:-1], refs[-1])
+    if heads:
+        for l in range(LAYERS):
+            top = TAP_ROWS * l
+            for i in range(2):
+                conv_qk[l, i] = taps[top + 4 * i : top + 4 * i + 4, : conv_qk.shape[3]]
+                head[l, i : i + 1, :] = taps[top + 12 : top + 13, i * heads : (i + 1) * heads]
+                norm_gains[l, i : i + 1, :] = norms[2 * l + i : 2 * l + i + 1, :]
+            conv_v[l] = taps[top + 8 : top + 12, : conv_v.shape[2]]
+            out_gain[l : l + 1, :] = norms[2 * LAYERS + l : 2 * LAYERS + l + 1, : out_gain.shape[1]]
     for copy in copies:
         copy.wait()
 
 
-def finish_call(mixer_grads, ffn_grads, rows, grad, taps, norms, places, like):
-    operands = list(mixer_grads) + list(ffn_grads) + [rows, grad, taps, norms]
-    own = mixer_grads[0].shape[0]
-    heads = like[2].shape[2]
-    full = [(LAYERS, own, width) for _, width, _ in places]
+def finish_call(sums, places, others=(), like=()):
+    own = sums[0].shape[0]
+    heads = like[2].shape[2] if like else 0
+    full = [(LAYERS, own, width) for width, _ in places]
     turned = [is_turned(shape) for shape in full]
     shapes = [(s[0], s[2], s[1]) if t else s for s, t in zip(full, turned)]
     places = [p + (t,) for p, t in zip(places, turned)]
     count = len(places)
+    direct = [array.shape for array in others[:2]]
     outs = pl.pallas_call(
         functools.partial(finish_kernel, places, heads),
-        in_specs=[pl.BlockSpec(memory_space=pltpu.VMEM)] * len(operands),
-        out_specs=[pl.BlockSpec(memory_space=pl.ANY)] * (count + 2) + [pl.BlockSpec(memory_space=pltpu.VMEM)] * 5,
-        out_shape=[jax.ShapeDtypeStruct(shape, F32) for shape in shapes + [rows.shape, grad.shape]]
+        in_specs=[pl.BlockSpec(memory_space=pltpu.VMEM)] * (len(sums) + len(others)),
+        out_specs=[pl.BlockSpec(memory_space=pl.ANY)] * (count + len(direct))
+        + [pl.BlockSpec(memory_space=pltpu.VMEM)] * len(like),
+        out_shape=[jax.ShapeDtypeStruct(shape, F32) for shape in shapes + direct]
         + [jax.ShapeDtypeStruct(array.shape, F32) for array in like],
-        scratch_shapes=[pltpu.VMEM(shape, F32) for shape in shapes] + [DMA((count + 2,))],
+        scratch_shapes=[pltpu.VMEM(shape, F32) for shape in shapes] + [DMA((count + len(direct),))],
         compiler_params=pltpu.CompilerParams(vmem_limit_bytes=VMEM_LIMIT),
+        cost_estimate=cost(3),
         name="finish",
-    )(*operands)
-    weight_grads = [jnp.swapaxes(o, 1, 2) if t else o for o, t in zip(outs[:count], turned)]
-    return outs[count], outs[count + 1], weight_grads, outs[count + 2 :]
+    )(*sums, *others)
+    return [jnp.swapaxes(o, 1, 2) if t else o for o, t in zip(outs[:count], turned)], outs[count:]
 
 
 CHUNK = 128
@@ -1481,7 +1675,6 @@
     local_rows, width = tokens.shape
     block = local_rows // HALVES
     total_rows = 4 * local_rows
-    tables = segment_tables(segment_ids, CHUNK)
 
     def gathered(matrix):
         return lax.all_gather(matrix, "dp", axis=0, tiled=True)
@@ -1508,10 +1701,14 @@
     dp = lax.axis_size("dp")
     rows = split_rows(tokens)
     cot_rows = split_rows(cotangent)
-    w_rest = [gathered(cast_call(rest_weights, rest_units, 0))]
-    normed, cot, w_in, *low = start_call(rows, cot_rows, gain_of(0, 0), in_weights, rest_weights, rest_units, dp)
+    w_rest = [gathered(cast_call(rest_weights[:3], rest_units[:3], 0))]
+    normed, cot, w_in, first_down, *low = start_call(
+        rows, cot_rows, gain_of(0, 0), segment_ids, CHUNK, in_weights, rest_weights, rest_units, dp
+    )
+    tables, low = low[:2], low[2:]
     w_in = [w_in.reshape(width, w_in.shape[2])] + [gathered(part) for part in low[::2]]
     w_rest += [gathered(part) for part in low[1::2]]
+    w_down = [first_down] + [w.reshape(dp, width // dp, w.shape[1]) for w in w_rest[1:]]
     kept = []
     for l in range(LAYERS):
         last = l == LAYERS - 1
@@ -1521,12 +1718,12 @@
         mixer = split_all(mixer)
         gain_next = gain_of(min(l + 1, LAYERS - 1), 0)
         middle, normed_ffn, pre, hidden, out_rows, *following = ffn_forward_call(
-            mixer, w_rest[l], rows, gain_of(l, 1), gain_next, l, last
+            mixer, w_rest[l], w_down[l], rows, gain_of(l, 1), gain_next, l, last, dp, hidden_pad
         )
         kept.append((rows, normed, proj, small, mixer, saved, middle, normed_ffn, pre, hidden))
         rows = out_rows
         if not last:
-            normed = following[0]
+            normed, w_down[l] = following
     output = rows
     grad = cot_rows
     grads_shape = (dp // 2, 2, width // dp)
@@ -1535,7 +1732,7 @@
     for l in reversed(range(LAYERS)):
         rows, normed, proj, small, mixer, saved, middle, normed_ffn, pre, hidden = kept[l]
         d_mixer, ffn_grad, mixer_cot, grad, second_gain, *summed = ffn_backward_call(
-            cot, hidden, pre, normed_ffn, middle, grad, gain_of(l, 1), w_rest[l], v_width, grads_shape, owed, l
+            cot, hidden, pre, normed_ffn, middle, grad, gain_of(l, 1), w_rest[l], w_down[l], v_width, grads_shape, owed, l
         )
         if summed:
             mixer_grads[l + 1] = summed[0]
@@ -1554,14 +1751,21 @@
     grad, mixer_grads[0], taps, norms = last_call(
         d_proj, w_in[0], normed, mixer, mixer_cot, rows, grad, gain_of(0, 0), smalls, first_gains[1:], grads_shape, heads
     )
-    output, grad, weight_grads, others = finish_call(
-        mixer_grads, ffn_grads, output, grad, taps, norms,
-        [(0, qk_width, v_width), (0, qk_width, v_width + qk_width), (0, v_width, v_width + 2 * qk_width),
-         (0, v_width, 2 * v_width + 2 * qk_width), (0, pair_width, 3 * v_width + 2 * qk_width), (0, v_width, 0),
-         (1, hidden_width, hidden_pad), (1, hidden_width, 2 * hidden_pad), (1, hidden_width, 0)],
+    places, start = [], v_width
+    for size in (qk_width, qk_width, v_width, v_width, pair_width):
+        places.append((size, start))
+        start += size
+    mixer_outs, others = finish_call(
+        mixer_grads, places + [(v_width, 0)], (output, grad, taps, norms),
         (conv_query_key, conv_value, head_params, norm_gains, out_gain),
     )
-    return (output.reshape(local_rows, width), grad.reshape(local_rows, width), *weight_grads, *others)
+    ffn_outs, _ = finish_call(
+        ffn_grads, [(hidden_width, hidden_pad), (hidden_width, 2 * hidden_pad), (hidden_width, 0)]
+    )
+    output, grad, *smalls = others
+    return (
+        output.reshape(local_rows, width), grad.reshape(local_rows, width), *mixer_outs, *ffn_outs, *smalls
+    )
 
 
 def solution(mesh):

time: 475 us -> 463 us (0.975)
  the two profiles are of different devices: /device:TPU:23 before, /device:TPU:0 now
where the time goes in v5:
time: 463 us; the launch traced here: 454 us
  Pallas kernels  424 us (92%)
  between operations  14.7 us (3%)
  matrix products  8.8 us (2%)
    pallas_call x7, Pallas kernels, line_call(): pl.pallas_call(staged if fetches or puts else kernel, in_specs=[pl.BlockS...  342 us
    pallas_call x2, Pallas kernels, delta_backward(): pl.pallas_call(functools.partial(backward_kernel, chunk, heads), grid=(se...  43.1 us
    pallas_call x2, Pallas kernels, delta_forward(): pl.pallas_call(functools.partial(forward_kernel, chunk, refine), grid=(se...  29.6 us
  transfers between devices with their start and end apart: 5, of which 1 were waited for; matrix products, arithmetic and copies ran while one was open for 2% of the time, Pallas kernels for 72%

profile of v5, /device:TPU:0, one launch (start us, length us, event | category | flops | bytes accessed | tf_op | source)
XLA Modules:
  0.0 454.1 jit_solution(16075286086198527851)
XLA Ops:
  7.2 0.0 all-gather.4.cloned.1.call-start
  7.2 2.2 cast.1
  9.4 0.0 all-gather.4.cloned.1.call-update
  9.5 0.0 all-gather.6.cloned.1.call-start
  9.5 1.4 slice_bitcast_fusion.4
  10.9 45.4 %start.1 = (bf16[4,2,64,1024]{3,2,1,0:T(8,128)(2,1)}, bf16[4,2,64,1024]{3,2,1,0:T(8,128)(2,1)}, bf16[8,128,1664]{2,1,0:T(8,128)(2,1)}, bf16[128,768]{1,0:T(8,128...) custom-call(bf16[2,64,1024]{2,1,0:T(8,128)(2,1)} %bitcast.62, ...), custom_call_target="tpu_custom_call" | custom-call | bytes 122500000 | tf_op jit(solution)/shard_map/start/pallas_call | solution.py:1426
  56.4 0.0 all-gather.6.cloned.1.call-update
  56.4 0.0 all-gather.8.cloned.1.call-start
  56.4 0.7 all-gather.8.cloned.1.call-update
  57.1 0.0 reduce-scatter.3.cloned.1.call-start
  57.4 4.4 fusion.1.qref.kref.vref.gref.pair_ref
  61.8 14.8 %delta_forward.2 = (bf16[512,512]{1,0:T(8,128)(2,1)S(1)}, f32[512,512]{1,0:T(8,128)}, f32[512,512]{1,0:T(8,128)}, f32[1,2,4,128,128]{4,3,2,1,0:T(8,128)}, f32[1,...) custom-call(f32[512,1664]{1,0:T(8,128)S(1)} %fusion.1.qref.kref.vref, ...), custom_call_target="tpu_custom_call" | custom-call | bytes 52500000 | tf_op jit(solution)/shard_map/delta_forward/pallas_call | solution.py:375
  76.6 0.8 copy-done.4
  77.4 62.6 %ffn_forward.2 = (f32[2,64,1024]{2,1,0:T(8,128)}, bf16[4,2,64,1024]{3,2,1,0:T(8,128)(2,1)}, f32[4,2,64,1536]{3,2,1,0:T(8,128)}, bf16[4,2,64,768]{3,2,1,0:T(8,128...) custom-call(bf16[4,2,64,512]{3,2,1,0:T(8,128)(2,1)} %bitcast.48, ...), custom_call_target="tpu_custom_call" | custom-call | bytes 227500000 | tf_op jit(solution)/shard_map/ffn_forward/pallas_call | solution.py:1426
  140.1 0.0 all-gather.6.cloned.1.call-done.refs_1_
  140.1 4.4 fusion.2.qref.kref.vref.gref.pair_ref
  144.6 14.8 %delta_forward.3 = (bf16[512,512]{1,0:T(8,128)(2,1)S(1)}, f32[512,512]{1,0:T(8,128)}, f32[512,512]{1,0:T(8,128)}, f32[1,2,4,128,128]{4,3,2,1,0:T(8,128)}, f32[1,...) custom-call(f32[512,1664]{1,0:T(8,128)S(1)} %fusion.2.qref.kref.vref, ...), custom_call_target="tpu_custom_call" | custom-call | bytes 52500000 | tf_op jit(solution)/shard_map/delta_forward/pallas_call | solution.py:375
  159.4 0.8 copy-done.5
  160.2 51.4 %ffn_forward.3 = (f32[2,64,1024]{2,1,0:T(8,128)}, bf16[4,2,64,1024]{3,2,1,0:T(8,128)(2,1)}, f32[4,2,64,1536]{3,2,1,0:T(8,128)}, bf16[4,2,64,768]{3,2,1,0:T(8,128)(2,1)}, f32[2,64,1024]{2,1,0:T(8,128)}) custom-call(bf16[4,2,64,512]{3,2,1,0:T(8,128)(2,1)} %bitcast.50, bf16[1024,2816]{1,0:T(8,128)(2,1)} %all-gather.8.cloned.1.call-done.refs_1_.refs_7_, ...), custom_call_target="tpu_custom_call" | custom-call | bytes 227500000 | tf_op jit(solution)/shard_map/ffn_forward/pallas_call | solution.py:1426
  211.6 41.9 %ffn_backward.2 = (f32[4,2,64,512]{3,2,1,0:T(8,128)}, bf16[4,2,128,2304]{3,2,1,0:T(8,128)(2,1)}, bf16[4,2,64,1024]{3,2,1,0:T(8,128)(2,1)}, f32[2,64,1024]{2,1,0:T(8,128)}, f32[1,1024]{1,0:T(1,128)}) custom-call(bf16[4,2,64,1024]{3,2,1,0:T(8,128)(2,1)} %get-tuple-element.125.refs_0_, bf16[4,2,64,768]{3,2,1,0:T(8,128)(2,1)} %get-tuple-element.129.refs_1_, ...), custom_call_target="tpu_custom_call" | custom-call | bytes 140000000 | tf_op jit(solution)/shard_map/ffn_backward/pallas_call | solution.py:1426
  253.5 0.0 reduce-scatter.3.cloned.1.call-update
  253.5 0.0 reduce-scatter.5.cloned.1.call-start
  253.5 21.6 %delta_backward.2 = (bf16[512,1664]{1,0:T(8,128)(2,1)}, f32[1,2,4,256]{3,2,1,0:T(4,128)}, f32[1,4,512]{2,1,0:T(4,128)}, f32[1,2,8,128]{3,2,1,0:T(8,128)}, f32[1,2,1,256]{3,2,1,0:T(1,128)}) custom-call(f32[512,1664]{1,0:T(8,128)} %copy-done.1, f32[512,1664]{1,0:T(8,128)} %copy-done.1, f32[512,1664]{1,0:T(8,128)} %copy-done.1, f32[512,1664]{1,0:T(8,128)} %copy-done.1, ...), custom_call_target="tpu_custom_call" | custom-call | bytes 87500000 | tf_op jit(solution)/shard_map/delta_backward/pallas_call | solution.py:413
  275.1 36.6 %mixer_backward.1 = (f32[2,64,1024]{2,1,0:T(8,128)}, f32[1,1024]{1,0:T(1,128)}, bf16[4,2,128,2176]{3,2,1,0:T(8,128)(2,1)}, bf16[4,2,64,1024]{3,2,1,0:T(8,128)(2,1)}) custom-call(bf16[4,2,64,1664]{3,2,1,0:T(8,128)(2,1)} %bitcast.66, bf16[1024,1664]{1,0:T(8,128)(2,1)} %all-gather.6.cloned.1.call-done.refs_1_, ...), custom_call_target="tpu_custom_call" | custom-call | bytes 140000000 | tf_op jit(solution)/shard_map/mixer_backward/pallas_call | solution.py:1426
  311.8 50.7 %ffn_backward.3 = (f32[4,2,64,512]{3,2,1,0:T(8,128)}, bf16[4,2,128,2304]{3,2,1,0:T(8,128)(2,1)}, bf16[4,2,64,1024]{3,2,1,0:T(8,128)(2,1)}, f32[2,64,1024]{2,1,0:...) custom-call(bf16[4,2,64,1024]{3,2,1,0:T(8,128)(2,1)} %get-tuple-element.137.refs_0_, ...), custom_call_target="tpu_custom_call" | custom-call | bytes 140000000 | tf_op jit(solution)/shard_map/ffn_backward/pallas_call | solution.py:1426
  362.5 0.0 reduce-scatter.5.cloned.1.call-update
  362.5 0.0 reduce-scatter.3.cloned.1.call-done.refs_1_
  362.5 21.6 %delta_backward.3 = (bf16[512,1664]{1,0:T(8,128)(2,1)}, f32[1,2,4,256]{3,2,1,0:T(4,128)}, f32[1,4,512]{2,1,0:T(4,128)}, f32[1,2,8,128]{3,2,1,0:T(8,128)}, f32[1,2,1,256]{3,2,1,0:T(1,128)}) custom-call(f32[512,1664]{1,0:T(8,128)} %copy-done, f32[512,1664]{1,0:T(8,128)} %copy-done, f32[512,1664]{1,0:T(8,128)} %copy-done, f32[512,1664]{1,0:T(8,128)} %copy-done, ...), custom_call_target="tpu_custom_call" | custom-call | bytes 87500000 | tf_op jit(solution)/shard_map/delta_backward/pallas_call | solution.py:413
  384.1 53.8 %last.1 = (f32[2,64,1024]{2,1,0:T(8,128)}, f32[128,2176]{1,0:T(8,128)}, f32[32,512]{1,0:T(8,128)}, f32[8,1024]{1,0:T(8,128)}) custom-call(bf16[4,2,64,1664]{3,2,1,0:T(8,128)(2,1)} %bitcast.65, bf16[1024,1664]{1,0:T(8,128)(2,1)} %bitcast.57, bf16[4,2,64,1024]{3,2,1,0:T(8,128)(2,1)} %get-tuple-element.101.refs_2_, bf16[4,2,64,512]{3,2,1,0:T(8,128)(2,1)} %bitcast.49, ...), custom_call_target="tpu_custom_call" | custom-call | bytes 140000000 | tf_op jit(solution)/shard_map/last/pallas_call | solution.py:1426
  437.9 4.2 finish.2
  442.1 2.2 reduce-scatter.5.cloned.1.call-done.refs_0_
  444.3 2.8 finish.3
  (42 shorter events, 0.1 us)
Async XLA Ops:
  7.2 70.2 %all-gather.4.cloned.1.call-start = ((), (), s32[]{:S(2)}) async-start(), calls=%async_computation.2 | async-start | bytes 4718592 | tf_op jit(solution)/shard_map/all_gather | solution.py:1680
  9.4 47.8 %copy-start.17 = (f32[2,2,2]{2,1,0:T(2,128)S(1)}, f32[2,2,2]{2,1,0:T(2,128)}, u32[]{:S(2)}) copy-start(f32[2,2,2]{2,1,0:T(2,128)} %param.30) | copy-start | bytes 100
  9.4 47.8 %copy-start.18 = (f32[2,256]{1,0:T(2,128)S(1)}, f32[2,256]{1,0:T(2,128)}, u32[]{:S(2)}) copy-start(f32[2,256]{1,0:T(2,128)} %param.32) | copy-start | bytes 6148
  9.4 47.8 %copy-start.15 = (f32[2,2,4,256]{3,2,1,0:T(4,128)S(1)}, f32[2,2,4,256]{3,2,1,0:T(4,128)}, u32[]{:S(2)}) copy-start(f32[2,2,4,256]{3,2,1,0:T(4,128)} %param.28) | copy-start | bytes 49156
  9.4 47.8 %copy-start.16 = (f32[2,4,512]{2,1,0:T(4,128)S(1)}, f32[2,4,512]{2,1,0:T(4,128)}, u32[]{:S(2)}) copy-start(f32[2,4,512]{2,1,0:T(4,128)} %param.29) | copy-start | bytes 49156
  9.5 130.6 %all-gather.6.cloned.1.call-start = ((), (), s32[]{:S(2)}) async-start(), calls=%async_computation.3 | async-start | bytes 3833856 | tf_op jit(solution)/shard_map/all_gather | solution.py:1680
  56.4 103.8 %all-gather.8.cloned.1.call-start = ((), (), s32[]{:S(2)}) async-start(), calls=%async_computation.4 | async-start | bytes 6488064 | tf_op jit(solution)/shard_map/all_gather | solution.py:1680
  57.1 305.4 %reduce-scatter.3.cloned.1.call-start = ((), (), s32[]{:S(2)}) async-start(), calls=%async_computation.5 | async-start | bytes 5308416 | tf_op jit(solution)/shard_map/reduce_scatter | solution.py:1683
  57.2 4.6 %copy-start.11 = (f32[2,2]{1,0:T(2,128)}, f32[2,2]{1,0:T(2,128)S(1)}, u32[]{:S(2)}) copy-start(f32[2,2]{1,0:T(2,128)S(1)} %get-tuple-element.197.head_table) | copy-start | bytes 52
  57.2 87.3 %copy-start.13 = (f32[2,2]{1,0:T(2,128)}, f32[2,2]{1,0:T(2,128)S(1)}, u32[]{:S(2)}) copy-start(f32[2,2]{1,0:T(2,128)S(1)} %get-tuple-element.196.head_table) | copy-start | bytes 52
  57.2 4.5 copy-start.12
  57.3 87.3 %copy-start.14 = (f32[1,256]{1,0:T(1,128)}, f32[1,256]{1,0:T(1,128)S(1)}, u32[]{:S(2)}) copy-start(f32[1,256]{1,0:T(1,128)S(1)} %get-tuple-element.194.gain) | copy-start | bytes 3076
  57.3 4.5 copy-start.7
  57.3 87.3 %copy-start.9 = (f32[2,4,256]{2,1,0:T(4,128)}, f32[2,4,256]{2,1,0:T(4,128)S(1)}, u32[]{:S(2)}) copy-start(f32[2,4,256]{2,1,0:T(4,128)S(1)} %get-tuple-element.192.tap_qk) | copy-start | bytes 24580
  57.3 4.5 copy-start.8
  57.3 87.2 %copy-start.10 = (f32[4,512]{1,0:T(4,128)}, f32[4,512]{1,0:T(4,128)S(1)}, u32[]{:S(2)}) copy-start(f32[4,512]{1,0:T(4,128)S(1)} %get-tuple-element.190.tap_v) | copy-start | bytes 24580
  57.3 4.5 copy-start.2
  57.4 4.5 copy-start.6
  61.7 14.9 %copy-start = (f32[512,1664]{1,0:T(8,128)}, f32[512,1664]{1,0:T(8,128)S(1)}, u32[]{:S(2)}) copy-start(f32[512,1664]{1,0:T(8,128)S(1)} %fusion.1.qref.kref.vref.gref.pair_ref) | copy-start | bytes 10223620
  76.6 0.8 copy-start.4
  140.1 4.5 copy-start.3
  144.5 14.8 %copy-start.1 = (f32[512,1664]{1,0:T(8,128)}, f32[512,1664]{1,0:T(8,128)S(1)}, u32[]{:S(2)}) copy-start(f32[512,1664]{1,0:T(8,128)S(1)} %fusion.2.qref.kref.vref.gref.pair_ref) | copy-start | bytes 10223620
  159.4 0.8 copy-start.5
  253.5 190.8 %reduce-scatter.5.cloned.1.call-start = ((), (), s32[]{:S(2)}) async-start(), calls=%async_computation.6 | async-start | bytes 5308416 | tf_op jit(solution)/shard_map/reduce_scatter | solution.py:1683
Sparse Core Ops, SparseCore 0:
  10.5 47.7 all-gather.3
  60.2 41.1 all-gather.5
  103.3 43.8 all-gather.7
  253.6 72.1 reduce-scatter.2
  362.6 81.6 reduce-scatter.4
